TPU v7x, 128 devices: a whole 4x4x4 slice. The times are simulated.
128 devices in a mesh: ctx: 32 (over x, y, z_lo), head: 4 (over z_hi, core).
Axes of the slice: x: 4, y: 4, z: 4 (z_hi: 2, z_lo: 2; z = z_hi * 2 + z_lo), core: 2. Of those that a mesh axis runs over, the one named last changes fastest.
Arguments:
- tokens: bfloat16 [2, 8192, 2048], P(None, 'ctx'), may hold values from -6 to 6
- w_qkv: bfloat16 [2048, 4, 1536], P(None, 'head'), as said below
- w_rate: bfloat16 [2048, 4], P(None, 'head'), may hold values from -0.125 to 0.125
- w_out: bfloat16 [4, 512, 2048], P('head'), may hold values from -0.125 to 0.125
- fw_gain: float32 [4, 512], P('head'), may hold values from 0.25 to 1.75
- fast_first: float32 [4, 512, 512], P('head'), may hold values from -0.25 to 0.25
- fast_third: float32 [4, 512, 512], P('head'), may hold values from -0.25 to 0.25
- fast_second: float32 [4, 512, 512], P('head'), may hold values from -0.25 to 0.25
Outputs:
- mixed: bfloat16 [2, 8192, 2048], P(None, 'ctx', 'head')
- new_first: float32 [4, 512, 512], P('head')
- new_third: float32 [4, 512, 512], P('head')
- new_second: float32 [4, 512, 512], P('head')
Inputs may be any that keep to these rules, and one draw needn't show every extreme that they name: `w_qkv`: A projection scaled by its fan-in 2048.
All inputs are finite; a program needn't handle non-finite values.
Results may differ from a plain program's by a relative error of at most 0.039.
Values may be sent and summed in bfloat16 or wider, within the bound.
No kernel may reach another device: no remote copies, remote signals or barrier semaphores. Data moves between devices by JAX's collectives and lax.ppermute only.
A program may use at most 128 MiB of HBM per device.

v0:
```python
import jax
import jax.numpy as jnp
from jax import lax
from jax.experimental import pallas as pl
from jax.experimental.pallas import tpu as pltpu
from jax.sharding import PartitionSpec as P

NS_STEPS = 5
HALF = 256
SUPER = 512
REACH = 4
BF = jnp.bfloat16
F32 = jnp.float32

coeff_a = 3.4445
coeff_b = -4.775
coeff_c = 2.0315
fast_step = 0.5
norm_eps = 1e-06
MASKED = -1e30

CTX_X, CTX_Y, CTX_Z = 4, 4, 2


def nn(left, right):
    return lax.dot_general(left, right, (((1,), (0,)), ((), ())), preferred_element_type=F32)


def nt(left, right):
    return lax.dot_general(left, right, (((1,), (1,)), ((), ())), preferred_element_type=F32)


def tn(left, right):
    return lax.dot_general(left, right, (((0,), (0,)), ((), ())), preferred_element_type=F32)


def moved(value, route):
    pairs = []
    for ctx in range(CTX_X * CTX_Y * CTX_Z):
        x, y, z = ctx // 8, (ctx // 2) % 4, ctx % 2
        for head in range(4):
            target = route(x, y, z, head // 2, head % 2)
            if target is not None:
                tx, ty, tz, th, tc = target
                pairs.append((ctx * 4 + head, (tx * 8 + ty * 2 + tz) * 4 + th * 2 + tc))
    return lax.ppermute(value, ("ctx", "head"), pairs)


def to_role_same(x, y, z, zh, core):
    return (x, (y & 2) + core, z, zh, y & 1)


def to_role_other(x, y, z, zh, core):
    return (x, (y & 2) + core, 1 - z, zh, y & 1)


def quads_on(steps):
    def route(x, y, z, zh, core):
        place = z * 8 + 2 * x + (y >> 1) + steps
        if place >= 16:
            return None
        quad = place % 8
        return (quad // 2, (quad % 2) * 2 + (y & 1), place // 8, zh, core)

    return route


def across(x, y, z, zh, core):
    return (x, y ^ 2, z, zh, core)


def other_core(x, y, z, zh, core):
    return (x, y, z, zh, 1 - core)


def other_pair(x, y, z, zh, core):
    return (x, y, z, 1 - zh, core)


def vmem():
    return pl.BlockSpec(memory_space=pltpu.VMEM)


def smem():
    return pl.BlockSpec(memory_space=pltpu.SMEM)


def call(kernel, specs, outs, flops=1 << 20, scratch=(), limit=16):
    return pl.pallas_call(
        kernel,
        in_specs=specs,
        out_specs=[vmem()] * len(outs),
        out_shape=[jax.ShapeDtypeStruct(shape, dtype) for shape, dtype in outs],
        scratch_shapes=list(scratch),
        compiler_params=pltpu.CompilerParams(vmem_limit_bytes=limit << 20),
        cost_estimate=pl.CostEstimate(flops=flops, bytes_accessed=1 << 10, transcendentals=0),
        name=kernel.__name__,
    )


CHUNK = 256
CHUNKS = 6


def project(place, tokens_ref, w_ref, natural_ref, same, other):
    z = place[0]
    tokens = tokens_ref[...].reshape(2 * HALF, -1)
    for j in (2, 3, 0, 1, 4, 5):
        columns = slice(j * CHUNK, (j + 1) * CHUNK)
        result = nn(tokens, w_ref[:, columns]).astype(BF)
        low, high = result[:HALF], result[HALF:]
        natural_ref[0, :, columns] = low
        natural_ref[1, :, columns] = high
        part = slice((j % 2) * CHUNK, (j % 2 + 1) * CHUNK)
        rows = slice(j // 2 * HALF, (j // 2 + 1) * HALF)
        same[rows, part] = jnp.where(z == 0, low, high)
        other[rows, part] = jnp.where(z == 0, high, low)


def run_project(place, tokens, weights):
    return call(
        project,
        [smem(), vmem(), vmem()],
        [((2, HALF, 1536), BF)] + [((3 * HALF, 512), BF)] * 2,
    )(place, tokens, weights)


def spread(whole, outs, at):
    rows = outs[0].shape[0]
    for step, ref in enumerate(outs):
        start = pl.multiple_of((at ^ step) * rows, rows)
        ref[...] = whole[pl.ds(start, rows)]


def fast_grads(place, tokens_ref, rate_ref, qkv_ref, first_ref, third_ref, second_ref, *rest):
    out_ref = rest[4]
    drive = jnp.sum(
        tokens_ref[0].astype(F32) * rate_ref[...].astype(F32), axis=1, keepdims=True
    )
    rates = jnp.maximum(drive, 0.0) + jnp.log1p(jnp.exp(-jnp.abs(drive)))
    keys = qkv_ref[0, :, 512:1024]
    values = qkv_ref[0, :, 1024:]
    hidden_one = nn(keys, first_ref[...].astype(BF))
    hidden_three = nn(keys, third_ref[...].astype(BF))
    target = (-rates * values.astype(F32)).astype(BF)
    dactiv = nt(target, second_ref[...].astype(BF))
    sigma = jax.nn.sigmoid(hidden_one)
    silu = hidden_one * sigma
    activ = (silu * hidden_three).astype(BF)
    d_first = (dactiv * hidden_three * (sigma * (1.0 + hidden_one * (1.0 - sigma)))).astype(BF)
    d_third = (dactiv * silu).astype(BF)
    out_ref[0:512] = tn(keys, d_first).astype(BF)
    out_ref[512:1024] = tn(keys, d_third).astype(BF)
    out_ref[1024:1536] = tn(activ, target).astype(BF)
    spread(out_ref, rest[:4], place[4])


def summed(refs):
    total = refs[0][...].astype(F32)
    for ref in refs[1:]:
        total = total + ref[...].astype(F32)
    return total.astype(BF)


def reduce_x(place, *refs):
    refs[8][...] = summed(refs[:4])
    spread(refs[8], refs[4:8], place[5])


def reduce_y(*refs):
    refs[4][...] = summed(refs[:4])


def reduce_z(*refs):
    refs[2][...] = summed(refs[:2])


def applied(queries, first, third, second, gain):
    hidden_one = nn(queries, first)
    hidden_three = nn(queries, third)
    activ = (jax.nn.silu(hidden_one) * hidden_three).astype(BF)
    fast_out = nn(activ, second)
    mean = jnp.mean(fast_out * fast_out, axis=1, keepdims=True)
    return fast_out * lax.rsqrt(mean + norm_eps) * gain


def fast_apply(qkv_ref, first_ref, third_ref, second_ref, gain_ref, out_ref):
    out_ref[...] = applied(
        qkv_ref[0, :, :512],
        first_ref[...].astype(BF),
        third_ref[...].astype(BF),
        second_ref[...].astype(BF),
        gain_ref[...],
    )


def fast_update(
    place,
    part_zero,
    part_one,
    part_two,
    part_three,
    first_ref,
    third_ref,
    second_ref,
    qkv_ref,
    gain_ref,
    new_first_ref,
    new_third_ref,
    new_second_ref,
    normed_ref,
    current,
    grad_ref,
):
    x, y = place[4], place[5]
    for step, part in enumerate((part_zero, part_one, part_two, part_three)):
        for across_y in range(4):
            start = (x ^ step) * 384 + (y ^ across_y) * 96
            at = across_y * 96
            grad_ref[pl.ds(pl.multiple_of(start, 96), 96)] = part[at : at + 96]
    for which in range(3):
        grad = grad_ref[which * 512 : (which + 1) * 512].astype(F32)
        scale = lax.rsqrt(jnp.sum(grad * grad, keepdims=True) + norm_eps)
        current[which] = (grad * scale).astype(BF)

    def advanced():
        now = [current[which] for which in range(3)]
        grams = [nt(x, x) for x in now]
        narrow = [gram.astype(BF) for gram in grams]
        polys = [
            (coeff_b * gram + coeff_c * nn(low, low)).astype(BF)
            for gram, low in zip(grams, narrow)
        ]
        return [coeff_a * x.astype(F32) + nn(poly, x) for x, poly in zip(now, polys)]

    @pl.loop(0, NS_STEPS - 1)
    def _(step):
        for which, value in enumerate(advanced()):
            current[which] = value.astype(BF)

    last = advanced()
    old = (first_ref, third_ref, second_ref)
    new = [ref[...] - fast_step * value for ref, value in zip(old, last)]
    for ref, value in zip((new_first_ref, new_third_ref, new_second_ref), new):
        ref[...] = value
    narrow = [weight.astype(BF) for weight in new]
    normed_ref[...] = applied(qkv_ref[1, :, :512], *narrow, gain_ref[...])


ROWS = 128


def scores(place, queries_ref, own, swap_one, one, swap_two, two, out_ref, sum_ref, held):
    z, index, core = place[0], place[1], place[2]
    for tile in range(SUPER // ROWS):
        queries = queries_ref[tile * ROWS : (tile + 1) * ROWS]
        query_at = (
            ((tile // 2) ^ z) * HALF
            + (tile % 2) * ROWS
            + lax.broadcasted_iota(jnp.int32, (ROWS, SUPER), 0)
        )
        column = lax.broadcasted_iota(jnp.int32, (ROWS, SUPER), 1)
        highest = jnp.full((ROWS, 1), MASKED, F32)
        order = ((own, 0), (one, 2), (two, REACH), (swap_one, 1 + 2 * core), (swap_two, 3 - 2 * core))
        for slot, (piece, distance) in enumerate(order):
            source = z * 16 + index - distance
            part = nt(queries, piece[...]) * (512 ** (-0.5))
            if slot == 0:
                shift = z * HALF
                key_at = jnp.where(column < HALF, column + shift, column - shift)
                part = jnp.where(key_at <= query_at, part, MASKED)
            elif slot == 2:
                shift = jnp.where(source >= 16, HALF, 0)
                key_at = jnp.where(column < HALF, column + shift, column - shift)
                part = jnp.where((key_at > query_at) & (source >= 0), part, MASKED)
            else:
                part = jnp.where(source >= 0, part, MASKED)
            held[slot] = part
            highest = jnp.maximum(highest, jnp.max(part, axis=1, keepdims=True))
        total = jnp.zeros((ROWS, 1), F32)
        rows = slice(tile * ROWS, (tile + 1) * ROWS)
        for slot in range(5):
            weights = jnp.exp(held[slot] - highest)
            total = total + jnp.sum(weights, axis=1, keepdims=True)
            out_ref[slot, rows] = weights.astype(BF)
        sum_ref[rows] = jnp.broadcast_to(1.0 / total, (ROWS, 128))


def gathered(weights_ref, sum_ref, own, swap_one, one, swap_two, two, same_ref, other_ref):
    for half, out_ref in enumerate((same_ref, other_ref)):
        rows = slice(half * HALF, (half + 1) * HALF)
        result = jnp.zeros((HALF, 512), F32)
        for slot, piece in enumerate((own, one, two, swap_one, swap_two)):
            result = result + nn(weights_ref[slot, rows], piece[...])
        out_ref[...] = (result * sum_ref[rows, 0:1]).astype(BF)


def mix(place, near_ref, far_ref, normed_ref, w_ref, keep_ref, send_ref, *, block_num):
    z, core, pair = place[0], place[2], place[3]
    attended = jnp.where(z == block_num, near_ref[...], far_ref[...])
    combined = (attended.astype(F32) + normed_ref[...]).astype(BF)
    for step in range(2):
        for out_ref, whose in ((keep_ref, core), (send_ref, 1 - core)):
            column = pl.multiple_of(((pair ^ step) * 2 + whose) * 512, 512)
            out_ref[step] = nn(combined, w_ref[:, pl.ds(column, 512)]).astype(BF)


def mix_zero(*refs):
    mix(*refs, block_num=0)


def mix_one(*refs):
    mix(*refs, block_num=1)


def over_heads(place, near, far, normed, w_out, kernel):
    keep, send = call(
        kernel,
        [smem()] + [vmem()] * 4,
        [((2, HALF, 512), BF)] * 2,
    )(place, near, far, normed, w_out)
    return keep.astype(F32) + moved(send, other_core).astype(F32)


def ordered(values, *before):
    kept = lax.optimization_barrier((tuple(values), before))
    return list(kept[0])


def exchanged(pieces, axis):
    received = [pieces[0]]
    for step in range(1, len(pieces)):
        dx, dy, dz = (step if axis == name else 0 for name in "xyz")

        def route(x, y, z, zh, core):
            return (x ^ dx, y ^ dy, z ^ dz, zh, core)

        received.append(moved(pieces[step], route))
    return received


def to_pair(near):
    return near[0] + moved(near[1].astype(BF), other_pair).astype(F32)


def shards(tokens, w_qkv, w_rate, w_out, fw_gain, fast_first, fast_third, fast_second):
    width = tokens.shape[2]
    ctx, head = lax.axis_index("ctx"), lax.axis_index("head")
    x, y, z = ctx // 8, (ctx // 2) % 4, ctx % 2
    zh, core = head // 2, head % 2
    index = 4 * x + (y & 2) + core
    place = jnp.stack([z, index, core, zh, x, y]).astype(jnp.int32)
    first, third, second = fast_first[0], fast_third[0], fast_second[0]

    natural, same, other = run_project(
        place, tokens, w_qkv.reshape(width, 1536)
    )
    same = moved(same, to_role_same)
    other = moved(other, to_role_other)
    grads = call(
        fast_grads,
        [smem()] + [vmem()] * 6,
        [((384, 512), BF)] * 4,
        scratch=(pltpu.VMEM((1536, 512), BF),),
        limit=24,
    )(place, tokens, w_rate.reshape(1, width), natural, first, third, second)
    same, other = ordered([same, other], *grads)
    grads = exchanged(grads, "x")
    queries, own_keys, own_values = (
        jnp.concatenate([half[at * HALF : (at + 1) * HALF] for half in (same, other)], axis=0)
        for at in range(3)
    )
    grads = call(
        reduce_x,
        [smem()] + [vmem()] * 4,
        [((96, 512), BF)] * 4,
        scratch=(pltpu.VMEM((384, 512), BF),),
    )(place, *grads)
    (own_keys,) = ordered([own_keys], grads[0])
    two_keys = moved(own_keys, quads_on(2))
    grads = exchanged(grads, "y")
    (piece,) = call(reduce_y, [vmem()] * 4, [((96, 512), BF)])(*grads)
    (own_values,) = ordered([own_values], piece)
    two_values = moved(own_values, quads_on(2))
    (piece,) = call(reduce_z, [vmem()] * 2, [((96, 512), BF)])(*exchanged([piece] * 2, "z"))

    def onward(own, two):
        return jnp.where(y >= 2, two, own), jnp.where(core == 0, own, two)

    (two_keys,) = ordered([two_keys], piece)
    one_keys, swap_two_keys = onward(own_keys, two_keys)
    piece = exchanged([piece] * 4, "y")
    piece = jnp.concatenate(ordered(piece, one_keys), axis=0)
    one_keys = moved(one_keys, across)
    swap_two_keys = moved(swap_two_keys, other_core)
    parts = exchanged([piece] * 4, "x")
    (two_values,) = ordered([two_values], piece)
    one_values, swap_two_values = onward(own_values, two_values)
    (queries,) = ordered([queries], one_values)
    one_values = moved(one_values, across)
    swap_two_values = moved(swap_two_values, other_core)

    swap_one_keys = moved(one_keys, other_core)
    weights, sums = call(
        scores,
        [smem()] + [vmem()] * 6,
        [((5, SUPER, SUPER), BF), ((SUPER, 128), F32)],
        scratch=(pltpu.VMEM((5, ROWS, SUPER), F32),),
    )(place, queries, own_keys, swap_one_keys, one_keys, swap_two_keys, two_keys)
    swap_one_values = moved(one_values, other_core)
    near, far = call(gathered, [vmem()] * 7, [((HALF, 512), BF)] * 2)(
        weights, sums, own_values, swap_one_values, one_values, swap_two_values, two_values
    )
    parts = ordered(parts, near, far)
    near = moved(near, to_role_same)
    far = moved(far, to_role_other)

    (normed_zero,) = call(
        fast_apply, [vmem()] * 5, [((HALF, 512), F32)]
    )(natural, first, third, second, fw_gain)
    new_first, new_third, new_second, normed_one = call(
        fast_update,
        [smem()] + [vmem()] * 9,
        [((512, 512), F32)] * 3 + [((HALF, 512), F32)],
        scratch=(pltpu.VMEM((3, 512, 512), BF), pltpu.VMEM((1536, 512), BF)),
        limit=24,
    )(place, *parts, first, third, second, natural, fw_gain)
    (normed_zero,) = ordered([normed_zero], normed_one)
    half_zero = over_heads(place, near, far, normed_zero, w_out[0], mix_zero)
    half_one = over_heads(place, near, far, normed_one, w_out[0], mix_one)
    mixed = jnp.stack([to_pair(half_zero), to_pair(half_one)]).astype(BF)
    return (mixed, new_first[None], new_third[None], new_second[None])


def solution(mesh):
    placed = (
        P(None, "ctx", None),
        P(None, "head", None),
        P(None, "head"),
        P("head", None, None),
        P("head", None),
        P("head", None, None),
        P("head", None, None),
        P("head", None, None),
    )
    return jax.shard_map(
        shards,
        mesh=mesh,
        in_specs=placed,
        out_specs=(
            P(None, "ctx", "head"),
            P("head", None, None),
            P("head", None, None),
            P("head", None, None),
        ),
        check_vma=False,
    )
```

profile of v0, /device:TPU:1, one launch (start us, length us, event | category | flops | bytes accessed | tf_op | source)
XLA Modules:
  0.0 158.7 jit_solution(9536286619328684026)
XLA Ops:
  0.7 0.1 stack.39.place.refs_0_
  0.8 1.6 %copy-done.6 = bf16[2,256,2048]{2,1,0:T(8,128)(2,1)S(1)} copy-done((bf16[2,256,2048]{2,1,0:T(8,128)(2,1)S(1)}, bf16[2,256,2048]{2,1,0:T(8,128)(2,1)}, u32[]{:S(2)}) %copy-start.6) | copy-done | bytes 2097176
  2.4 2.8 %copy-done.8 = bf16[2048,1,1536]{2,0,1:T(8,128)(2,1)S(1)} copy-done((bf16[2048,1,1536]{2,0,1:T(8,128)(2,1)S(1)}, bf16[2048,1,1536]{2,0,1:T(8,128)(2,1)}, u32[]{:S(2)}) %copy-start.8) | copy-done | bytes 6291480
  5.2 4.0 %project.1 = (bf16[2,256,1536]{2,1,0:T(8,128)(2,1)S(1)}, bf16[768,512]{1,0:T(8,128)(2,1)S(1)}, bf16[768,512]{1,0:T(8,128)(2,1)S(1)}) custom-call(s32[6]{0:T(128)S(1)} %stack.39.place.refs_0_, bf16[2,256,2048]{2,1,0:T(8,128)(2,1)S(1)} %copy-done.6, bf16[2048,1536]{1,0:T(8,128)(2,1)S(1)} %bitcast.50), custom_call_target="tpu_custom_call" | custom-call | flops 1048576 | bytes 1024 | tf_op jit(solution)/shard_map/project/pallas_call | solution.py:121
  9.2 4.6 %collective-permute-start = (bf16[768,512]{1,0:T(8,128)(2,1)S(1)}, bf16[768,512]{1,0:T(8,128)(2,1)S(1)}, u32[]{:S(2)}, u32[]{:S(2)}) collective-permute-start(bf16[768,512]{1,0:T(8,128)(2,1)S(1)} %get-tuple-element.43), channel_id=1, source_target_pairs={{0,0},{1,8},{2,2},{3,10},{4,4},{5,12},{6,6},{7,14},{8,1},{9,9},{10... | collective-permute-start | bytes 2359304 | tf_op jit(solution)/shard_map/ppermute | solution.py:46
  13.8 1.4 collective-permute-start.1
  15.2 2.1 %fast_grads.1 = (bf16[384,512]{1,0:T(8,128)(2,1)S(1)}, bf16[384,512]{1,0:T(8,128)(2,1)S(1)}, bf16[384,512]{1,0:T(8,128)(2,1)S(1)}, bf16[384,512]{1,0:T(8,128)(2,1)S(1)}) custom-call(s32[6]{0:T(128)S(1)} %stack.39.place.refs_0_, bf16[2,256,2048]{2,1,0:T(8,128)(2,1)S(1)} %copy-done.7, bf16[1,2048]{1,0:T(2,128)(2,1)S(1)} %bitcast.51, ...), custom_call_target="tpu_custom_call" | custom-call | flops 1048576 | bytes 1024 | tf_op jit(solution)/shard_map/fast_grads/pallas_call | solution.py:360
  17.4 1.3 collective-permute-start.2
  18.7 2.5 %collective-permute-start.3 = (bf16[384,512]{1,0:T(8,128)(2,1)S(1)}, bf16[384,512]{1,0:T(8,128)(2,1)S(1)}, u32[]{:S(2)}, u32[]{:S(2)}) collective-permute-start(bf16[384,512]{1,0:T(8,128)(2,1)S(1)} %get-tuple-element.48), channel_id=1, source_target_pairs={{0,64},{1,65},{2,66},{3,67},{4,68},{5,69},{6,70},{7,71},{8,72},{9,... | collective-permute-start | bytes 1179656 | tf_op jit(solution)/shard_map/ppermute | solution.py:46
  21.1 0.2 collective-permute-start.4
  21.3 7.3 %collective-permute-done.2.refs_1_ = bf16[384,512]{1,0:T(8,128)(2,1)S(1)} collective-permute-done((bf16[384,512]{1,0:T(8,128)(2,1)S(1)}, bf16[384,512]{1,0:T(8,128)(2,1)S(1)}, u32[]{:S(2)}, u32[]{:S(2)}) %collective-permute-start.2) | collective-permute-done | bytes 393248 | tf_op jit(solution)/shard_map/ppermute | solution.py:46
  28.6 9.0 %collective-permute-done.3.refs_2_ = bf16[384,512]{1,0:T(8,128)(2,1)S(1)} collective-permute-done((bf16[384,512]{1,0:T(8,128)(2,1)S(1)}, bf16[384,512]{1,0:T(8,128)(2,1)S(1)}, u32[]{:S(2)}, u32[]{:S(2)}) %collective-permute-start.3) | collective-permute-done | bytes 393248 | tf_op jit(solution)/shard_map/ppermute | solution.py:46
  37.6 3.1 %collective-permute-done.4.refs_3_ = bf16[384,512]{1,0:T(8,128)(2,1)S(1)} collective-permute-done((bf16[384,512]{1,0:T(8,128)(2,1)S(1)}, bf16[384,512]{1,0:T(8,128)(2,1)S(1)}, u32[]{:S(2)}, u32[]{:S(2)}) %collective-permute-start.4) | collective-permute-done | bytes 393248 | tf_op jit(solution)/shard_map/ppermute | solution.py:46
  40.8 0.9 reduce_x.1
  41.8 1.0 fusion.8
  42.8 2.1 %collective-permute-start.13 = (bf16[512,512]{1,0:T(8,128)(2,1)S(1)}, bf16[512,512]{1,0:T(8,128)(2,1)}, u32[]{:S(2)}, u32[]{:S(2)}) collective-permute-start(bf16[512,512]{1,0:T(8,128)(2,1)S(1)} %pad_maximum_fusion.2.own), channel_id=1, source_target_pairs={{0,32},{1,33},{2,34},{3,35},{4,36},{5,37},{6,38},{7,39},{8,40},{9,... | collective-permute-start | bytes 1572872 | tf_op jit(solution)/shard_map/ppermute | solution.py:46
  44.9 2.9 %collective-permute-start.6 = (bf16[96,512]{1,0:T(8,128)(2,1)S(1)}, bf16[96,512]{1,0:T(8,128)(2,1)S(1)}, u32[]{:S(2)}, u32[]{:S(2)}) collective-permute-start(bf16[96,512]{1,0:T(8,128)(2,1)S(1)} %get-tuple-element.54), channel_id=1, source_target_pairs={{0,16},{1,17},{2,18},{3,19},{4,20},{5,21},{6,22},{7,23},{8,24},{9,... | collective-permute-start | bytes 294920 | tf_op jit(solution)/shard_map/ppermute | solution.py:46
  47.8 0.9 collective-permute-start.7
  48.7 0.7 collective-permute-done.5.refs_1_
  49.4 3.6 %collective-permute-done.6.refs_2_ = bf16[96,512]{1,0:T(8,128)(2,1)S(1)} collective-permute-done((bf16[96,512]{1,0:T(8,128)(2,1)S(1)}, bf16[96,512]{1,0:T(8,128)(2,1)S(1)}, u32[]{:S(2)}, u32[]{:S(2)}) %collective-permute-start.6) | collective-permute-done | bytes 98336 | tf_op jit(solution)/shard_map/ppermute | solution.py:46
  53.0 2.3 %collective-permute-done.7.refs_3_ = bf16[96,512]{1,0:T(8,128)(2,1)S(1)} collective-permute-done((bf16[96,512]{1,0:T(8,128)(2,1)S(1)}, bf16[96,512]{1,0:T(8,128)(2,1)S(1)}, u32[]{:S(2)}, u32[]{:S(2)}) %collective-permute-start.7) | collective-permute-done | bytes 98336 | tf_op jit(solution)/shard_map/ppermute | solution.py:46
  55.3 0.1 reduce_y.1.refs_0_
  55.3 0.1 collective-permute-start.9
  55.4 4.8 %collective-permute-done.9.refs_1_ = bf16[96,512]{1,0:T(8,128)(2,1)S(1)} collective-permute-done((bf16[96,512]{1,0:T(8,128)(2,1)S(1)}, bf16[96,512]{1,0:T(8,128)(2,1)S(1)}, u32[]{:S(2)}, u32[]{:S(2)}) %collective-permute-start.9) | collective-permute-done | bytes 98336 | tf_op jit(solution)/shard_map/ppermute | solution.py:46
  60.2 0.1 collective-permute-start.10
  60.3 3.1 %collective-permute-start.11 = (bf16[96,512]{1,0:T(8,128)(2,1)S(1)}, bf16[96,512]{1,0:T(8,128)(2,1)S(1)}, u32[]{:S(2)}, u32[]{:S(2)}) collective-permute-start(bf16[96,512]{1,0:T(8,128)(2,1)S(1)} %reduce_z.1), channel_id=1, source_target_pairs={{0,16},{1,17},{2,18},{3,19},{4,20},{5,21},{6,22},{7,23},{8,24},{9,... | collective-permute-start | bytes 294920 | tf_op jit(solution)/shard_map/ppermute | solution.py:46
  63.5 0.7 collective-permute-start.12
  64.2 1.1 pad_maximum_fusion.1.own
  65.3 1.5 collective-permute-start.8
  66.7 1.1 broadcast_select_fusion.1
  67.9 1.9 %collective-permute-start.14 = (bf16[512,512]{1,0:T(8,128)(2,1)S(1)}, bf16[512,512]{1,0:T(8,128)(2,1)S(1)}, u32[]{:S(2)}, u32[]{:S(2)}) collective-permute-start(bf16[512,512]{1,0:T(8,128)(2,1)S(1)} %get-tuple-element.85), channel_id=1, source_target_pairs={{0,16},{1,17},{2,18},{3,19},{4,20},{5,21},{6,22},{7,23},{8,24},{9,... | collective-permute-start | bytes 1572872 | tf_op jit(solution)/shard_map/ppermute | solution.py:46
  69.8 1.0 collective-permute-done.12
  70.9 6.0 %collective-permute-done.8.two = bf16[512,512]{1,0:T(8,128)(2,1)S(1)} collective-permute-done((bf16[512,512]{1,0:T(8,128)(2,1)S(1)}, bf16[512,512]{1,0:T(8,128)(2,1)S(1)}, u32[]{:S(2)}, u32[]{:S(2)}) %collective-permute-start.8) | collective-permute-done | bytes 524320 | tf_op jit(solution)/shard_map/ppermute | solution.py:46
  76.9 0.1 broadcast_select_fusion
  76.9 1.9 %collective-permute-start.17 = (bf16[512,512]{1,0:T(8,128)(2,1)S(1)}, bf16[512,512]{1,0:T(8,128)(2,1)S(1)}, u32[]{:S(2)}, u32[]{:S(2)}) collective-permute-start(bf16[512,512]{1,0:T(8,128)(2,1)S(1)} %get-tuple-element.83), channel_id=1, source_target_pairs={{0,16},{1,17},{2,18},{3,19},{4,20},{5,21},{6,22},{7,23},{8,24},{9,... | collective-permute-start | bytes 1572872 | tf_op jit(solution)/shard_map/ppermute | solution.py:46
  78.8 2.2 %collective-permute-start.16 = (bf16[512,512]{1,0:T(8,128)(2,1)S(1)}, bf16[512,512]{1,0:T(8,128)(2,1)S(1)}, u32[]{:S(2)}, u32[]{:S(2)}) collective-permute-start(bf16[512,512]{1,0:T(8,128)(2,1)S(1)} %get-tuple-element.84), channel_id=1, source_target_pairs={{0,1},{1,0},{2,3},{3,2},{4,5},{5,4},{6,7},{7,6},{8,9},{9,8},{10,11... | collective-permute-start | bytes 1572872 | tf_op jit(solution)/shard_map/ppermute | solution.py:46
  81.1 0.4 collective-permute-done.14.one
  81.5 4.1 %collective-permute-start.15 = (bf16[512,512]{1,0:T(8,128)(2,1)S(1)}, bf16[512,512]{1,0:T(8,128)(2,1)S(1)}, u32[]{:S(2)}, u32[]{:S(2)}) collective-permute-start(bf16[512,512]{1,0:T(8,128)(2,1)S(1)} %collective-permute-done.14.one), channel_id=1, source_target_pairs={{0,1},{1,0},{2,3},{3,2},{4,5},{5,4},{6,7},{7,6},{8,9},{9,8},{10,11... | collective-permute-start | bytes 1572872 | tf_op jit(solution)/shard_map/ppermute | solution.py:46
  85.6 7.2 %collective-permute-done.17.one = bf16[512,512]{1,0:T(8,128)(2,1)S(1)} collective-permute-done((bf16[512,512]{1,0:T(8,128)(2,1)S(1)}, bf16[512,512]{1,0:T(8,128)(2,1)S(1)}, u32[]{:S(2)}, u32[]{:S(2)}) %collective-permute-start.17) | collective-permute-done | bytes 524320 | tf_op jit(solution)/shard_map/ppermute | solution.py:46
  92.8 2.2 %collective-permute-start.18 = (bf16[512,512]{1,0:T(8,128)(2,1)S(1)}, bf16[512,512]{1,0:T(8,128)(2,1)S(1)}, u32[]{:S(2)}, u32[]{:S(2)}) collective-permute-start(bf16[512,512]{1,0:T(8,128)(2,1)S(1)} %collective-permute-done.17.one), channel_id=1, source_target_pairs={{0,1},{1,0},{2,3},{3,2},{4,5},{5,4},{6,7},{7,6},{8,9},{9,8},{10,11... | collective-permute-start | bytes 1572872 | tf_op jit(solution)/shard_map/ppermute | solution.py:46
  95.0 0.6 collective-permute-start.22
  95.6 5.8 %collective-permute-start.23 = (bf16[384,512]{1,0:T(8,128)(2,1)S(1)}, bf16[384,512]{1,0:T(8,128)(2,1)S(1)}, u32[]{:S(2)}, u32[]{:S(2)}) collective-permute-start(bf16[384,512]{1,0:T(8,128)(2,1)S(1)} %constant_dynamic-update-slice_fusion.part_zero), channel_id=1, source_target_pairs={{0,64},{1,65},{2,66},{3,67},{4,68},{5,69},{6,70},{7,71},{8,72},{9,... | collective-permute-start | bytes 1179656 | tf_op jit(solution)/shard_map/ppermute | solution.py:46
  101.4 5.2 %scores.1 = (bf16[5,512,512]{2,1,0:T(8,128)(2,1)S(1)}, f32[512,128]{1,0:T(8,128)S(1)}) custom-call(s32[6]{0:T(128)S(1)} %stack.39.place.refs_0_, bf16[512,512]{1,0:T(8,128)(2,1)S(1)} %pad_maximum_fusion.queries_ref, bf16[512,512]{1,0:T(8,128)(2,1)S(1)} %pad_maximum_fusion.2.own, bf16[512,512]{1,0:T(8,128)(2,1)S(1)} %collective-permute-done.15.swap_one, ...), custom_call_target="tpu_custom_call" | custom-call | flops 1048576 | bytes 1024 | tf_op jit(solution)/shard_map/scores/pallas_call | solution.py:404
  106.7 1.5 gathered.1
  108.2 2.4 %collective-permute-start.20 = (bf16[256,512]{1,0:T(8,128)(2,1)S(1)}, bf16[256,512]{1,0:T(8,128)(2,1)S(1)}, u32[]{:S(2)}, u32[]{:S(2)}) collective-permute-start(bf16[256,512]{1,0:T(8,128)(2,1)S(1)} %get-tuple-element.67), channel_id=1, source_target_pairs={{0,0},{1,8},{2,2},{3,10},{4,4},{5,12},{6,6},{7,14},{8,1},{9,9},{10... | collective-permute-start | bytes 786440 | tf_op jit(solution)/shard_map/ppermute | solution.py:46
  110.7 3.2 %collective-permute-start.21 = (bf16[256,512]{1,0:T(8,128)(2,1)S(1)}, bf16[256,512]{1,0:T(8,128)(2,1)S(1)}, u32[]{:S(2)}, u32[]{:S(2)}) collective-permute-start(bf16[256,512]{1,0:T(8,128)(2,1)S(1)} %get-tuple-element.68), channel_id=1, source_target_pairs={{0,4},{1,12},{2,6},{3,14},{4,0},{5,8},{6,2},{7,10},{8,5},{9,13},{1... | collective-permute-start | bytes 786440 | tf_op jit(solution)/shard_map/ppermute | solution.py:46
  113.9 0.7 fast_apply.1.refs_3_
  114.7 4.5 %collective-permute-done.23.part_two = bf16[384,512]{1,0:T(8,128)(2,1)S(1)} collective-permute-done((bf16[384,512]{1,0:T(8,128)(2,1)S(1)}, bf16[384,512]{1,0:T(8,128)(2,1)S(1)}, u32[]{:S(2)}, u32[]{:S(2)}) %collective-permute-start.23) | collective-permute-done | bytes 393248 | tf_op jit(solution)/shard_map/ppermute | solution.py:46
  119.1 2.0 %collective-permute-done.24.part_three = bf16[384,512]{1,0:T(8,128)(2,1)S(1)} collective-permute-done((bf16[384,512]{1,0:T(8,128)(2,1)S(1)}, bf16[384,512]{1,0:T(8,128)(2,1)S(1)}, u32[]{:S(2)}, u32[]{:S(2)}) %collective-permute-start.24) | collective-permute-done | bytes 393248 | tf_op jit(solution)/shard_map/ppermute | solution.py:46
  121.1 16.3 %fast_update.1 = (f32[512,512]{1,0:T(8,128)}, f32[512,512]{1,0:T(8,128)}, f32[512,512]{1,0:T(8,128)}, f32[256,512]{1,0:T(8,128)S(1)}) custom-call(s32[6]{0:T(128)S(1)} %stack.39.place.refs_0_, bf16[384,512]{1,0:T(8,128)(2,1)S(1)} %constant_dynamic-update-slice_fusion.part_zero, bf16[384,512]{1,0:T(8,128)(2,1)S(1)} %collective-permute-done.22.part_one, ...), custom_call_target="tpu_custom_call" | custom-call | flops 1048576 | bytes 1024 | tf_op jit(solution)/shard_map/fast_update/pallas_call | solution.py:421
  137.4 1.3 mix_zero.1
  138.7 1.5 collective-permute-start.25
  140.2 1.3 mix_one.1
  141.5 0.1 collective-permute-start.27
  141.6 0.1 collective-permute-done.25
  141.7 0.1 convert_add_fusion.1
  141.9 3.8 %collective-permute-start.26 = (bf16[256,512]{1,0:T(8,128)(2,1)S(1)}, bf16[256,512]{1,0:T(8,128)(2,1)S(1)}, u32[]{:S(2)}, u32[]{:S(2)}) collective-permute-start(bf16[256,512]{1,0:T(8,128)(2,1)S(1)} %fusion.5), channel_id=1, source_target_pairs={{0,2},{1,3},{2,0},{3,1},{4,6},{5,7},{6,4},{7,5},{8,10},{9,11},{10,... | collective-permute-start | bytes 786440 | tf_op jit(solution)/shard_map/ppermute | solution.py:46
  145.8 0.2 convert_add_fusion
  146.0 1.5 collective-permute-start.28
  147.5 4.6 %collective-permute-done.26 = bf16[256,512]{1,0:T(8,128)(2,1)S(1)} collective-permute-done((bf16[256,512]{1,0:T(8,128)(2,1)S(1)}, bf16[256,512]{1,0:T(8,128)(2,1)S(1)}, u32[]{:S(2)}, u32[]{:S(2)}) %collective-permute-start.26) | collective-permute-done | bytes 262176 | tf_op jit(solution)/shard_map/ppermute | solution.py:46
  152.1 0.1 fusion.4
  152.2 5.5 %collective-permute-done.28 = bf16[256,512]{1,0:T(8,128)(2,1)S(1)} collective-permute-done((bf16[256,512]{1,0:T(8,128)(2,1)S(1)}, bf16[256,512]{1,0:T(8,128)(2,1)S(1)}, u32[]{:S(2)}, u32[]{:S(2)}) %collective-permute-start.28) | collective-permute-done | bytes 262176 | tf_op jit(solution)/shard_map/ppermute | solution.py:46
  157.8 0.1 fusion.6
  157.8 0.8 pad_maximum_fusion.3
  (49 shorter events, 0.3 us)
Async XLA Ops:
  0.8 1.6 %copy-start.6 = (bf16[2,256,2048]{2,1,0:T(8,128)(2,1)S(1)}, bf16[2,256,2048]{2,1,0:T(8,128)(2,1)}, u32[]{:S(2)}) copy-start(bf16[2,256,2048]{2,1,0:T(8,128)(2,1)} %tokens_ref.3) | copy-start | bytes 6291460
  2.4 2.8 %copy-start.8 = (bf16[2048,1,1536]{2,0,1:T(8,128)(2,1)S(1)}, bf16[2048,1,1536]{2,0,1:T(8,128)(2,1)}, u32[]{:S(2)}) copy-start(bf16[2048,1,1536]{2,0,1:T(8,128)(2,1)} %param.9) | copy-start | bytes 18874372
  5.2 10.1 %copy-start = (f32[1,512,512]{2,1,0:T(8,128)S(1)}, f32[1,512,512]{2,1,0:T(8,128)}, u32[]{:S(2)}) copy-start(f32[1,512,512]{2,1,0:T(8,128)} %param.13) | copy-start | bytes 3145732
  5.2 10.1 %copy-start.1 = (f32[1,512,512]{2,1,0:T(8,128)S(1)}, f32[1,512,512]{2,1,0:T(8,128)}, u32[]{:S(2)}) copy-start(f32[1,512,512]{2,1,0:T(8,128)} %param.14) | copy-start | bytes 3145732
  5.2 10.1 %copy-start.3 = (f32[1,512,512]{2,1,0:T(8,128)S(1)}, f32[1,512,512]{2,1,0:T(8,128)}, u32[]{:S(2)}) copy-start(f32[1,512,512]{2,1,0:T(8,128)} %param.15) | copy-start | bytes 3145732
  5.2 10.1 %copy-start.7 = (bf16[2,256,2048]{2,1,0:T(8,128)(2,1)S(1)}, bf16[2,256,2048]{2,1,0:T(8,128)(2,1)}, u32[]{:S(2)}) copy-start(bf16[2,256,2048]{2,1,0:T(8,128)(2,1)} %tokens_ref.3) | copy-start | bytes 6291460
  5.2 10.1 %copy-start.9 = (bf16[2048,1]{0,1:T(2,128)(2,1)S(1)}, bf16[2048,1]{0,1:T(2,128)(2,1)}, u32[]{:S(2)}) copy-start(bf16[2048,1]{0,1:T(2,128)(2,1)} %param.10) | copy-start | bytes 12292
  9.2 32.6 %collective-permute-start = (bf16[768,512]{1,0:T(8,128)(2,1)S(1)}, bf16[768,512]{1,0:T(8,128)(2,1)S(1)}, u32[]{:S(2)}, u32[]{:S(2)}) collective-permute-start(bf16[768,512]{1,0:T(8,128)(2,1)S(1)} %get-tuple-element.43), channel_id=1, source_target_pairs={{0,0},{1,8},{2,2},{3,10},{4,4},{5,12},{6,6},{7,14},{8,1},{9,9},{10... | collective-permute-start | bytes 2359304 | tf_op jit(solution)/shard_map/ppermute | solution.py:46
  13.8 28.0 %collective-permute-start.1 = (bf16[768,512]{1,0:T(8,128)(2,1)S(1)}, bf16[768,512]{1,0:T(8,128)(2,1)S(1)}, u32[]{:S(2)}, u32[]{:S(2)}) collective-permute-start(bf16[768,512]{1,0:T(8,128)(2,1)S(1)} %get-tuple-element.44), channel_id=1, source_target_pairs={{0,4},{1,12},{2,6},{3,14},{4,0},{5,8},{6,2},{7,10},{8,5},{9,13},{1... | collective-permute-start | bytes 2359304 | tf_op jit(solution)/shard_map/ppermute | solution.py:46
  17.4 11.3 %collective-permute-start.2 = (bf16[384,512]{1,0:T(8,128)(2,1)S(1)}, bf16[384,512]{1,0:T(8,128)(2,1)S(1)}, u32[]{:S(2)}, u32[]{:S(2)}) collective-permute-start(bf16[384,512]{1,0:T(8,128)(2,1)S(1)} %get-tuple-element.47), channel_id=1, source_target_pairs={{0,32},{1,33},{2,34},{3,35},{4,36},{5,37},{6,38},{7,39},{8,40},{9,... | collective-permute-start | bytes 1179656 | tf_op jit(solution)/shard_map/ppermute | solution.py:46
  18.7 19.0 %collective-permute-start.3 = (bf16[384,512]{1,0:T(8,128)(2,1)S(1)}, bf16[384,512]{1,0:T(8,128)(2,1)S(1)}, u32[]{:S(2)}, u32[]{:S(2)}) collective-permute-start(bf16[384,512]{1,0:T(8,128)(2,1)S(1)} %get-tuple-element.48), channel_id=1, source_target_pairs={{0,64},{1,65},{2,66},{3,67},{4,68},{5,69},{6,70},{7,71},{8,72},{9,... | collective-permute-start | bytes 1179656 | tf_op jit(solution)/shard_map/ppermute | solution.py:46
  21.1 19.7 %collective-permute-start.4 = (bf16[384,512]{1,0:T(8,128)(2,1)S(1)}, bf16[384,512]{1,0:T(8,128)(2,1)S(1)}, u32[]{:S(2)}, u32[]{:S(2)}) collective-permute-start(bf16[384,512]{1,0:T(8,128)(2,1)S(1)} %get-tuple-element.49), channel_id=1, source_target_pairs={{0,96},{1,97},{2,98},{3,99},{4,100},{5,101},{6,102},{7,103},{8,104... | collective-permute-start | bytes 1179656 | tf_op jit(solution)/shard_map/ppermute | solution.py:46
  42.8 24.0 %collective-permute-start.13 = (bf16[512,512]{1,0:T(8,128)(2,1)S(1)}, bf16[512,512]{1,0:T(8,128)(2,1)}, u32[]{:S(2)}, u32[]{:S(2)}) collective-permute-start(bf16[512,512]{1,0:T(8,128)(2,1)S(1)} %pad_maximum_fusion.2.own), channel_id=1, source_target_pairs={{0,32},{1,33},{2,34},{3,35},{4,36},{5,37},{6,38},{7,39},{8,40},{9,... | collective-permute-start | bytes 1572872 | tf_op jit(solution)/shard_map/ppermute | solution.py:46
  44.9 4.5 %collective-permute-start.5 = (bf16[96,512]{1,0:T(8,128)(2,1)S(1)}, bf16[96,512]{1,0:T(8,128)(2,1)S(1)}, u32[]{:S(2)}, u32[]{:S(2)}) collective-permute-start(bf16[96,512]{1,0:T(8,128)(2,1)S(1)} %get-tuple-element.53), channel_id=1, source_target_pairs={{0,8},{1,9},{2,10},{3,11},{4,12},{5,13},{6,14},{7,15},{8,0},{9,1},... | collective-permute-start | bytes 294920 | tf_op jit(solution)/shard_map/ppermute | solution.py:46
  44.9 8.1 %collective-permute-start.6 = (bf16[96,512]{1,0:T(8,128)(2,1)S(1)}, bf16[96,512]{1,0:T(8,128)(2,1)S(1)}, u32[]{:S(2)}, u32[]{:S(2)}) collective-permute-start(bf16[96,512]{1,0:T(8,128)(2,1)S(1)} %get-tuple-element.54), channel_id=1, source_target_pairs={{0,16},{1,17},{2,18},{3,19},{4,20},{5,21},{6,22},{7,23},{8,24},{9,... | collective-permute-start | bytes 294920 | tf_op jit(solution)/shard_map/ppermute | solution.py:46
  47.8 7.5 %collective-permute-start.7 = (bf16[96,512]{1,0:T(8,128)(2,1)S(1)}, bf16[96,512]{1,0:T(8,128)(2,1)S(1)}, u32[]{:S(2)}, u32[]{:S(2)}) collective-permute-start(bf16[96,512]{1,0:T(8,128)(2,1)S(1)} %get-tuple-element.55), channel_id=1, source_target_pairs={{0,24},{1,25},{2,26},{3,27},{4,28},{5,29},{6,30},{7,31},{8,16},{9,... | collective-permute-start | bytes 294920 | tf_op jit(solution)/shard_map/ppermute | solution.py:46
  55.3 4.9 %collective-permute-start.9 = (bf16[96,512]{1,0:T(8,128)(2,1)S(1)}, bf16[96,512]{1,0:T(8,128)(2,1)S(1)}, u32[]{:S(2)}, u32[]{:S(2)}) collective-permute-start(bf16[96,512]{1,0:T(8,128)(2,1)S(1)} %reduce_y.1.refs_0_), channel_id=1, source_target_pairs={{0,4},{1,5},{2,6},{3,7},{4,0},{5,1},{6,2},{7,3},{8,12},{9,13},{10,... | collective-permute-start | bytes 294920 | tf_op jit(solution)/shard_map/ppermute | solution.py:46
  60.2 9.6 %collective-permute-start.10 = (bf16[96,512]{1,0:T(8,128)(2,1)S(1)}, bf16[96,512]{1,0:T(8,128)(2,1)S(1)}, u32[]{:S(2)}, u32[]{:S(2)}) collective-permute-start(bf16[96,512]{1,0:T(8,128)(2,1)S(1)} %reduce_z.1), channel_id=1, source_target_pairs={{0,8},{1,9},{2,10},{3,11},{4,12},{5,13},{6,14},{7,15},{8,0},{9,1},... | collective-permute-start | bytes 294920 | tf_op jit(solution)/shard_map/ppermute | solution.py:46
  60.3 9.5 %collective-permute-start.11 = (bf16[96,512]{1,0:T(8,128)(2,1)S(1)}, bf16[96,512]{1,0:T(8,128)(2,1)S(1)}, u32[]{:S(2)}, u32[]{:S(2)}) collective-permute-start(bf16[96,512]{1,0:T(8,128)(2,1)S(1)} %reduce_z.1), channel_id=1, source_target_pairs={{0,16},{1,17},{2,18},{3,19},{4,20},{5,21},{6,22},{7,23},{8,24},{9,... | collective-permute-start | bytes 294920 | tf_op jit(solution)/shard_map/ppermute | solution.py:46
  63.5 7.4 %collective-permute-start.12 = (bf16[96,512]{1,0:T(8,128)(2,1)S(1)}, bf16[96,512]{1,0:T(8,128)(2,1)S(1)}, u32[]{:S(2)}, u32[]{:S(2)}) collective-permute-start(bf16[96,512]{1,0:T(8,128)(2,1)S(1)} %reduce_z.1), channel_id=1, source_target_pairs={{0,24},{1,25},{2,26},{3,27},{4,28},{5,29},{6,30},{7,31},{8,16},{9,... | collective-permute-start | bytes 294920 | tf_op jit(solution)/shard_map/ppermute | solution.py:46
  65.2 36.2 %copy-start.11 = (bf16[256,512]{1,0:T(8,128)(2,1)S(1)}, bf16[256,512]{1,0:T(8,128)(2,1)}, u32[]{:S(2)}) copy-start(bf16[256,512]{1,0:T(8,128)(2,1)} %get-tuple-element.88) | copy-start | bytes 786436
  65.2 36.1 %copy-start.12 = (bf16[256,512]{1,0:T(8,128)(2,1)S(1)}, bf16[256,512]{1,0:T(8,128)(2,1)}, u32[]{:S(2)}) copy-start(bf16[256,512]{1,0:T(8,128)(2,1)} %get-tuple-element.92) | copy-start | bytes 786436
  65.3 11.6 %collective-permute-start.8 = (bf16[512,512]{1,0:T(8,128)(2,1)S(1)}, bf16[512,512]{1,0:T(8,128)(2,1)S(1)}, u32[]{:S(2)}, u32[]{:S(2)}) collective-permute-start(bf16[512,512]{1,0:T(8,128)(2,1)S(1)} %pad_maximum_fusion.1.own), channel_id=1, source_target_pairs={{0,32},{1,33},{2,34},{3,35},{4,36},{5,37},{6,38},{7,39},{8,40},{9,... | collective-permute-start | bytes 1572872 | tf_op jit(solution)/shard_map/ppermute | solution.py:46
  67.9 13.7 %collective-permute-start.14 = (bf16[512,512]{1,0:T(8,128)(2,1)S(1)}, bf16[512,512]{1,0:T(8,128)(2,1)S(1)}, u32[]{:S(2)}, u32[]{:S(2)}) collective-permute-start(bf16[512,512]{1,0:T(8,128)(2,1)S(1)} %get-tuple-element.85), channel_id=1, source_target_pairs={{0,16},{1,17},{2,18},{3,19},{4,20},{5,21},{6,22},{7,23},{8,24},{9,... | collective-permute-start | bytes 1572872 | tf_op jit(solution)/shard_map/ppermute | solution.py:46
  76.9 15.8 %collective-permute-start.17 = (bf16[512,512]{1,0:T(8,128)(2,1)S(1)}, bf16[512,512]{1,0:T(8,128)(2,1)S(1)}, u32[]{:S(2)}, u32[]{:S(2)}) collective-permute-start(bf16[512,512]{1,0:T(8,128)(2,1)S(1)} %get-tuple-element.83), channel_id=1, source_target_pairs={{0,16},{1,17},{2,18},{3,19},{4,20},{5,21},{6,22},{7,23},{8,24},{9,... | collective-permute-start | bytes 1572872 | tf_op jit(solution)/shard_map/ppermute | solution.py:46
  78.8 16.8 %collective-permute-start.16 = (bf16[512,512]{1,0:T(8,128)(2,1)S(1)}, bf16[512,512]{1,0:T(8,128)(2,1)S(1)}, u32[]{:S(2)}, u32[]{:S(2)}) collective-permute-start(bf16[512,512]{1,0:T(8,128)(2,1)S(1)} %get-tuple-element.84), channel_id=1, source_target_pairs={{0,1},{1,0},{2,3},{3,2},{4,5},{5,4},{6,7},{7,6},{8,9},{9,8},{10,11... | collective-permute-start | bytes 1572872 | tf_op jit(solution)/shard_map/ppermute | solution.py:46
  81.5 19.8 %collective-permute-start.15 = (bf16[512,512]{1,0:T(8,128)(2,1)S(1)}, bf16[512,512]{1,0:T(8,128)(2,1)S(1)}, u32[]{:S(2)}, u32[]{:S(2)}) collective-permute-start(bf16[512,512]{1,0:T(8,128)(2,1)S(1)} %collective-permute-done.14.one), channel_id=1, source_target_pairs={{0,1},{1,0},{2,3},{3,2},{4,5},{5,4},{6,7},{7,6},{8,9},{9,8},{10,11... | collective-permute-start | bytes 1572872 | tf_op jit(solution)/shard_map/ppermute | solution.py:46
  85.6 21.0 %collective-permute-start.19 = (bf16[512,512]{1,0:T(8,128)(2,1)S(1)}, bf16[512,512]{1,0:T(8,128)(2,1)S(1)}, u32[]{:S(2)}, u32[]{:S(2)}) collective-permute-start(bf16[512,512]{1,0:T(8,128)(2,1)S(1)} %get-tuple-element.82), channel_id=1, source_target_pairs={{0,1},{1,0},{2,3},{3,2},{4,5},{5,4},{6,7},{7,6},{8,9},{9,8},{10,11... | collective-permute-start | bytes 1572872 | tf_op jit(solution)/shard_map/ppermute | solution.py:46
  92.8 13.9 %collective-permute-start.18 = (bf16[512,512]{1,0:T(8,128)(2,1)S(1)}, bf16[512,512]{1,0:T(8,128)(2,1)S(1)}, u32[]{:S(2)}, u32[]{:S(2)}) collective-permute-start(bf16[512,512]{1,0:T(8,128)(2,1)S(1)} %collective-permute-done.17.one), channel_id=1, source_target_pairs={{0,1},{1,0},{2,3},{3,2},{4,5},{5,4},{6,7},{7,6},{8,9},{9,8},{10,11... | collective-permute-start | bytes 1572872 | tf_op jit(solution)/shard_map/ppermute | solution.py:46
  95.0 19.6 %collective-permute-start.22 = (bf16[384,512]{1,0:T(8,128)(2,1)S(1)}, bf16[384,512]{1,0:T(8,128)(2,1)S(1)}, u32[]{:S(2)}, u32[]{:S(2)}) collective-permute-start(bf16[384,512]{1,0:T(8,128)(2,1)S(1)} %constant_dynamic-update-slice_fusion.part_zero), channel_id=1, source_target_pairs={{0,32},{1,33},{2,34},{3,35},{4,36},{5,37},{6,38},{7,39},{8,40},{9,... | collective-permute-start | bytes 1179656 | tf_op jit(solution)/shard_map/ppermute | solution.py:46
  95.6 23.5 %collective-permute-start.23 = (bf16[384,512]{1,0:T(8,128)(2,1)S(1)}, bf16[384,512]{1,0:T(8,128)(2,1)S(1)}, u32[]{:S(2)}, u32[]{:S(2)}) collective-permute-start(bf16[384,512]{1,0:T(8,128)(2,1)S(1)} %constant_dynamic-update-slice_fusion.part_zero), channel_id=1, source_target_pairs={{0,64},{1,65},{2,66},{3,67},{4,68},{5,69},{6,70},{7,71},{8,72},{9,... | collective-permute-start | bytes 1179656 | tf_op jit(solution)/shard_map/ppermute | solution.py:46
  101.4 19.7 %collective-permute-start.24 = (bf16[384,512]{1,0:T(8,128)(2,1)S(1)}, bf16[384,512]{1,0:T(8,128)(2,1)S(1)}, u32[]{:S(2)}, u32[]{:S(2)}) collective-permute-start(bf16[384,512]{1,0:T(8,128)(2,1)S(1)} %constant_dynamic-update-slice_fusion.part_zero), channel_id=1, source_target_pairs={{0,96},{1,97},{2,98},{3,99},{4,100},{5,101},{6,102},{7,103},{8,104... | collective-permute-start | bytes 1179656 | tf_op jit(solution)/shard_map/ppermute | solution.py:46
  106.7 7.2 %copy-start.2 = (f32[1,512,512]{2,1,0:T(8,128)S(1)}, f32[1,512,512]{2,1,0:T(8,128)}, u32[]{:S(2)}) copy-start(f32[1,512,512]{2,1,0:T(8,128)} %param.14) | copy-start | bytes 3145732
  106.7 7.2 %copy-start.4 = (f32[1,512,512]{2,1,0:T(8,128)S(1)}, f32[1,512,512]{2,1,0:T(8,128)}, u32[]{:S(2)}) copy-start(f32[1,512,512]{2,1,0:T(8,128)} %param.15) | copy-start | bytes 3145732
  106.7 7.2 %copy-start.10 = (f32[1,512]{1,0:T(1,128)S(1)}, f32[1,512]{1,0:T(1,128)}, u32[]{:S(2)}) copy-start(f32[1,512]{1,0:T(1,128)} %gain_ref.3) | copy-start | bytes 6148
  108.2 29.2 %collective-permute-start.20 = (bf16[256,512]{1,0:T(8,128)(2,1)S(1)}, bf16[256,512]{1,0:T(8,128)(2,1)S(1)}, u32[]{:S(2)}, u32[]{:S(2)}) collective-permute-start(bf16[256,512]{1,0:T(8,128)(2,1)S(1)} %get-tuple-element.67), channel_id=1, source_target_pairs={{0,0},{1,8},{2,2},{3,10},{4,4},{5,12},{6,6},{7,14},{8,1},{9,9},{10... | collective-permute-start | bytes 786440 | tf_op jit(solution)/shard_map/ppermute | solution.py:46
  110.7 26.7 %collective-permute-start.21 = (bf16[256,512]{1,0:T(8,128)(2,1)S(1)}, bf16[256,512]{1,0:T(8,128)(2,1)S(1)}, u32[]{:S(2)}, u32[]{:S(2)}) collective-permute-start(bf16[256,512]{1,0:T(8,128)(2,1)S(1)} %get-tuple-element.68), channel_id=1, source_target_pairs={{0,4},{1,12},{2,6},{3,14},{4,0},{5,8},{6,2},{7,10},{8,5},{9,13},{1... | collective-permute-start | bytes 786440 | tf_op jit(solution)/shard_map/ppermute | solution.py:46
  114.6 22.8 %copy-start.5 = (bf16[1,512,2048]{2,1,0:T(8,128)(2,1)S(1)}, bf16[1,512,2048]{2,1,0:T(8,128)(2,1)}, u32[]{:S(2)}) copy-start(bf16[1,512,2048]{2,1,0:T(8,128)(2,1)} %param.11) | copy-start | bytes 6291460
  138.7 3.0 %collective-permute-start.25 = (bf16[2,256,512]{2,1,0:T(8,128)(2,1)S(1)}, bf16[2,256,512]{2,1,0:T(8,128)(2,1)S(1)}, u32[]{:S(2)}, u32[]{:S(2)}) collective-permute-start(bf16[2,256,512]{2,1,0:T(8,128)(2,1)S(1)} %get-tuple-element.76), channel_id=1, source_target_pairs={{0,1},{1,0},{2,3},{3,2},{4,5},{5,4},{6,7},{7,6},{8,9},{9,8},{10,11... | collective-permute-start | bytes 1572872 | tf_op jit(solution)/shard_map/ppermute | solution.py:46
  141.5 4.3 %collective-permute-start.27 = (bf16[2,256,512]{2,1,0:T(8,128)(2,1)S(1)}, bf16[2,256,512]{2,1,0:T(8,128)(2,1)S(1)}, u32[]{:S(2)}, u32[]{:S(2)}) collective-permute-start(bf16[2,256,512]{2,1,0:T(8,128)(2,1)S(1)} %get-tuple-element.78), channel_id=1, source_target_pairs={{0,1},{1,0},{2,3},{3,2},{4,5},{5,4},{6,7},{7,6},{8,9},{9,8},{10,11... | collective-permute-start | bytes 1572872 | tf_op jit(solution)/shard_map/ppermute | solution.py:46
  141.9 10.2 %collective-permute-start.26 = (bf16[256,512]{1,0:T(8,128)(2,1)S(1)}, bf16[256,512]{1,0:T(8,128)(2,1)S(1)}, u32[]{:S(2)}, u32[]{:S(2)}) collective-permute-start(bf16[256,512]{1,0:T(8,128)(2,1)S(1)} %fusion.5), channel_id=1, source_target_pairs={{0,2},{1,3},{2,0},{3,1},{4,6},{5,7},{6,4},{7,5},{8,10},{9,11},{10,... | collective-permute-start | bytes 786440 | tf_op jit(solution)/shard_map/ppermute | solution.py:46
  146.0 11.8 %collective-permute-start.28 = (bf16[256,512]{1,0:T(8,128)(2,1)S(1)}, bf16[256,512]{1,0:T(8,128)(2,1)S(1)}, u32[]{:S(2)}, u32[]{:S(2)}) collective-permute-start(bf16[256,512]{1,0:T(8,128)(2,1)S(1)} %fusion.7), channel_id=1, source_target_pairs={{0,2},{1,3},{2,0},{3,1},{4,6},{5,7},{6,4},{7,5},{8,10},{9,11},{10,... | collective-permute-start | bytes 786440 | tf_op jit(solution)/shard_map/ppermute | solution.py:46
where the time goes:
time: 159 us
  waiting for transfers between devices  62.3 us (39%)
  starting transfers between devices  52.8 us (33%)
  Pallas kernels  33.4 us (21%)
  local copies, waits for them, and re-layouts  5.6 us (4%)
  other arithmetic  3.62 us (2%)
    ppermute x29, waiting for transfers between devices, moved(): return lax.ppermute(value, ('ctx', 'head'), pairs)  62.3 us
    ppermute x29, starting transfers between devices, moved(): return lax.ppermute(value, ('ctx', 'head'), pairs)  52.8 us
    pallas_call x1, Pallas kernels, shards(): call(fast_update, [smem()] + [vmem()] * 9, [((512, 512), F32)] * 3 + [((H...  16.3 us
    pallas_call x1, Pallas kernels, shards(): call(scores, [smem()] + [vmem()] * 6, [((5, SUPER, SUPER), BF), ((SUPER,...  5.2 us
    unnamed x29, local copies, waits for them, and re-layouts  4.46 us
    pallas_call x1, Pallas kernels, run_project(): call(project, [smem(), vmem(), vmem()], [((2, HALF, 1536), BF)] + [((3 *...  3.99 us
  transfers between devices with their start and end apart: 29, of which 16 were waited for; matrix products, arithmetic and copies ran while one was open for 2% of the time, Pallas kernels for 18%

commit v1 on v0

--- a/solution.py
+++ b/solution.py
@@ -6,6 +6,8 @@
 from jax.sharding import PartitionSpec as P
 
 NS_STEPS = 5
+FIRST_STEPS = 1
+MIDDLE_STEPS = 1
 HALF = 256
 SUPER = 512
 REACH = 4
@@ -194,12 +196,46 @@
     )
 
 
-def fast_update(
-    place,
-    part_zero,
-    part_one,
-    part_two,
-    part_three,
+def advanced(now):
+    grams = [nt(x, x) for x in now]
+    narrow = [gram.astype(BF) for gram in grams]
+    polys = [
+        (coeff_b * gram + coeff_c * nn(low, low)).astype(BF)
+        for gram, low in zip(grams, narrow)
+    ]
+    return [coeff_a * x.astype(F32) + nn(poly, x) for x, poly in zip(now, polys)]
+
+
+def repeated(ref, steps):
+    @pl.loop(0, steps)
+    def _(step):
+        for which, value in enumerate(advanced([ref[which] for which in range(3)])):
+            ref[which] = value.astype(BF)
+
+
+def update_start(place, parts_ref, out_ref, grad_ref):
+    y = place[5]
+    for at_x in range(4):
+        for across_y in range(4):
+            start = at_x * 384 + (y ^ across_y) * 96
+            at = across_y * 96
+            grad_ref[pl.ds(pl.multiple_of(start, 96), 96)] = parts_ref[
+                at_x, at : at + 96
+            ]
+    for which in range(3):
+        grad = grad_ref[which * 512 : (which + 1) * 512].astype(F32)
+        scale = lax.rsqrt(jnp.sum(grad * grad, keepdims=True) + norm_eps)
+        out_ref[which] = (grad * scale).astype(BF)
+    repeated(out_ref, FIRST_STEPS)
+
+
+def update_middle(in_ref, out_ref):
+    out_ref[...] = in_ref[...]
+    repeated(out_ref, MIDDLE_STEPS)
+
+
+def update_end(
+    in_ref,
     first_ref,
     third_ref,
     second_ref,
@@ -209,36 +245,11 @@
     new_third_ref,
     new_second_ref,
     normed_ref,
-    current,
-    grad_ref,
+    held,
 ):
-    x, y = place[4], place[5]
-    for step, part in enumerate((part_zero, part_one, part_two, part_three)):
-        for across_y in range(4):
-            start = (x ^ step) * 384 + (y ^ across_y) * 96
-            at = across_y * 96
-            grad_ref[pl.ds(pl.multiple_of(start, 96), 96)] = part[at : at + 96]
-    for which in range(3):
-        grad = grad_ref[which * 512 : (which + 1) * 512].astype(F32)
-        scale = lax.rsqrt(jnp.sum(grad * grad, keepdims=True) + norm_eps)
-        current[which] = (grad * scale).astype(BF)
-
-    def advanced():
-        now = [current[which] for which in range(3)]
-        grams = [nt(x, x) for x in now]
-        narrow = [gram.astype(BF) for gram in grams]
-        polys = [
-            (coeff_b * gram + coeff_c * nn(low, low)).astype(BF)
-            for gram, low in zip(grams, narrow)
-        ]
-        return [coeff_a * x.astype(F32) + nn(poly, x) for x, poly in zip(now, polys)]
-
-    @pl.loop(0, NS_STEPS - 1)
-    def _(step):
-        for which, value in enumerate(advanced()):
-            current[which] = value.astype(BF)
-
-    last = advanced()
+    held[...] = in_ref[...]
+    repeated(held, NS_STEPS - 1 - FIRST_STEPS - MIDDLE_STEPS)
+    last = advanced([held[which] for which in range(3)])
     old = (first_ref, third_ref, second_ref)
     new = [ref[...] - fast_step * value for ref, value in zip(old, last)]
     for ref, value in zip((new_first_ref, new_third_ref, new_second_ref), new):
@@ -313,13 +324,10 @@
     mix(*refs, block_num=1)
 
 
-def over_heads(place, near, far, normed, w_out, kernel):
-    keep, send = call(
-        kernel,
-        [smem()] + [vmem()] * 4,
-        [((2, HALF, 512), BF)] * 2,
-    )(place, near, far, normed, w_out)
-    return keep.astype(F32) + moved(send, other_core).astype(F32)
+def mixed_by(kernel, place, near, far, normed, w_out):
+    return call(kernel, [smem()] + [vmem()] * 4, [((2, HALF, 512), BF)] * 2)(
+        place, near, far, normed, w_out
+    )
 
 
 def ordered(values, *before):
@@ -337,10 +345,6 @@
 
         received.append(moved(pieces[step], route))
     return received
-
-
-def to_pair(near):
-    return near[0] + moved(near[1].astype(BF), other_pair).astype(F32)
 
 
 def shards(tokens, w_qkv, w_rate, w_out, fw_gain, fast_first, fast_third, fast_second):
@@ -393,10 +397,12 @@
     piece = jnp.concatenate(ordered(piece, one_keys), axis=0)
     one_keys = moved(one_keys, across)
     swap_two_keys = moved(swap_two_keys, other_core)
-    parts = exchanged([piece] * 4, "x")
-    (two_values,) = ordered([two_values], piece)
+    lines = [[8 * at_x + at for at_x in range(CTX_X)] for at in range(8)]
+    sent = jnp.broadcast_to(piece[None], (CTX_X, 384, 512))
+    parts = [lax.all_to_all(sent, "ctx", 0, 0, axis_index_groups=lines, tiled=True)]
+    (two_values,) = ordered([two_values], sent)
     one_values, swap_two_values = onward(own_values, two_values)
-    (queries,) = ordered([queries], one_values)
+    (queries,) = ordered([queries], piece)
     one_values = moved(one_values, across)
     swap_two_values = moved(swap_two_values, other_core)
 
@@ -407,6 +413,7 @@
         [((5, SUPER, SUPER), BF), ((SUPER, 128), F32)],
         scratch=(pltpu.VMEM((5, ROWS, SUPER), F32),),
     )(place, queries, own_keys, swap_one_keys, one_keys, swap_two_keys, two_keys)
+    (one_values,) = ordered([one_values], weights)
     swap_one_values = moved(one_values, other_core)
     near, far = call(gathered, [vmem()] * 7, [((HALF, 512), BF)] * 2)(
         weights, sums, own_values, swap_one_values, one_values, swap_two_values, two_values
@@ -418,17 +425,37 @@
     (normed_zero,) = call(
         fast_apply, [vmem()] * 5, [((HALF, 512), F32)]
     )(natural, first, third, second, fw_gain)
+    normed_zero, near, far = ordered([normed_zero, near, far], *parts)
+    (held,) = call(
+        update_start,
+        [smem(), vmem()],
+        [((3, 512, 512), BF)],
+        scratch=(pltpu.VMEM((1536, 512), BF),),
+        limit=24,
+    )(place, *parts)
+    (normed_zero,) = ordered([normed_zero], held)
+    keep, send = mixed_by(mix_zero, place, near, far, normed_zero, w_out[0])
+    (held,) = ordered([held], send)
+    taken = moved(send, other_core)
+    (held,) = call(update_middle, [vmem()], [((3, 512, 512), BF)], limit=24)(held)
+    (taken,) = ordered([taken], held)
+    half_zero = keep.astype(F32) + taken.astype(F32)
+    crossing = half_zero[1].astype(BF)
+    (held,) = ordered([held], crossing)
+    crossing = moved(crossing, other_pair)
     new_first, new_third, new_second, normed_one = call(
-        fast_update,
-        [smem()] + [vmem()] * 9,
+        update_end,
+        [vmem()] * 6,
         [((512, 512), F32)] * 3 + [((HALF, 512), F32)],
-        scratch=(pltpu.VMEM((3, 512, 512), BF), pltpu.VMEM((1536, 512), BF)),
+        scratch=(pltpu.VMEM((3, 512, 512), BF),),
         limit=24,
-    )(place, *parts, first, third, second, natural, fw_gain)
-    (normed_zero,) = ordered([normed_zero], normed_one)
-    half_zero = over_heads(place, near, far, normed_zero, w_out[0], mix_zero)
-    half_one = over_heads(place, near, far, normed_one, w_out[0], mix_one)
-    mixed = jnp.stack([to_pair(half_zero), to_pair(half_one)]).astype(BF)
+    )(held, first, third, second, natural, fw_gain)
+    (normed_one,) = ordered([normed_one], crossing)
+    keep, send = mixed_by(mix_one, place, near, far, normed_one, w_out[0])
+    half_one = keep.astype(F32) + moved(send, other_core).astype(F32)
+    done_zero = half_zero[0] + crossing.astype(F32)
+    done_one = half_one[0] + moved(half_one[1].astype(BF), other_pair).astype(F32)
+    mixed = jnp.stack([done_zero, done_one]).astype(BF)
     return (mixed, new_first[None], new_third[None], new_second[None])
 
 

time: 159 us -> 154 us (0.969)
  waiting for transfers between devices: 62.3 us -> 51.7 us
  Pallas kernels: 33.4 us -> 37.4 us
  starting transfers between devices: 52.8 us -> 49.8 us
  other arithmetic: 3.62 us -> 6.31 us
    ppermute x29 -> x26, waiting for transfers between devices: 62.3 us -> 50.3 us  [moved(): return lax.ppermute(value, ('ctx', 'head'), pairs)]
    ppermute x29 -> x26, starting transfers between devices: 52.8 us -> 43.4 us  [moved(): return lax.ppermute(value, ('ctx', 'head'), pairs)]
    all_to_all x0 -> x1, starting transfers between devices: none -> 6.45 us  [shards(): lax.all_to_all(sent, 'ctx', 0, 0, axis_index_groups=lines, tiled=True)]
    pallas_call x1, Pallas kernels: 1.51 us -> 3.41 us  [shards(): call(gathered, [vmem()] * 7, [((HALF, 512), BF)] * 2)]
    select_n x2, other arithmetic: 1.19 us -> 2.95 us  [onward(): return (jnp.where(y >= 2, two, own), jnp.where(core == 0, own, two))]
    pallas_call x3 -> x5, Pallas kernels: 18.8 us -> 20.5 us  [the longest x1 9.52 us: shards(): call(update_end, [vmem()] * 6, [((512, 512), F32)] * 3 + [((HALF, 512), F...]
    unnamed x29 -> x39, local copies, waits for them, and re-layouts: 4.46 us -> 4.48 us
  transfers between devices with their start and end apart: 29 -> 27, of which waited for: 16 -> 13; matrix products, arithmetic and copies ran while one was open for 2% -> 4% of each run, Pallas kernels for 18% -> 20%
where the time goes in v1:
time: 154 us; the launch traced here: 153 us
  waiting for transfers between devices  51.7 us (34%)
  starting transfers between devices  49.8 us (32%)
  Pallas kernels  37.4 us (24%)
  local copies, waits for them, and re-layouts  6.98 us (5%)
  other arithmetic  6.31 us (4%)
    ppermute x26, waiting for transfers between devices, moved(): return lax.ppermute(value, ('ctx', 'head'), pairs)  50.3 us
    ppermute x26, starting transfers between devices, moved(): return lax.ppermute(value, ('ctx', 'head'), pairs)  43.4 us
    pallas_call x1, Pallas kernels, shards(): call(update_end, [vmem()] * 6, [((512, 512), F32)] * 3 + [((HALF, 512), F...  9.52 us
    all_to_all x1, starting transfers between devices, shards(): lax.all_to_all(sent, 'ctx', 0, 0, axis_index_groups=lines, tiled=True)  6.45 us
    pallas_call x1, Pallas kernels, shards(): call(scores, [smem()] + [vmem()] * 6, [((5, SUPER, SUPER), BF), ((SUPER,...  5.65 us
    pallas_call x1, Pallas kernels, shards(): call(update_start, [smem(), vmem()], [((3, 512, 512), BF)], scratch=(pltp...  4.9 us
    unnamed x39, local copies, waits for them, and re-layouts  4.48 us
    pallas_call x1, Pallas kernels, run_project(): call(project, [smem(), vmem(), vmem()], [((2, HALF, 1536), BF)] + [((3 *...  3.99 us
  transfers between devices with their start and end apart: 27, of which 13 were waited for; matrix products, arithmetic and copies ran while one was open for 4% of the time, Pallas kernels for 20%

profile of v1, /device:TPU:1, one launch (start us, length us, event | category | flops | bytes accessed | tf_op | source)
XLA Modules:
  0.0 153.3 jit_solution(13658342545394779564)
XLA Ops:
  0.7 0.1 stack.39.place.refs_0_
  0.8 1.6 %copy-done.8 = bf16[2,256,2048]{2,1,0:T(8,128)(2,1)S(1)} copy-done((bf16[2,256,2048]{2,1,0:T(8,128)(2,1)S(1)}, bf16[2,256,2048]{2,1,0:T(8,128)(2,1)}, u32[]{:S(2)}) %copy-start.8) | copy-done | bytes 2097176
  2.4 2.8 %copy-done.10 = bf16[2048,1,1536]{2,0,1:T(8,128)(2,1)S(1)} copy-done((bf16[2048,1,1536]{2,0,1:T(8,128)(2,1)S(1)}, bf16[2048,1,1536]{2,0,1:T(8,128)(2,1)}, u32[]{:S(2)}) %copy-start.10) | copy-done | bytes 6291480
  5.2 4.0 %project.1 = (bf16[2,256,1536]{2,1,0:T(8,128)(2,1)S(1)}, bf16[768,512]{1,0:T(8,128)(2,1)S(1)}, bf16[768,512]{1,0:T(8,128)(2,1)S(1)}) custom-call(s32[6]{0:T(128)S(1)} %stack.39.place.refs_0_, bf16[2,256,2048]{2,1,0:T(8,128)(2,1)S(1)} %copy-done.8, bf16[2048,1536]{1,0:T(8,128)(2,1)S(1)} %bitcast.50), custom_call_target="tpu_custom_call" | custom-call | flops 1048576 | bytes 1024 | tf_op jit(solution)/shard_map/project/pallas_call | solution.py:123
  9.2 4.6 %collective-permute-start = (bf16[768,512]{1,0:T(8,128)(2,1)S(1)}, bf16[768,512]{1,0:T(8,128)(2,1)S(1)}, u32[]{:S(2)}, u32[]{:S(2)}) collective-permute-start(bf16[768,512]{1,0:T(8,128)(2,1)S(1)} %get-tuple-element.49), channel_id=1, source_target_pairs={{0,0},{1,8},{2,2},{3,10},{4,4},{5,12},{6,6},{7,14},{8,1},{9,9},{10... | collective-permute-start | bytes 2359304 | tf_op jit(solution)/shard_map/ppermute | solution.py:48
  13.8 1.4 collective-permute-start.1
  15.2 2.1 %fast_grads.1 = (bf16[384,512]{1,0:T(8,128)(2,1)S(1)}, bf16[384,512]{1,0:T(8,128)(2,1)S(1)}, bf16[384,512]{1,0:T(8,128)(2,1)S(1)}, bf16[384,512]{1,0:T(8,128)(2,1)S(1)}) custom-call(s32[6]{0:T(128)S(1)} %stack.39.place.refs_0_, bf16[2,256,2048]{2,1,0:T(8,128)(2,1)S(1)} %copy-done.9, bf16[1,2048]{1,0:T(2,128)(2,1)S(1)} %bitcast.51, ...), custom_call_target="tpu_custom_call" | custom-call | flops 1048576 | bytes 1024 | tf_op jit(solution)/shard_map/fast_grads/pallas_call | solution.py:364
  17.4 1.3 collective-permute-start.2
  18.7 2.5 %collective-permute-start.3 = (bf16[384,512]{1,0:T(8,128)(2,1)S(1)}, bf16[384,512]{1,0:T(8,128)(2,1)S(1)}, u32[]{:S(2)}, u32[]{:S(2)}) collective-permute-start(bf16[384,512]{1,0:T(8,128)(2,1)S(1)} %get-tuple-element.53), channel_id=1, source_target_pairs={{0,64},{1,65},{2,66},{3,67},{4,68},{5,69},{6,70},{7,71},{8,72},{9,... | collective-permute-start | bytes 1179656 | tf_op jit(solution)/shard_map/ppermute | solution.py:48
  21.1 0.2 collective-permute-start.4
  21.3 7.3 %collective-permute-done.2.refs_1_ = bf16[384,512]{1,0:T(8,128)(2,1)S(1)} collective-permute-done((bf16[384,512]{1,0:T(8,128)(2,1)S(1)}, bf16[384,512]{1,0:T(8,128)(2,1)S(1)}, u32[]{:S(2)}, u32[]{:S(2)}) %collective-permute-start.2) | collective-permute-done | bytes 393248 | tf_op jit(solution)/shard_map/ppermute | solution.py:48
  28.6 9.0 %collective-permute-done.3.refs_2_ = bf16[384,512]{1,0:T(8,128)(2,1)S(1)} collective-permute-done((bf16[384,512]{1,0:T(8,128)(2,1)S(1)}, bf16[384,512]{1,0:T(8,128)(2,1)S(1)}, u32[]{:S(2)}, u32[]{:S(2)}) %collective-permute-start.3) | collective-permute-done | bytes 393248 | tf_op jit(solution)/shard_map/ppermute | solution.py:48
  37.6 3.1 %collective-permute-done.4.refs_3_ = bf16[384,512]{1,0:T(8,128)(2,1)S(1)} collective-permute-done((bf16[384,512]{1,0:T(8,128)(2,1)S(1)}, bf16[384,512]{1,0:T(8,128)(2,1)S(1)}, u32[]{:S(2)}, u32[]{:S(2)}) %collective-permute-start.4) | collective-permute-done | bytes 393248 | tf_op jit(solution)/shard_map/ppermute | solution.py:48
  40.8 0.9 reduce_x.1
  41.7 1.0 fusion.8
  42.8 2.1 %collective-permute-start.12 = (bf16[512,512]{1,0:T(8,128)(2,1)S(1)}, bf16[512,512]{1,0:T(8,128)(2,1)}, u32[]{:S(2)}, u32[]{:S(2)}) collective-permute-start(bf16[512,512]{1,0:T(8,128)(2,1)S(1)} %pad_maximum_fusion.1.own), channel_id=1, source_target_pairs={{0,32},{1,33},{2,34},{3,35},{4,36},{5,37},{6,38},{7,39},{8,40},{9,... | collective-permute-start | bytes 1572872 | tf_op jit(solution)/shard_map/ppermute | solution.py:48
  44.9 2.9 %collective-permute-start.6 = (bf16[96,512]{1,0:T(8,128)(2,1)S(1)}, bf16[96,512]{1,0:T(8,128)(2,1)S(1)}, u32[]{:S(2)}, u32[]{:S(2)}) collective-permute-start(bf16[96,512]{1,0:T(8,128)(2,1)S(1)} %get-tuple-element.59), channel_id=1, source_target_pairs={{0,16},{1,17},{2,18},{3,19},{4,20},{5,21},{6,22},{7,23},{8,24},{9,... | collective-permute-start | bytes 294920 | tf_op jit(solution)/shard_map/ppermute | solution.py:48
  47.8 0.9 collective-permute-start.7
  48.7 0.7 collective-permute-done.5.refs_1_
  49.4 3.6 %collective-permute-done.6.refs_2_ = bf16[96,512]{1,0:T(8,128)(2,1)S(1)} collective-permute-done((bf16[96,512]{1,0:T(8,128)(2,1)S(1)}, bf16[96,512]{1,0:T(8,128)(2,1)S(1)}, u32[]{:S(2)}, u32[]{:S(2)}) %collective-permute-start.6) | collective-permute-done | bytes 98336 | tf_op jit(solution)/shard_map/ppermute | solution.py:48
  53.0 2.3 %collective-permute-done.7.refs_3_ = bf16[96,512]{1,0:T(8,128)(2,1)S(1)} collective-permute-done((bf16[96,512]{1,0:T(8,128)(2,1)S(1)}, bf16[96,512]{1,0:T(8,128)(2,1)S(1)}, u32[]{:S(2)}, u32[]{:S(2)}) %collective-permute-start.7) | collective-permute-done | bytes 98336 | tf_op jit(solution)/shard_map/ppermute | solution.py:48
  55.3 0.1 collective-permute-start.8
  55.4 4.8 %collective-permute-done.8.refs_1_ = bf16[96,512]{1,0:T(8,128)(2,1)S(1)} collective-permute-done((bf16[96,512]{1,0:T(8,128)(2,1)S(1)}, bf16[96,512]{1,0:T(8,128)(2,1)S(1)}, u32[]{:S(2)}, u32[]{:S(2)}) %collective-permute-start.8) | collective-permute-done | bytes 98336 | tf_op jit(solution)/shard_map/ppermute | solution.py:48
  60.2 0.3 collective-permute-start.11
  60.5 2.9 %collective-permute-start.10 = (bf16[96,512]{1,0:T(8,128)(2,1)S(1)}, bf16[96,512]{1,0:T(8,128)(2,1)S(1)}, u32[]{:S(2)}, u32[]{:S(2)}) collective-permute-start(bf16[96,512]{1,0:T(8,128)(2,1)S(1)} %reduce_z.1), channel_id=1, source_target_pairs={{0,16},{1,17},{2,18},{3,19},{4,20},{5,21},{6,22},{7,23},{8,24},{9,... | collective-permute-start | bytes 294920 | tf_op jit(solution)/shard_map/ppermute | solution.py:48
  63.5 0.1 collective-permute-start.9
  63.6 1.1 pad_maximum_fusion.2.own
  64.6 1.3 collective-permute-start.16
  66.0 1.9 %broadcast_select_fusion.1 = (bf16[512,512]{1,0:T(8,128)(2,1)}, bf16[512,512]{1,0:T(8,128)(2,1)S(1)}) fusion(bf16[512,512]{1,0:T(8,128)(2,1)S(1)} %pad_maximum_fusion.1.own, bf16[512,512]{1,0:T(8,128)(2,1)} %collective-permute-done.12.two, pred[]{:T(512)S(6)} %eq.8, pred[]{:T(512)S(6)} %ge.4), kind=kLoop, calls=%fused_computation.15 | loop fusion | flops 524288 | bytes 2097154 | tf_op jit(solution)/shard_map/jit(_where)/select_n | solution.py:392
  67.9 3.1 %collective-permute-start.13 = (bf16[512,512]{1,0:T(8,128)(2,1)S(1)}, bf16[512,512]{1,0:T(8,128)(2,1)}, u32[]{:S(2)}, u32[]{:S(2)}) collective-permute-start(bf16[512,512]{1,0:T(8,128)(2,1)S(1)} %get-tuple-element.95), channel_id=1, source_target_pairs={{0,16},{1,17},{2,18},{3,19},{4,20},{5,21},{6,22},{7,23},{8,24},{9,... | collective-permute-start | bytes 1572872 | tf_op jit(solution)/shard_map/ppermute | solution.py:48
  71.0 1.7 %collective-permute-start.15 = (bf16[512,512]{1,0:T(8,128)(2,1)}, bf16[512,512]{1,0:T(8,128)(2,1)}, u32[]{:S(2)}, u32[]{:S(2)}) collective-permute-start(bf16[512,512]{1,0:T(8,128)(2,1)} %get-tuple-element.94), channel_id=1, source_target_pairs={{0,1},{1,0},{2,3},{3,2},{4,5},{5,4},{6,7},{7,6},{8,9},{9,8},{10,11... | collective-permute-start | bytes 1572872 | tf_op jit(solution)/shard_map/ppermute | solution.py:48
  72.7 3.4 %collective-permute-done.16.two = bf16[512,512]{1,0:T(8,128)(2,1)S(1)} collective-permute-done((bf16[512,512]{1,0:T(8,128)(2,1)S(1)}, bf16[512,512]{1,0:T(8,128)(2,1)S(1)}, u32[]{:S(2)}, u32[]{:S(2)}) %collective-permute-start.16) | collective-permute-done | bytes 524320 | tf_op jit(solution)/shard_map/ppermute | solution.py:48
  76.1 1.4 broadcast_in_dim.15
  77.5 4.4 %collective-permute-done.13.one = bf16[512,512]{1,0:T(8,128)(2,1)} collective-permute-done((bf16[512,512]{1,0:T(8,128)(2,1)S(1)}, bf16[512,512]{1,0:T(8,128)(2,1)}, u32[]{:S(2)}, u32[]{:S(2)}) %collective-permute-start.13) | collective-permute-done | bytes 524320 | tf_op jit(solution)/shard_map/ppermute | solution.py:48
  81.8 2.1 %collective-permute-start.14 = (bf16[512,512]{1,0:T(8,128)(2,1)}, bf16[512,512]{1,0:T(8,128)(2,1)}, u32[]{:S(2)}, u32[]{:S(2)}) collective-permute-start(bf16[512,512]{1,0:T(8,128)(2,1)} %collective-permute-done.13.one), channel_id=1, source_target_pairs={{0,1},{1,0},{2,3},{3,2},{4,5},{5,4},{6,7},{7,6},{8,9},{9,8},{10,11... | collective-permute-start | bytes 1572872 | tf_op jit(solution)/shard_map/ppermute | solution.py:48
  84.0 1.0 broadcast_select_fusion
  85.0 3.0 %collective-permute-start.17 = (bf16[512,512]{1,0:T(8,128)(2,1)}, bf16[512,512]{1,0:T(8,128)(2,1)}, u32[]{:S(2)}, u32[]{:S(2)}) collective-permute-start(bf16[512,512]{1,0:T(8,128)(2,1)} %get-tuple-element.93), channel_id=1, source_target_pairs={{0,16},{1,17},{2,18},{3,19},{4,20},{5,21},{6,22},{7,23},{8,24},{9,... | collective-permute-start | bytes 1572872 | tf_op jit(solution)/shard_map/ppermute | solution.py:48
  88.0 6.4 %all-to-all-start = ((bf16[4,384,512]{2,1,0:T(8,128)(2,1)}), bf16[4,384,512]{2,1,0:T(8,128)(2,1)}, u32[]{:S(2)}, u32[]{:S(2)}) async-start(bf16[4,384,512]{2,1,0:T(8,128)(2,1)} %broadcast_in_dim.15), calls=%async_computation | async-start | bytes 3145728 | tf_op jit(solution)/shard_map/all_to_all | solution.py:402
  94.4 1.0 pad_maximum_fusion.queries_ref
  95.4 0.8 collective-permute-start.19
  96.3 5.6 %scores.1 = (bf16[5,512,512]{2,1,0:T(8,128)(2,1)S(1)}, f32[512,128]{1,0:T(8,128)S(1)}) custom-call(s32[6]{0:T(128)S(1)} %stack.39.place.refs_0_, bf16[512,512]{1,0:T(8,128)(2,1)S(1)} %pad_maximum_fusion.queries_ref, bf16[512,512]{1,0:T(8,128)(2,1)S(1)} %pad_maximum_fusion.1.own, bf16[512,512]{1,0:T(8,128)(2,1)} %collective-permute-done.14.swap_one, ...), custom_call_target="tpu_custom_call" | custom-call | flops 1048576 | bytes 1024 | tf_op jit(solution)/shard_map/scores/pallas_call | solution.py:410
  101.9 0.1 collective-permute-start.18
  102.0 2.1 %collective-permute-done.18.swap_one = bf16[512,512]{1,0:T(8,128)(2,1)S(1)} collective-permute-done((bf16[512,512]{1,0:T(8,128)(2,1)}, bf16[512,512]{1,0:T(8,128)(2,1)S(1)}, u32[]{:S(2)}, u32[]{:S(2)}) %collective-permute-start.18) | collective-permute-done | bytes 524320 | tf_op jit(solution)/shard_map/ppermute | solution.py:48
  104.1 3.4 %gathered.1 = (bf16[256,512]{1,0:T(8,128)(2,1)}, bf16[256,512]{1,0:T(8,128)(2,1)}) custom-call(bf16[5,512,512]{2,1,0:T(8,128)(2,1)S(1)} %get-tuple-element.68.weights_ref, f32[512,128]{1,0:T(8,128)S(1)} %get-tuple-element.69.sum_ref, bf16[512,512]{1,0:T(8,128)(2,1)S(1)} %copy-done.12, bf16[512,512]{1,0:T(8,128)(2,1)S(1)} %collective-permute-done.18.swap_one, ...), custom_call_target="tpu_custom_call" | custom-call | flops 1048576 | bytes 1024 | tf_op jit(solution)/shard_map/gathered/pallas_call | solution.py:418
  107.6 2.2 %collective-permute-start.20 = (bf16[256,512]{1,0:T(8,128)(2,1)}, bf16[256,512]{1,0:T(8,128)(2,1)S(1)}, u32[]{:S(2)}, u32[]{:S(2)}) collective-permute-start(bf16[256,512]{1,0:T(8,128)(2,1)} %get-tuple-element.73), channel_id=1, source_target_pairs={{0,0},{1,8},{2,2},{3,10},{4,4},{5,12},{6,6},{7,14},{8,1},{9,9},{10... | collective-permute-start | bytes 786440 | tf_op jit(solution)/shard_map/ppermute | solution.py:48
  109.8 2.8 %collective-permute-start.21 = (bf16[256,512]{1,0:T(8,128)(2,1)}, bf16[256,512]{1,0:T(8,128)(2,1)}, u32[]{:S(2)}, u32[]{:S(2)}) collective-permute-start(bf16[256,512]{1,0:T(8,128)(2,1)} %get-tuple-element.74), channel_id=1, source_target_pairs={{0,4},{1,12},{2,6},{3,14},{4,0},{5,8},{6,2},{7,10},{8,5},{9,13},{1... | collective-permute-start | bytes 786440 | tf_op jit(solution)/shard_map/ppermute | solution.py:48
  112.6 0.7 fast_apply.1.refs_3_
  113.3 1.4 all-to-all-done.parts_ref
  114.8 4.9 %update_start.1.in_ref = bf16[3,512,512]{2,1,0:T(8,128)(2,1)S(1)} custom-call(s32[6]{0:T(128)S(1)} %stack.39.place.refs_0_, bf16[4,384,512]{2,1,0:T(8,128)(2,1)} %all-to-all-done.parts_ref), custom_call_target="tpu_custom_call" | custom-call | flops 1048576 | bytes 1024 | tf_op jit(solution)/shard_map/update_start/pallas_call | solution.py:429
  119.7 1.7 %mix_zero.1 = (bf16[2,256,512]{2,1,0:T(8,128)(2,1)S(1)}, bf16[2,256,512]{2,1,0:T(8,128)(2,1)S(1)}) custom-call(s32[6]{0:T(128)S(1)} %stack.39.place.refs_0_, bf16[256,512]{1,0:T(8,128)(2,1)S(1)} %collective-permute-done.20.refs_1_, bf16[256,512]{1,0:T(8,128)(2,1)} %collective-permute-done.21.refs_2_, f32[256,512]{1,0:T(8,128)S(1)} %fast_apply.1.refs_3_, ...), custom_call_target="tpu_custom_call" | custom-call | flops 1048576 | bytes 1024 | tf_op jit(solution)/shard_map/mix_zero/pallas_call | solution.py:328
  121.4 1.6 %collective-permute-start.22 = (bf16[2,256,512]{2,1,0:T(8,128)(2,1)S(1)}, bf16[2,256,512]{2,1,0:T(8,128)(2,1)S(1)}, u32[]{:S(2)}, u32[]{:S(2)}) collective-permute-start(bf16[2,256,512]{2,1,0:T(8,128)(2,1)S(1)} %get-tuple-element.81), channel_id=1, source_target_pairs={{0,1},{1,0},{2,3},{3,2},{4,5},{5,4},{6,7},{7,6},{8,9},{9,8},{10,11... | collective-permute-start | bytes 1572872 | tf_op jit(solution)/shard_map/ppermute | solution.py:48
  123.0 2.7 %update_middle.1.in_ref = bf16[3,512,512]{2,1,0:T(8,128)(2,1)S(1)} custom-call(bf16[3,512,512]{2,1,0:T(8,128)(2,1)S(1)} %update_start.1.in_ref), custom_call_target="tpu_custom_call" | custom-call | flops 1048576 | bytes 1024 | tf_op jit(solution)/shard_map/update_middle/pallas_call | solution.py:440
  125.7 0.2 convert_add_fusion.1
  125.9 3.9 %collective-permute-start.23 = (bf16[256,512]{1,0:T(8,128)(2,1)S(1)}, bf16[256,512]{1,0:T(8,128)(2,1)S(1)}, u32[]{:S(2)}, u32[]{:S(2)}) collective-permute-start(bf16[256,512]{1,0:T(8,128)(2,1)S(1)} %fusion.5), channel_id=1, source_target_pairs={{0,2},{1,3},{2,0},{3,1},{4,6},{5,7},{6,4},{7,5},{8,10},{9,11},{10,... | collective-permute-start | bytes 786440 | tf_op jit(solution)/shard_map/ppermute | solution.py:48
  129.8 9.5 %update_end.1 = (f32[512,512]{1,0:T(8,128)}, f32[512,512]{1,0:T(8,128)}, f32[512,512]{1,0:T(8,128)}, f32[256,512]{1,0:T(8,128)S(1)}) custom-call(bf16[3,512,512]{2,1,0:T(8,128)(2,1)S(1)} %update_middle.1.in_ref, f32[512,512]{1,0:T(8,128)S(1)} %bitcast.41, f32[512,512]{1,0:T(8,128)S(1)} %bitcast.44, f32[512,512]{1,0:T(8,128)S(1)} %bitcast.47, ...), custom_call_target="tpu_custom_call" | custom-call | flops 1048576 | bytes 1024 | tf_op jit(solution)/shard_map/update_end/pallas_call | solution.py:446
  139.3 1.7 %mix_one.1 = (bf16[2,256,512]{2,1,0:T(8,128)(2,1)S(1)}, bf16[2,256,512]{2,1,0:T(8,128)(2,1)S(1)}) custom-call(s32[6]{0:T(128)S(1)} %stack.39.place.refs_0_, bf16[256,512]{1,0:T(8,128)(2,1)S(1)} %collective-permute-done.20.refs_1_, bf16[256,512]{1,0:T(8,128)(2,1)} %collective-permute-done.21.refs_2_, f32[256,512]{1,0:T(8,128)S(1)} %get-tuple-element.86.refs_3_, ...), custom_call_target="tpu_custom_call" | custom-call | flops 1048576 | bytes 1024 | tf_op jit(solution)/shard_map/mix_one/pallas_call | solution.py:328
  141.0 0.4 collective-permute-start.24
  141.4 1.6 %collective-permute-done.24 = bf16[2,256,512]{2,1,0:T(8,128)(2,1)S(1)} collective-permute-done((bf16[2,256,512]{2,1,0:T(8,128)(2,1)S(1)}, bf16[2,256,512]{2,1,0:T(8,128)(2,1)S(1)}, u32[]{:S(2)}, u32[]{:S(2)}) %collective-permute-start.24) | collective-permute-done | bytes 524320 | tf_op jit(solution)/shard_map/ppermute | solution.py:48
  143.0 0.2 convert_add_fusion
  143.2 1.1 collective-permute-start.25
  144.3 0.1 fusion.4
  144.4 8.0 %collective-permute-done.25 = bf16[256,512]{1,0:T(8,128)(2,1)S(1)} collective-permute-done((bf16[256,512]{1,0:T(8,128)(2,1)S(1)}, bf16[256,512]{1,0:T(8,128)(2,1)S(1)}, u32[]{:S(2)}, u32[]{:S(2)}) %collective-permute-start.25) | collective-permute-done | bytes 262176 | tf_op jit(solution)/shard_map/ppermute | solution.py:48
  152.4 0.1 fusion.6
  152.5 0.8 pad_maximum_fusion.3
  (58 shorter events, 0.3 us)
Async XLA Ops:
  0.8 1.6 %copy-start.8 = (bf16[2,256,2048]{2,1,0:T(8,128)(2,1)S(1)}, bf16[2,256,2048]{2,1,0:T(8,128)(2,1)}, u32[]{:S(2)}) copy-start(bf16[2,256,2048]{2,1,0:T(8,128)(2,1)} %tokens_ref.3) | copy-start | bytes 6291460
  2.4 2.8 %copy-start.10 = (bf16[2048,1,1536]{2,0,1:T(8,128)(2,1)S(1)}, bf16[2048,1,1536]{2,0,1:T(8,128)(2,1)}, u32[]{:S(2)}) copy-start(bf16[2048,1,1536]{2,0,1:T(8,128)(2,1)} %param.9) | copy-start | bytes 18874372
  5.2 10.1 %copy-start = (f32[1,512,512]{2,1,0:T(8,128)S(1)}, f32[1,512,512]{2,1,0:T(8,128)}, u32[]{:S(2)}) copy-start(f32[1,512,512]{2,1,0:T(8,128)} %param.13) | copy-start | bytes 3145732
  5.2 10.1 %copy-start.1 = (f32[1,512,512]{2,1,0:T(8,128)S(1)}, f32[1,512,512]{2,1,0:T(8,128)}, u32[]{:S(2)}) copy-start(f32[1,512,512]{2,1,0:T(8,128)} %param.14) | copy-start | bytes 3145732
  5.2 10.1 %copy-start.4 = (f32[1,512,512]{2,1,0:T(8,128)S(1)}, f32[1,512,512]{2,1,0:T(8,128)}, u32[]{:S(2)}) copy-start(f32[1,512,512]{2,1,0:T(8,128)} %param.15) | copy-start | bytes 3145732
  5.2 10.1 %copy-start.9 = (bf16[2,256,2048]{2,1,0:T(8,128)(2,1)S(1)}, bf16[2,256,2048]{2,1,0:T(8,128)(2,1)}, u32[]{:S(2)}) copy-start(bf16[2,256,2048]{2,1,0:T(8,128)(2,1)} %tokens_ref.3) | copy-start | bytes 6291460
  5.2 10.1 %copy-start.15 = (bf16[2048,1]{0,1:T(2,128)(2,1)S(1)}, bf16[2048,1]{0,1:T(2,128)(2,1)}, u32[]{:S(2)}) copy-start(bf16[2048,1]{0,1:T(2,128)(2,1)} %param.10) | copy-start | bytes 12292
  9.2 32.5 %collective-permute-start = (bf16[768,512]{1,0:T(8,128)(2,1)S(1)}, bf16[768,512]{1,0:T(8,128)(2,1)S(1)}, u32[]{:S(2)}, u32[]{:S(2)}) collective-permute-start(bf16[768,512]{1,0:T(8,128)(2,1)S(1)} %get-tuple-element.49), channel_id=1, source_target_pairs={{0,0},{1,8},{2,2},{3,10},{4,4},{5,12},{6,6},{7,14},{8,1},{9,9},{10... | collective-permute-start | bytes 2359304 | tf_op jit(solution)/shard_map/ppermute | solution.py:48
  13.8 28.0 %collective-permute-start.1 = (bf16[768,512]{1,0:T(8,128)(2,1)S(1)}, bf16[768,512]{1,0:T(8,128)(2,1)S(1)}, u32[]{:S(2)}, u32[]{:S(2)}) collective-permute-start(bf16[768,512]{1,0:T(8,128)(2,1)S(1)} %get-tuple-element.50), channel_id=1, source_target_pairs={{0,4},{1,12},{2,6},{3,14},{4,0},{5,8},{6,2},{7,10},{8,5},{9,13},{1... | collective-permute-start | bytes 2359304 | tf_op jit(solution)/shard_map/ppermute | solution.py:48
  17.4 11.3 %collective-permute-start.2 = (bf16[384,512]{1,0:T(8,128)(2,1)S(1)}, bf16[384,512]{1,0:T(8,128)(2,1)S(1)}, u32[]{:S(2)}, u32[]{:S(2)}) collective-permute-start(bf16[384,512]{1,0:T(8,128)(2,1)S(1)} %get-tuple-element.52), channel_id=1, source_target_pairs={{0,32},{1,33},{2,34},{3,35},{4,36},{5,37},{6,38},{7,39},{8,40},{9,... | collective-permute-start | bytes 1179656 | tf_op jit(solution)/shard_map/ppermute | solution.py:48
  18.7 19.0 %collective-permute-start.3 = (bf16[384,512]{1,0:T(8,128)(2,1)S(1)}, bf16[384,512]{1,0:T(8,128)(2,1)S(1)}, u32[]{:S(2)}, u32[]{:S(2)}) collective-permute-start(bf16[384,512]{1,0:T(8,128)(2,1)S(1)} %get-tuple-element.53), channel_id=1, source_target_pairs={{0,64},{1,65},{2,66},{3,67},{4,68},{5,69},{6,70},{7,71},{8,72},{9,... | collective-permute-start | bytes 1179656 | tf_op jit(solution)/shard_map/ppermute | solution.py:48
  21.1 19.7 %collective-permute-start.4 = (bf16[384,512]{1,0:T(8,128)(2,1)S(1)}, bf16[384,512]{1,0:T(8,128)(2,1)S(1)}, u32[]{:S(2)}, u32[]{:S(2)}) collective-permute-start(bf16[384,512]{1,0:T(8,128)(2,1)S(1)} %get-tuple-element.54), channel_id=1, source_target_pairs={{0,96},{1,97},{2,98},{3,99},{4,100},{5,101},{6,102},{7,103},{8,104... | collective-permute-start | bytes 1179656 | tf_op jit(solution)/shard_map/ppermute | solution.py:48
  42.8 23.2 %collective-permute-start.12 = (bf16[512,512]{1,0:T(8,128)(2,1)S(1)}, bf16[512,512]{1,0:T(8,128)(2,1)}, u32[]{:S(2)}, u32[]{:S(2)}) collective-permute-start(bf16[512,512]{1,0:T(8,128)(2,1)S(1)} %pad_maximum_fusion.1.own), channel_id=1, source_target_pairs={{0,32},{1,33},{2,34},{3,35},{4,36},{5,37},{6,38},{7,39},{8,40},{9,... | collective-permute-start | bytes 1572872 | tf_op jit(solution)/shard_map/ppermute | solution.py:48
  44.9 4.6 %collective-permute-start.5 = (bf16[96,512]{1,0:T(8,128)(2,1)S(1)}, bf16[96,512]{1,0:T(8,128)(2,1)S(1)}, u32[]{:S(2)}, u32[]{:S(2)}) collective-permute-start(bf16[96,512]{1,0:T(8,128)(2,1)S(1)} %get-tuple-element.58), channel_id=1, source_target_pairs={{0,8},{1,9},{2,10},{3,11},{4,12},{5,13},{6,14},{7,15},{8,0},{9,1},... | collective-permute-start | bytes 294920 | tf_op jit(solution)/shard_map/ppermute | solution.py:48
  44.9 8.1 %collective-permute-start.6 = (bf16[96,512]{1,0:T(8,128)(2,1)S(1)}, bf16[96,512]{1,0:T(8,128)(2,1)S(1)}, u32[]{:S(2)}, u32[]{:S(2)}) collective-permute-start(bf16[96,512]{1,0:T(8,128)(2,1)S(1)} %get-tuple-element.59), channel_id=1, source_target_pairs={{0,16},{1,17},{2,18},{3,19},{4,20},{5,21},{6,22},{7,23},{8,24},{9,... | collective-permute-start | bytes 294920 | tf_op jit(solution)/shard_map/ppermute | solution.py:48
  47.8 7.5 %collective-permute-start.7 = (bf16[96,512]{1,0:T(8,128)(2,1)S(1)}, bf16[96,512]{1,0:T(8,128)(2,1)S(1)}, u32[]{:S(2)}, u32[]{:S(2)}) collective-permute-start(bf16[96,512]{1,0:T(8,128)(2,1)S(1)} %get-tuple-element.60), channel_id=1, source_target_pairs={{0,24},{1,25},{2,26},{3,27},{4,28},{5,29},{6,30},{7,31},{8,16},{9,... | collective-permute-start | bytes 294920 | tf_op jit(solution)/shard_map/ppermute | solution.py:48
  55.3 4.9 %collective-permute-start.8 = (bf16[96,512]{1,0:T(8,128)(2,1)S(1)}, bf16[96,512]{1,0:T(8,128)(2,1)S(1)}, u32[]{:S(2)}, u32[]{:S(2)}) collective-permute-start(bf16[96,512]{1,0:T(8,128)(2,1)S(1)} %reduce_y.1.refs_0_), channel_id=1, source_target_pairs={{0,4},{1,5},{2,6},{3,7},{4,0},{5,1},{6,2},{7,3},{8,12},{9,13},{10,... | collective-permute-start | bytes 294920 | tf_op jit(solution)/shard_map/ppermute | solution.py:48
  60.2 10.7 %collective-permute-start.11 = (bf16[96,512]{1,0:T(8,128)(2,1)S(1)}, bf16[96,512]{1,0:T(8,128)(2,1)S(1)}, u32[]{:S(2)}, u32[]{:S(2)}) collective-permute-start(bf16[96,512]{1,0:T(8,128)(2,1)S(1)} %reduce_z.1), channel_id=1, source_target_pairs={{0,24},{1,25},{2,26},{3,27},{4,28},{5,29},{6,30},{7,31},{8,16},{9,... | collective-permute-start | bytes 294920 | tf_op jit(solution)/shard_map/ppermute | solution.py:48
  60.5 10.4 %collective-permute-start.10 = (bf16[96,512]{1,0:T(8,128)(2,1)S(1)}, bf16[96,512]{1,0:T(8,128)(2,1)S(1)}, u32[]{:S(2)}, u32[]{:S(2)}) collective-permute-start(bf16[96,512]{1,0:T(8,128)(2,1)S(1)} %reduce_z.1), channel_id=1, source_target_pairs={{0,16},{1,17},{2,18},{3,19},{4,20},{5,21},{6,22},{7,23},{8,24},{9,... | collective-permute-start | bytes 294920 | tf_op jit(solution)/shard_map/ppermute | solution.py:48
  63.5 7.5 %collective-permute-start.9 = (bf16[96,512]{1,0:T(8,128)(2,1)S(1)}, bf16[96,512]{1,0:T(8,128)(2,1)S(1)}, u32[]{:S(2)}, u32[]{:S(2)}) collective-permute-start(bf16[96,512]{1,0:T(8,128)(2,1)S(1)} %reduce_z.1), channel_id=1, source_target_pairs={{0,8},{1,9},{2,10},{3,11},{4,12},{5,13},{6,14},{7,15},{8,0},{9,1},... | collective-permute-start | bytes 294920 | tf_op jit(solution)/shard_map/ppermute | solution.py:48
  64.6 19.3 %copy-start.11 = (bf16[512,512]{1,0:T(8,128)(2,1)}, bf16[512,512]{1,0:T(8,128)(2,1)S(1)}, u32[]{:S(2)}) copy-start(bf16[512,512]{1,0:T(8,128)(2,1)S(1)} %pad_maximum_fusion.2.own) | copy-start | bytes 1572868
  64.6 11.5 %collective-permute-start.16 = (bf16[512,512]{1,0:T(8,128)(2,1)S(1)}, bf16[512,512]{1,0:T(8,128)(2,1)S(1)}, u32[]{:S(2)}, u32[]{:S(2)}) collective-permute-start(bf16[512,512]{1,0:T(8,128)(2,1)S(1)} %pad_maximum_fusion.2.own), channel_id=1, source_target_pairs={{0,32},{1,33},{2,34},{3,35},{4,36},{5,37},{6,38},{7,39},{8,40},{9,... | collective-permute-start | bytes 1572872 | tf_op jit(solution)/shard_map/ppermute | solution.py:48
  67.9 13.9 %collective-permute-start.13 = (bf16[512,512]{1,0:T(8,128)(2,1)S(1)}, bf16[512,512]{1,0:T(8,128)(2,1)}, u32[]{:S(2)}, u32[]{:S(2)}) collective-permute-start(bf16[512,512]{1,0:T(8,128)(2,1)S(1)} %get-tuple-element.95), channel_id=1, source_target_pairs={{0,16},{1,17},{2,18},{3,19},{4,20},{5,21},{6,22},{7,23},{8,24},{9,... | collective-permute-start | bytes 1572872 | tf_op jit(solution)/shard_map/ppermute | solution.py:48
  71.0 25.3 %collective-permute-start.15 = (bf16[512,512]{1,0:T(8,128)(2,1)}, bf16[512,512]{1,0:T(8,128)(2,1)}, u32[]{:S(2)}, u32[]{:S(2)}) collective-permute-start(bf16[512,512]{1,0:T(8,128)(2,1)} %get-tuple-element.94), channel_id=1, source_target_pairs={{0,1},{1,0},{2,3},{3,2},{4,5},{5,4},{6,7},{7,6},{8,9},{9,8},{10,11... | collective-permute-start | bytes 1572872 | tf_op jit(solution)/shard_map/ppermute | solution.py:48
  76.1 8.9 %copy-start.13 = (bf16[512,512]{1,0:T(8,128)(2,1)}, bf16[512,512]{1,0:T(8,128)(2,1)S(1)}, u32[]{:S(2)}) copy-start(bf16[512,512]{1,0:T(8,128)(2,1)S(1)} %collective-permute-done.16.two) | copy-start | bytes 1572868
  81.8 14.4 %collective-permute-start.14 = (bf16[512,512]{1,0:T(8,128)(2,1)}, bf16[512,512]{1,0:T(8,128)(2,1)}, u32[]{:S(2)}, u32[]{:S(2)}) collective-permute-start(bf16[512,512]{1,0:T(8,128)(2,1)} %collective-permute-done.13.one), channel_id=1, source_target_pairs={{0,1},{1,0},{2,3},{3,2},{4,5},{5,4},{6,7},{7,6},{8,9},{9,8},{10,11... | collective-permute-start | bytes 1572872 | tf_op jit(solution)/shard_map/ppermute | solution.py:48
  85.0 9.4 %copy-start.17 = (bf16[256,512]{1,0:T(8,128)(2,1)S(1)}, bf16[256,512]{1,0:T(8,128)(2,1)}, u32[]{:S(2)}) copy-start(bf16[256,512]{1,0:T(8,128)(2,1)} %get-tuple-element.98) | copy-start | bytes 786436
  85.0 16.9 %collective-permute-start.17 = (bf16[512,512]{1,0:T(8,128)(2,1)}, bf16[512,512]{1,0:T(8,128)(2,1)}, u32[]{:S(2)}, u32[]{:S(2)}) collective-permute-start(bf16[512,512]{1,0:T(8,128)(2,1)} %get-tuple-element.93), channel_id=1, source_target_pairs={{0,16},{1,17},{2,18},{3,19},{4,20},{5,21},{6,22},{7,23},{8,24},{9,... | collective-permute-start | bytes 1572872 | tf_op jit(solution)/shard_map/ppermute | solution.py:48
  88.0 26.8 %all-to-all-start = ((bf16[4,384,512]{2,1,0:T(8,128)(2,1)}), bf16[4,384,512]{2,1,0:T(8,128)(2,1)}, u32[]{:S(2)}, u32[]{:S(2)}) async-start(bf16[4,384,512]{2,1,0:T(8,128)(2,1)} %broadcast_in_dim.15), calls=%async_computation | async-start | bytes 3145728 | tf_op jit(solution)/shard_map/all_to_all | solution.py:402
  95.4 8.7 %copy-start.12 = (bf16[512,512]{1,0:T(8,128)(2,1)S(1)}, bf16[512,512]{1,0:T(8,128)(2,1)}, u32[]{:S(2)}) copy-start(bf16[512,512]{1,0:T(8,128)(2,1)} %copy-done.11) | copy-start | bytes 1572868
  95.4 8.7 %copy-start.14 = (bf16[512,512]{1,0:T(8,128)(2,1)S(1)}, bf16[512,512]{1,0:T(8,128)(2,1)}, u32[]{:S(2)}) copy-start(bf16[512,512]{1,0:T(8,128)(2,1)} %copy-done.13) | copy-start | bytes 1572868
  95.4 6.6 %collective-permute-start.19 = (bf16[512,512]{1,0:T(8,128)(2,1)}, bf16[512,512]{1,0:T(8,128)(2,1)S(1)}, u32[]{:S(2)}, u32[]{:S(2)}) collective-permute-start(bf16[512,512]{1,0:T(8,128)(2,1)} %get-tuple-element.92), channel_id=1, source_target_pairs={{0,1},{1,0},{2,3},{3,2},{4,5},{5,4},{6,7},{7,6},{8,9},{9,8},{10,11... | collective-permute-start | bytes 1572872 | tf_op jit(solution)/shard_map/ppermute | solution.py:48
  101.9 2.2 %collective-permute-start.18 = (bf16[512,512]{1,0:T(8,128)(2,1)}, bf16[512,512]{1,0:T(8,128)(2,1)S(1)}, u32[]{:S(2)}, u32[]{:S(2)}) collective-permute-start(bf16[512,512]{1,0:T(8,128)(2,1)} %collective-permute-done.17.one), channel_id=1, source_target_pairs={{0,1},{1,0},{2,3},{3,2},{4,5},{5,4},{6,7},{7,6},{8,9},{9,8},{10,11... | collective-permute-start | bytes 1572872 | tf_op jit(solution)/shard_map/ppermute | solution.py:48
  104.1 8.5 %copy-start.2 = (f32[1,512,512]{2,1,0:T(8,128)S(1)}, f32[1,512,512]{2,1,0:T(8,128)}, u32[]{:S(2)}) copy-start(f32[1,512,512]{2,1,0:T(8,128)} %param.14) | copy-start | bytes 3145732
  104.1 8.5 %copy-start.5 = (f32[1,512,512]{2,1,0:T(8,128)S(1)}, f32[1,512,512]{2,1,0:T(8,128)}, u32[]{:S(2)}) copy-start(f32[1,512,512]{2,1,0:T(8,128)} %param.15) | copy-start | bytes 3145732
  104.1 8.5 %copy-start.16 = (f32[1,512]{1,0:T(1,128)S(1)}, f32[1,512]{1,0:T(1,128)}, u32[]{:S(2)}) copy-start(f32[1,512]{1,0:T(1,128)} %gain_ref.3) | copy-start | bytes 6148
  107.6 12.1 %collective-permute-start.20 = (bf16[256,512]{1,0:T(8,128)(2,1)}, bf16[256,512]{1,0:T(8,128)(2,1)S(1)}, u32[]{:S(2)}, u32[]{:S(2)}) collective-permute-start(bf16[256,512]{1,0:T(8,128)(2,1)} %get-tuple-element.73), channel_id=1, source_target_pairs={{0,0},{1,8},{2,2},{3,10},{4,4},{5,12},{6,6},{7,14},{8,1},{9,9},{10... | collective-permute-start | bytes 786440 | tf_op jit(solution)/shard_map/ppermute | solution.py:48
  109.8 9.9 %collective-permute-start.21 = (bf16[256,512]{1,0:T(8,128)(2,1)}, bf16[256,512]{1,0:T(8,128)(2,1)}, u32[]{:S(2)}, u32[]{:S(2)}) collective-permute-start(bf16[256,512]{1,0:T(8,128)(2,1)} %get-tuple-element.74), channel_id=1, source_target_pairs={{0,4},{1,12},{2,6},{3,14},{4,0},{5,8},{6,2},{7,10},{8,5},{9,13},{1... | collective-permute-start | bytes 786440 | tf_op jit(solution)/shard_map/ppermute | solution.py:48
  114.8 4.9 %copy-start.7 = (bf16[1,512,2048]{2,1,0:T(8,128)(2,1)S(1)}, bf16[1,512,2048]{2,1,0:T(8,128)(2,1)}, u32[]{:S(2)}) copy-start(bf16[1,512,2048]{2,1,0:T(8,128)(2,1)} %param.11) | copy-start | bytes 6291460
  121.4 4.3 %collective-permute-start.22 = (bf16[2,256,512]{2,1,0:T(8,128)(2,1)S(1)}, bf16[2,256,512]{2,1,0:T(8,128)(2,1)S(1)}, u32[]{:S(2)}, u32[]{:S(2)}) collective-permute-start(bf16[2,256,512]{2,1,0:T(8,128)(2,1)S(1)} %get-tuple-element.81), channel_id=1, source_target_pairs={{0,1},{1,0},{2,3},{3,2},{4,5},{5,4},{6,7},{7,6},{8,9},{9,8},{10,11... | collective-permute-start | bytes 1572872 | tf_op jit(solution)/shard_map/ppermute | solution.py:48
  125.7 4.1 %copy-start.3 = (f32[1,512,512]{2,1,0:T(8,128)S(1)}, f32[1,512,512]{2,1,0:T(8,128)}, u32[]{:S(2)}) copy-start(f32[1,512,512]{2,1,0:T(8,128)} %param.14) | copy-start | bytes 3145732
  125.7 4.1 %copy-start.6 = (f32[1,512,512]{2,1,0:T(8,128)S(1)}, f32[1,512,512]{2,1,0:T(8,128)}, u32[]{:S(2)}) copy-start(f32[1,512,512]{2,1,0:T(8,128)} %param.15) | copy-start | bytes 3145732
  125.9 13.4 %collective-permute-start.23 = (bf16[256,512]{1,0:T(8,128)(2,1)S(1)}, bf16[256,512]{1,0:T(8,128)(2,1)S(1)}, u32[]{:S(2)}, u32[]{:S(2)}) collective-permute-start(bf16[256,512]{1,0:T(8,128)(2,1)S(1)} %fusion.5), channel_id=1, source_target_pairs={{0,2},{1,3},{2,0},{3,1},{4,6},{5,7},{6,4},{7,5},{8,10},{9,11},{10,... | collective-permute-start | bytes 786440 | tf_op jit(solution)/shard_map/ppermute | solution.py:48
  141.0 2.0 %collective-permute-start.24 = (bf16[2,256,512]{2,1,0:T(8,128)(2,1)S(1)}, bf16[2,256,512]{2,1,0:T(8,128)(2,1)S(1)}, u32[]{:S(2)}, u32[]{:S(2)}) collective-permute-start(bf16[2,256,512]{2,1,0:T(8,128)(2,1)S(1)} %get-tuple-element.88), channel_id=1, source_target_pairs={{0,1},{1,0},{2,3},{3,2},{4,5},{5,4},{6,7},{7,6},{8,9},{9,8},{10,11... | collective-permute-start | bytes 1572872 | tf_op jit(solution)/shard_map/ppermute | solution.py:48
  143.2 9.2 %collective-permute-start.25 = (bf16[256,512]{1,0:T(8,128)(2,1)S(1)}, bf16[256,512]{1,0:T(8,128)(2,1)S(1)}, u32[]{:S(2)}, u32[]{:S(2)}) collective-permute-start(bf16[256,512]{1,0:T(8,128)(2,1)S(1)} %fusion.7), channel_id=1, source_target_pairs={{0,2},{1,3},{2,0},{3,1},{4,6},{5,7},{6,4},{7,5},{8,10},{9,11},{10,... | collective-permute-start | bytes 786440 | tf_op jit(solution)/shard_map/ppermute | solution.py:48

commit v2 on v1

--- a/solution.py
+++ b/solution.py
@@ -7,7 +7,7 @@
 
 NS_STEPS = 5
 FIRST_STEPS = 1
-MIDDLE_STEPS = 1
+MIDDLE_STEPS = 2
 HALF = 256
 SUPER = 512
 REACH = 4
@@ -100,30 +100,60 @@
     )
 
 
-CHUNK = 256
-CHUNKS = 6
-
-
-def project(place, tokens_ref, w_ref, natural_ref, same, other):
+CHUNKS = 4
+DEPTH = 512
+
+
+def project(place, tokens_ref, w_ref, natural_ref, same, other, tokens_held, held, total, sems):
+    copies = []
+    for j in range(CHUNKS):
+        rows = pl.ds(j * DEPTH, DEPTH)
+        copies.append(
+            (
+                pltpu.make_async_copy(
+                    tokens_ref.at[:, :, rows], tokens_held.at[:, :, rows], sems.at[CHUNKS + j]
+                ),
+                pltpu.make_async_copy(w_ref.at[rows], held.at[rows], sems.at[j]),
+            )
+        )
+    for pair in copies:
+        for copy in pair:
+            copy.start()
     z = place[0]
-    tokens = tokens_ref[...].reshape(2 * HALF, -1)
-    for j in (2, 3, 0, 1, 4, 5):
-        columns = slice(j * CHUNK, (j + 1) * CHUNK)
-        result = nn(tokens, w_ref[:, columns]).astype(BF)
-        low, high = result[:HALF], result[HALF:]
-        natural_ref[0, :, columns] = low
-        natural_ref[1, :, columns] = high
-        part = slice((j % 2) * CHUNK, (j % 2 + 1) * CHUNK)
-        rows = slice(j // 2 * HALF, (j // 2 + 1) * HALF)
-        same[rows, part] = jnp.where(z == 0, low, high)
-        other[rows, part] = jnp.where(z == 0, high, low)
+    for j, pair in enumerate(copies):
+        for copy in pair:
+            copy.wait()
+        depth = slice(j * DEPTH, (j + 1) * DEPTH)
+        tokens = tokens_held[:, :, depth].reshape(2 * HALF, DEPTH)
+        for at in range(3):
+            columns = slice(at * 512, (at + 1) * 512)
+            part = nn(tokens, held[depth, columns])
+            if j == 0:
+                total[:, columns] = part
+            elif j < CHUNKS - 1:
+                total[:, columns] += part
+            else:
+                result = (total[:, columns] + part).astype(BF)
+                low, high = result[:HALF], result[HALF:]
+                natural_ref[0, :, columns] = low
+                natural_ref[1, :, columns] = high
+                rows = slice(at * HALF, (at + 1) * HALF)
+                same[rows] = jnp.where(z == 0, low, high)
+                other[rows] = jnp.where(z == 0, high, low)
 
 
 def run_project(place, tokens, weights):
     return call(
         project,
-        [smem(), vmem(), vmem()],
+        [smem()] + [pl.BlockSpec(memory_space=pltpu.HBM)] * 2,
         [((2, HALF, 1536), BF)] + [((3 * HALF, 512), BF)] * 2,
+        scratch=(
+            pltpu.VMEM((2, HALF, 2048), BF),
+            pltpu.VMEM((2048, 1536), BF),
+            pltpu.VMEM((SUPER, 1536), F32),
+            pltpu.SemaphoreType.DMA((2 * CHUNKS,)),
+        ),
+        limit=50,
     )(place, tokens, weights)
 
 
@@ -413,19 +443,7 @@
         [((5, SUPER, SUPER), BF), ((SUPER, 128), F32)],
         scratch=(pltpu.VMEM((5, ROWS, SUPER), F32),),
     )(place, queries, own_keys, swap_one_keys, one_keys, swap_two_keys, two_keys)
-    (one_values,) = ordered([one_values], weights)
-    swap_one_values = moved(one_values, other_core)
-    near, far = call(gathered, [vmem()] * 7, [((HALF, 512), BF)] * 2)(
-        weights, sums, own_values, swap_one_values, one_values, swap_two_values, two_values
-    )
-    parts = ordered(parts, near, far)
-    near = moved(near, to_role_same)
-    far = moved(far, to_role_other)
-
-    (normed_zero,) = call(
-        fast_apply, [vmem()] * 5, [((HALF, 512), F32)]
-    )(natural, first, third, second, fw_gain)
-    normed_zero, near, far = ordered([normed_zero, near, far], *parts)
+    parts = ordered(parts, weights)
     (held,) = call(
         update_start,
         [smem(), vmem()],
@@ -433,16 +451,23 @@
         scratch=(pltpu.VMEM((1536, 512), BF),),
         limit=24,
     )(place, *parts)
-    (normed_zero,) = ordered([normed_zero], held)
+    (one_values,) = ordered([one_values], weights, held)
+    swap_one_values = moved(one_values, other_core)
+    near, far = call(gathered, [vmem()] * 7, [((HALF, 512), BF)] * 2)(
+        weights, sums, own_values, swap_one_values, one_values, swap_two_values, two_values
+    )
+    (held,) = ordered([held], near, far)
+    near = moved(near, to_role_same)
+    far = moved(far, to_role_other)
+
+    (normed_zero,) = call(
+        fast_apply, [vmem()] * 5, [((HALF, 512), F32)]
+    )(natural, first, third, second, fw_gain)
+    (held,) = call(update_middle, [vmem()], [((3, 512, 512), BF)], limit=24)(held)
+    normed_zero, near, far = ordered([normed_zero, near, far], held)
     keep, send = mixed_by(mix_zero, place, near, far, normed_zero, w_out[0])
     (held,) = ordered([held], send)
     taken = moved(send, other_core)
-    (held,) = call(update_middle, [vmem()], [((3, 512, 512), BF)], limit=24)(held)
-    (taken,) = ordered([taken], held)
-    half_zero = keep.astype(F32) + taken.astype(F32)
-    crossing = half_zero[1].astype(BF)
-    (held,) = ordered([held], crossing)
-    crossing = moved(crossing, other_pair)
     new_first, new_third, new_second, normed_one = call(
         update_end,
         [vmem()] * 6,
@@ -450,7 +475,11 @@
         scratch=(pltpu.VMEM((3, 512, 512), BF),),
         limit=24,
     )(held, first, third, second, natural, fw_gain)
+    (taken,) = ordered([taken], normed_one)
+    half_zero = keep.astype(F32) + taken.astype(F32)
+    crossing = half_zero[1].astype(BF)
     (normed_one,) = ordered([normed_one], crossing)
+    crossing = moved(crossing, other_pair)
     keep, send = mixed_by(mix_one, place, near, far, normed_one, w_out[0])
     half_one = keep.astype(F32) + moved(send, other_core).astype(F32)
     done_zero = half_zero[0] + crossing.astype(F32)

time: 154 us -> 148 us (0.961)
  waiting for transfers between devices: 51.7 us -> 45.2 us
  local copies, waits for them, and re-layouts: 6.98 us -> 4.08 us
    ppermute x26, waiting for transfers between devices: 50.3 us -> 45.2 us  [moved(): return lax.ppermute(value, ('ctx', 'head'), pairs)]
    pallas_call x1, Pallas kernels: 9.52 us -> 6.42 us  [shards(): call(update_end, [vmem()] * 6, [((512, 512), F32)] * 3 + [((HALF, 512), F...]
    unnamed x39 -> x29, local copies, waits for them, and re-layouts: 4.48 us -> 1.56 us
    pallas_call x1, Pallas kernels: 2.71 us -> 5.49 us  [shards(): held, = call(update_middle, [vmem()], [((3, 512, 512), BF)], limit=24)(held)]
    pallas_call x1, Pallas kernels: 3.99 us -> 6.24 us  [run_project(): call(project, [smem()] + [pl.BlockSpec(memory_space=pltpu.HBM)] * 2, [((2...]
    ppermute x26, starting transfers between devices: 43.4 us -> 45.6 us  [moved(): return lax.ppermute(value, ('ctx', 'head'), pairs)]
  transfers between devices with their start and end apart: 27 -> 27, of which waited for: 13 -> 13; matrix products, arithmetic and copies ran while one was open for 4% -> 5% of each run, Pallas kernels for 20% -> 18%
where the time goes in v2:
time: 148 us; the launch traced here: 147 us
  starting transfers between devices  51.3 us (35%)
  waiting for transfers between devices  45.2 us (31%)
  Pallas kernels  38 us (26%)
  other arithmetic  7.53 us (5%)
  local copies, waits for them, and re-layouts  4.08 us (3%)
    ppermute x26, starting transfers between devices, moved(): return lax.ppermute(value, ('ctx', 'head'), pairs)  45.6 us
    ppermute x26, waiting for transfers between devices, moved(): return lax.ppermute(value, ('ctx', 'head'), pairs)  45.2 us
    pallas_call x1, Pallas kernels, shards(): call(update_end, [vmem()] * 6, [((512, 512), F32)] * 3 + [((HALF, 512), F...  6.42 us
    pallas_call x1, Pallas kernels, run_project(): call(project, [smem()] + [pl.BlockSpec(memory_space=pltpu.HBM)] * 2, [((2...  6.24 us
    all_to_all x1, starting transfers between devices, shards(): lax.all_to_all(sent, 'ctx', 0, 0, axis_index_groups=lines, tiled=True)  5.69 us
    pallas_call x1, Pallas kernels, shards(): held, = call(update_middle, [vmem()], [((3, 512, 512), BF)], limit=24)(held)  5.49 us
    pallas_call x1, Pallas kernels, shards(): call(scores, [smem()] + [vmem()] * 6, [((5, SUPER, SUPER), BF), ((SUPER,...  5.33 us
    pallas_call x1, Pallas kernels, shards(): call(update_start, [smem(), vmem()], [((3, 512, 512), BF)], scratch=(pltp...  4.9 us
  transfers between devices with their start and end apart: 27, of which 13 were waited for; matrix products, arithmetic and copies ran while one was open for 5% of the time, Pallas kernels for 18%

profile of v2, /device:TPU:1, one launch (start us, length us, event | category | flops | bytes accessed | tf_op | source)
XLA Modules:
  0.0 147.1 jit_solution(1544262600604060953)
XLA Ops:
  0.7 0.1 stack.39.place.refs_0_
  0.8 6.2 %project.1 = (bf16[2,256,1536]{2,1,0:T(8,128)(2,1)S(1)}, bf16[768,512]{1,0:T(8,128)(2,1)S(1)}, bf16[768,512]{1,0:T(8,128)(2,1)S(1)}) custom-call(s32[6]{0:T(128)S(1)} %stack.39.place.refs_0_, bf16[2,256,2048]{2,1,0:T(8,128)(2,1)} %tokens_ref.3, bf16[2048,1536]{1,0:T(8,128)(2,1)} %bitcast.51), custom_call_target="tpu_custom_call" | custom-call | flops 1048576 | bytes 1024 | tf_op jit(solution)/shard_map/project/pallas_call | solution.py:146
  7.1 4.6 %collective-permute-start = (bf16[768,512]{1,0:T(8,128)(2,1)S(1)}, bf16[768,512]{1,0:T(8,128)(2,1)S(1)}, u32[]{:S(2)}, u32[]{:S(2)}) collective-permute-start(bf16[768,512]{1,0:T(8,128)(2,1)S(1)} %get-tuple-element.48), channel_id=1, source_target_pairs={{0,0},{1,8},{2,2},{3,10},{4,4},{5,12},{6,6},{7,14},{8,1},{9,9},{10... | collective-permute-start | bytes 2359304 | tf_op jit(solution)/shard_map/ppermute | solution.py:48
  11.7 1.4 collective-permute-start.1
  13.1 2.1 %fast_grads.1 = (bf16[384,512]{1,0:T(8,128)(2,1)S(1)}, bf16[384,512]{1,0:T(8,128)(2,1)S(1)}, bf16[384,512]{1,0:T(8,128)(2,1)S(1)}, bf16[384,512]{1,0:T(8,128)(2,1)S(1)}) custom-call(s32[6]{0:T(128)S(1)} %stack.39.place.refs_0_, bf16[2,256,2048]{2,1,0:T(8,128)(2,1)S(1)} %copy-done.6, bf16[1,2048]{1,0:T(2,128)(2,1)S(1)} %bitcast.50, ...), custom_call_target="tpu_custom_call" | custom-call | flops 1048576 | bytes 1024 | tf_op jit(solution)/shard_map/fast_grads/pallas_call | solution.py:394
  15.2 1.3 collective-permute-start.2
  16.5 2.4 %collective-permute-start.3 = (bf16[384,512]{1,0:T(8,128)(2,1)S(1)}, bf16[384,512]{1,0:T(8,128)(2,1)S(1)}, u32[]{:S(2)}, u32[]{:S(2)}) collective-permute-start(bf16[384,512]{1,0:T(8,128)(2,1)S(1)} %get-tuple-element.52), channel_id=1, source_target_pairs={{0,64},{1,65},{2,66},{3,67},{4,68},{5,69},{6,70},{7,71},{8,72},{9,... | collective-permute-start | bytes 1179656 | tf_op jit(solution)/shard_map/ppermute | solution.py:48
  19.0 0.2 collective-permute-start.4
  19.2 7.3 %collective-permute-done.2.refs_1_ = bf16[384,512]{1,0:T(8,128)(2,1)S(1)} collective-permute-done((bf16[384,512]{1,0:T(8,128)(2,1)S(1)}, bf16[384,512]{1,0:T(8,128)(2,1)S(1)}, u32[]{:S(2)}, u32[]{:S(2)}) %collective-permute-start.2) | collective-permute-done | bytes 393248 | tf_op jit(solution)/shard_map/ppermute | solution.py:48
  26.5 9.0 %collective-permute-done.3.refs_2_ = bf16[384,512]{1,0:T(8,128)(2,1)S(1)} collective-permute-done((bf16[384,512]{1,0:T(8,128)(2,1)S(1)}, bf16[384,512]{1,0:T(8,128)(2,1)S(1)}, u32[]{:S(2)}, u32[]{:S(2)}) %collective-permute-start.3) | collective-permute-done | bytes 393248 | tf_op jit(solution)/shard_map/ppermute | solution.py:48
  35.5 3.1 %collective-permute-done.4.refs_3_ = bf16[384,512]{1,0:T(8,128)(2,1)S(1)} collective-permute-done((bf16[384,512]{1,0:T(8,128)(2,1)S(1)}, bf16[384,512]{1,0:T(8,128)(2,1)S(1)}, u32[]{:S(2)}, u32[]{:S(2)}) %collective-permute-start.4) | collective-permute-done | bytes 393248 | tf_op jit(solution)/shard_map/ppermute | solution.py:48
  38.7 0.9 reduce_x.1
  39.6 1.0 fusion.8
  40.7 2.1 %collective-permute-start.12 = (bf16[512,512]{1,0:T(8,128)(2,1)S(1)}, bf16[512,512]{1,0:T(8,128)(2,1)}, u32[]{:S(2)}, u32[]{:S(2)}) collective-permute-start(bf16[512,512]{1,0:T(8,128)(2,1)S(1)} %pad_maximum_fusion.1.own), channel_id=1, source_target_pairs={{0,32},{1,33},{2,34},{3,35},{4,36},{5,37},{6,38},{7,39},{8,40},{9,... | collective-permute-start | bytes 1572872 | tf_op jit(solution)/shard_map/ppermute | solution.py:48
  42.8 2.9 %collective-permute-start.6 = (bf16[96,512]{1,0:T(8,128)(2,1)S(1)}, bf16[96,512]{1,0:T(8,128)(2,1)S(1)}, u32[]{:S(2)}, u32[]{:S(2)}) collective-permute-start(bf16[96,512]{1,0:T(8,128)(2,1)S(1)} %get-tuple-element.58), channel_id=1, source_target_pairs={{0,16},{1,17},{2,18},{3,19},{4,20},{5,21},{6,22},{7,23},{8,24},{9,... | collective-permute-start | bytes 294920 | tf_op jit(solution)/shard_map/ppermute | solution.py:48
  45.7 0.9 collective-permute-start.7
  46.6 0.7 collective-permute-done.5.refs_1_
  47.3 3.6 %collective-permute-done.6.refs_2_ = bf16[96,512]{1,0:T(8,128)(2,1)S(1)} collective-permute-done((bf16[96,512]{1,0:T(8,128)(2,1)S(1)}, bf16[96,512]{1,0:T(8,128)(2,1)S(1)}, u32[]{:S(2)}, u32[]{:S(2)}) %collective-permute-start.6) | collective-permute-done | bytes 98336 | tf_op jit(solution)/shard_map/ppermute | solution.py:48
  50.9 2.3 %collective-permute-done.7.refs_3_ = bf16[96,512]{1,0:T(8,128)(2,1)S(1)} collective-permute-done((bf16[96,512]{1,0:T(8,128)(2,1)S(1)}, bf16[96,512]{1,0:T(8,128)(2,1)S(1)}, u32[]{:S(2)}, u32[]{:S(2)}) %collective-permute-start.7) | collective-permute-done | bytes 98336 | tf_op jit(solution)/shard_map/ppermute | solution.py:48
  53.2 0.1 reduce_y.1.refs_0_
  53.2 0.1 collective-permute-start.8
  53.3 4.8 %collective-permute-done.8.refs_1_ = bf16[96,512]{1,0:T(8,128)(2,1)S(1)} collective-permute-done((bf16[96,512]{1,0:T(8,128)(2,1)S(1)}, bf16[96,512]{1,0:T(8,128)(2,1)S(1)}, u32[]{:S(2)}, u32[]{:S(2)}) %collective-permute-start.8) | collective-permute-done | bytes 98336 | tf_op jit(solution)/shard_map/ppermute | solution.py:48
  58.2 0.3 collective-permute-start.11
  58.4 2.9 %collective-permute-start.10 = (bf16[96,512]{1,0:T(8,128)(2,1)S(1)}, bf16[96,512]{1,0:T(8,128)(2,1)S(1)}, u32[]{:S(2)}, u32[]{:S(2)}) collective-permute-start(bf16[96,512]{1,0:T(8,128)(2,1)S(1)} %reduce_z.1), channel_id=1, source_target_pairs={{0,16},{1,17},{2,18},{3,19},{4,20},{5,21},{6,22},{7,23},{8,24},{9,... | collective-permute-start | bytes 294920 | tf_op jit(solution)/shard_map/ppermute | solution.py:48
  61.4 0.1 collective-permute-start.9
  61.5 1.9 %pad_maximum_fusion.2.own = bf16[512,512]{1,0:T(8,128)(2,1)} fusion(bf16[256,512]{1,0:T(8,128)(2,1)} %get-tuple-element.102, bf16[256,512]{1,0:T(8,128)(2,1)} %get-tuple-element.94), kind=kLoop, calls=%fused_computation.12 | loop fusion | flops 1048576 | bytes 1048576 | tf_op jit(solution)/shard_map/concatenate | solution.py:404
  63.3 2.1 %collective-permute-start.16 = (bf16[512,512]{1,0:T(8,128)(2,1)}, bf16[512,512]{1,0:T(8,128)(2,1)}, u32[]{:S(2)}, u32[]{:S(2)}) collective-permute-start(bf16[512,512]{1,0:T(8,128)(2,1)} %pad_maximum_fusion.2.own), channel_id=1, source_target_pairs={{0,32},{1,33},{2,34},{3,35},{4,36},{5,37},{6,38},{7,39},{8,40},{9,... | collective-permute-start | bytes 1572872 | tf_op jit(solution)/shard_map/ppermute | solution.py:48
  65.4 2.1 %broadcast_select_fusion.1 = (bf16[512,512]{1,0:T(8,128)(2,1)}, bf16[512,512]{1,0:T(8,128)(2,1)}) fusion(bf16[512,512]{1,0:T(8,128)(2,1)S(1)} %pad_maximum_fusion.1.own, bf16[512,512]{1,0:T(8,128)(2,1)} %collective-permute-done.12.two, pred[]{:T(512)S(6)} %eq.8, pred[]{:T(512)S(6)} %ge.4), kind=kLoop, calls=%fused_computation.15 | loop fusion | flops 524288 | bytes 2097154 | tf_op jit(solution)/shard_map/jit(_where)/select_n | solution.py:422
  67.5 3.1 %collective-permute-start.13 = (bf16[512,512]{1,0:T(8,128)(2,1)}, bf16[512,512]{1,0:T(8,128)(2,1)}, u32[]{:S(2)}, u32[]{:S(2)}) collective-permute-start(bf16[512,512]{1,0:T(8,128)(2,1)} %get-tuple-element.93), channel_id=1, source_target_pairs={{0,16},{1,17},{2,18},{3,19},{4,20},{5,21},{6,22},{7,23},{8,24},{9,... | collective-permute-start | bytes 1572872 | tf_op jit(solution)/shard_map/ppermute | solution.py:48
  70.7 1.3 broadcast_in_dim.15
  72.0 5.7 %all-to-all-start = ((bf16[4,384,512]{2,1,0:T(8,128)(2,1)}), bf16[4,384,512]{2,1,0:T(8,128)(2,1)}, u32[]{:S(2)}, u32[]{:S(2)}) async-start(bf16[4,384,512]{2,1,0:T(8,128)(2,1)} %broadcast_in_dim.15), calls=%async_computation | async-start | bytes 3145728 | tf_op jit(solution)/shard_map/all_to_all | solution.py:432
  77.7 2.2 %collective-permute-start.15 = (bf16[512,512]{1,0:T(8,128)(2,1)}, bf16[512,512]{1,0:T(8,128)(2,1)S(1)}, u32[]{:S(2)}, u32[]{:S(2)}) collective-permute-start(bf16[512,512]{1,0:T(8,128)(2,1)} %get-tuple-element.92), channel_id=1, source_target_pairs={{0,1},{1,0},{2,3},{3,2},{4,5},{5,4},{6,7},{7,6},{8,9},{9,8},{10,11... | collective-permute-start | bytes 1572872 | tf_op jit(solution)/shard_map/ppermute | solution.py:48
  79.9 1.8 %collective-permute-done.13.one = bf16[512,512]{1,0:T(8,128)(2,1)} collective-permute-done((bf16[512,512]{1,0:T(8,128)(2,1)}, bf16[512,512]{1,0:T(8,128)(2,1)}, u32[]{:S(2)}, u32[]{:S(2)}) %collective-permute-start.13) | collective-permute-done | bytes 524320 | tf_op jit(solution)/shard_map/ppermute | solution.py:48
  81.6 2.1 %collective-permute-start.14 = (bf16[512,512]{1,0:T(8,128)(2,1)}, bf16[512,512]{1,0:T(8,128)(2,1)S(1)}, u32[]{:S(2)}, u32[]{:S(2)}) collective-permute-start(bf16[512,512]{1,0:T(8,128)(2,1)} %collective-permute-done.13.one), channel_id=1, source_target_pairs={{0,1},{1,0},{2,3},{3,2},{4,5},{5,4},{6,7},{7,6},{8,9},{9,8},{10,11... | collective-permute-start | bytes 1572872 | tf_op jit(solution)/shard_map/ppermute | solution.py:48
  83.8 2.2 %broadcast_select_fusion = (bf16[512,512]{1,0:T(8,128)(2,1)}, bf16[512,512]{1,0:T(8,128)(2,1)}) fusion(bf16[512,512]{1,0:T(8,128)(2,1)} %pad_maximum_fusion.2.own, bf16[512,512]{1,0:T(8,128)(2,1)} %collective-permute-done.16.two, pred[]{:T(512)S(6)} %eq.8, pred[]{:T(512)S(6)} %ge.4), kind=kLoop, calls=%fused_computation.14 | loop fusion | flops 524288 | bytes 2097154 | tf_op jit(solution)/shard_map/jit(_where)/select_n | solution.py:422
  86.0 3.0 %collective-permute-start.17 = (bf16[512,512]{1,0:T(8,128)(2,1)}, bf16[512,512]{1,0:T(8,128)(2,1)}, u32[]{:S(2)}, u32[]{:S(2)}) collective-permute-start(bf16[512,512]{1,0:T(8,128)(2,1)} %get-tuple-element.91), channel_id=1, source_target_pairs={{0,16},{1,17},{2,18},{3,19},{4,20},{5,21},{6,22},{7,23},{8,24},{9,... | collective-permute-start | bytes 1572872 | tf_op jit(solution)/shard_map/ppermute | solution.py:48
  89.0 0.5 collective-permute-start.19
  89.6 5.3 %scores.1 = (bf16[5,512,512]{2,1,0:T(8,128)(2,1)S(1)}, f32[512,128]{1,0:T(8,128)S(1)}) custom-call(s32[6]{0:T(128)S(1)} %stack.39.place.refs_0_, bf16[512,512]{1,0:T(8,128)(2,1)S(1)} %pad_maximum_fusion.queries_ref, bf16[512,512]{1,0:T(8,128)(2,1)S(1)} %pad_maximum_fusion.1.own, bf16[512,512]{1,0:T(8,128)(2,1)S(1)} %collective-permute-done.14.swap_one, ...), custom_call_target="tpu_custom_call" | custom-call | flops 1048576 | bytes 1024 | tf_op jit(solution)/shard_map/scores/pallas_call | solution.py:440
  94.9 1.5 %copy-done.7 = bf16[5,512,512]{2,1,0:T(8,128)(2,1)} copy-done((bf16[5,512,512]{2,1,0:T(8,128)(2,1)}, bf16[5,512,512]{2,1,0:T(8,128)(2,1)S(1)}, u32[]{:S(2)}) %copy-start.7) | copy-done | bytes 2621464
  96.4 4.9 %update_start.1.in_ref = bf16[3,512,512]{2,1,0:T(8,128)(2,1)S(1)} custom-call(s32[6]{0:T(128)S(1)} %stack.39.place.refs_0_, bf16[4,384,512]{2,1,0:T(8,128)(2,1)} %all-to-all-done.parts_ref), custom_call_target="tpu_custom_call" | custom-call | flops 1048576 | bytes 1024 | tf_op jit(solution)/shard_map/update_start/pallas_call | solution.py:447
  101.3 0.1 collective-permute-done.17.one
  101.4 3.5 %collective-permute-start.18 = (bf16[512,512]{1,0:T(8,128)(2,1)}, bf16[512,512]{1,0:T(8,128)(2,1)S(1)}, u32[]{:S(2)}, u32[]{:S(2)}) collective-permute-start(bf16[512,512]{1,0:T(8,128)(2,1)} %collective-permute-done.17.one), channel_id=1, source_target_pairs={{0,1},{1,0},{2,3},{3,2},{4,5},{5,4},{6,7},{7,6},{8,9},{9,8},{10,11... | collective-permute-start | bytes 1572872 | tf_op jit(solution)/shard_map/ppermute | solution.py:48
  104.9 1.7 %collective-permute-done.18.swap_one = bf16[512,512]{1,0:T(8,128)(2,1)S(1)} collective-permute-done((bf16[512,512]{1,0:T(8,128)(2,1)}, bf16[512,512]{1,0:T(8,128)(2,1)S(1)}, u32[]{:S(2)}, u32[]{:S(2)}) %collective-permute-start.18) | collective-permute-done | bytes 524320 | tf_op jit(solution)/shard_map/ppermute | solution.py:48
  106.6 3.2 %gathered.1 = (bf16[256,512]{1,0:T(8,128)(2,1)S(1)}, bf16[256,512]{1,0:T(8,128)(2,1)S(1)}) custom-call(bf16[5,512,512]{2,1,0:T(8,128)(2,1)S(1)} %copy-done.8, f32[512,128]{1,0:T(8,128)S(1)} %get-tuple-element.68.sum_ref, bf16[512,512]{1,0:T(8,128)(2,1)} %pad_maximum_fusion.2.own, bf16[512,512]{1,0:T(8,128)(2,1)S(1)} %collective-permute-done.18.swap_one, ...), custom_call_target="tpu_custom_call" | custom-call | flops 1048576 | bytes 1024 | tf_op jit(solution)/shard_map/gathered/pallas_call | solution.py:456
  109.8 3.5 %collective-permute-start.20 = (bf16[256,512]{1,0:T(8,128)(2,1)S(1)}, bf16[256,512]{1,0:T(8,128)(2,1)S(1)}, u32[]{:S(2)}, u32[]{:S(2)}) collective-permute-start(bf16[256,512]{1,0:T(8,128)(2,1)S(1)} %get-tuple-element.73), channel_id=1, source_target_pairs={{0,0},{1,8},{2,2},{3,10},{4,4},{5,12},{6,6},{7,14},{8,1},{9,9},{10... | collective-permute-start | bytes 786440 | tf_op jit(solution)/shard_map/ppermute | solution.py:48
  113.4 0.2 collective-permute-start.21
  113.6 0.7 fast_apply.1.refs_3_
  114.3 0.0 copy-start.5
  114.3 5.5 %update_middle.1.in_ref = bf16[3,512,512]{2,1,0:T(8,128)(2,1)S(1)} custom-call(bf16[3,512,512]{2,1,0:T(8,128)(2,1)S(1)} %update_start.1.in_ref), custom_call_target="tpu_custom_call" | custom-call | flops 1048576 | bytes 1024 | tf_op jit(solution)/shard_map/update_middle/pallas_call | solution.py:466
  119.8 0.5 collective-permute-done.21.refs_2_
  120.3 1.3 mix_zero.1
  121.6 0.3 collective-permute-start.22
  121.9 6.4 %update_end.1 = (f32[512,512]{1,0:T(8,128)}, f32[512,512]{1,0:T(8,128)}, f32[512,512]{1,0:T(8,128)}, f32[256,512]{1,0:T(8,128)S(1)}) custom-call(bf16[3,512,512]{2,1,0:T(8,128)(2,1)S(1)} %update_middle.1.in_ref, f32[512,512]{1,0:T(8,128)S(1)} %bitcast.41, f32[512,512]{1,0:T(8,128)S(1)} %bitcast.44, f32[512,512]{1,0:T(8,128)S(1)} %bitcast.47, ...), custom_call_target="tpu_custom_call" | custom-call | flops 1048576 | bytes 1024 | tf_op jit(solution)/shard_map/update_end/pallas_call | solution.py:471
  128.3 0.1 convert_add_fusion.1
  128.5 1.3 mix_one.1
  129.8 0.6 collective-permute-start.24
  130.4 3.6 %collective-permute-start.23 = (bf16[256,512]{1,0:T(8,128)(2,1)S(1)}, bf16[256,512]{1,0:T(8,128)(2,1)S(1)}, u32[]{:S(2)}, u32[]{:S(2)}) collective-permute-start(bf16[256,512]{1,0:T(8,128)(2,1)S(1)} %fusion.5), channel_id=1, source_target_pairs={{0,2},{1,3},{2,0},{3,1},{4,6},{5,7},{6,4},{7,5},{8,10},{9,11},{10,... | collective-permute-start | bytes 786440 | tf_op jit(solution)/shard_map/ppermute | solution.py:48
  134.0 0.2 convert_add_fusion
  134.2 1.6 %collective-permute-start.25 = (bf16[256,512]{1,0:T(8,128)(2,1)S(1)}, bf16[256,512]{1,0:T(8,128)(2,1)S(1)}, u32[]{:S(2)}, u32[]{:S(2)}) collective-permute-start(bf16[256,512]{1,0:T(8,128)(2,1)S(1)} %fusion.7), channel_id=1, source_target_pairs={{0,2},{1,3},{2,0},{3,1},{4,6},{5,7},{6,4},{7,5},{8,10},{9,11},{10,... | collective-permute-start | bytes 786440 | tf_op jit(solution)/shard_map/ppermute | solution.py:48
  135.8 4.8 %collective-permute-done.23 = bf16[256,512]{1,0:T(8,128)(2,1)S(1)} collective-permute-done((bf16[256,512]{1,0:T(8,128)(2,1)S(1)}, bf16[256,512]{1,0:T(8,128)(2,1)S(1)}, u32[]{:S(2)}, u32[]{:S(2)}) %collective-permute-start.23) | collective-permute-done | bytes 262176 | tf_op jit(solution)/shard_map/ppermute | solution.py:48
  140.6 0.1 fusion.4
  140.7 5.5 %collective-permute-done.25 = bf16[256,512]{1,0:T(8,128)(2,1)S(1)} collective-permute-done((bf16[256,512]{1,0:T(8,128)(2,1)S(1)}, bf16[256,512]{1,0:T(8,128)(2,1)S(1)}, u32[]{:S(2)}, u32[]{:S(2)}) %collective-permute-start.25) | collective-permute-done | bytes 262176 | tf_op jit(solution)/shard_map/ppermute | solution.py:48
  146.2 0.1 fusion.6
  146.3 0.8 pad_maximum_fusion.3
  (48 shorter events, 0.3 us)
Async XLA Ops:
  0.8 12.3 %copy-start = (f32[1,512,512]{2,1,0:T(8,128)S(1)}, f32[1,512,512]{2,1,0:T(8,128)}, u32[]{:S(2)}) copy-start(f32[1,512,512]{2,1,0:T(8,128)} %param.13) | copy-start | bytes 3145732
  0.8 12.3 %copy-start.1 = (f32[1,512,512]{2,1,0:T(8,128)S(1)}, f32[1,512,512]{2,1,0:T(8,128)}, u32[]{:S(2)}) copy-start(f32[1,512,512]{2,1,0:T(8,128)} %param.14) | copy-start | bytes 3145732
  0.8 12.3 %copy-start.3 = (f32[1,512,512]{2,1,0:T(8,128)S(1)}, f32[1,512,512]{2,1,0:T(8,128)}, u32[]{:S(2)}) copy-start(f32[1,512,512]{2,1,0:T(8,128)} %param.15) | copy-start | bytes 3145732
  0.8 12.3 %copy-start.6 = (bf16[2,256,2048]{2,1,0:T(8,128)(2,1)S(1)}, bf16[2,256,2048]{2,1,0:T(8,128)(2,1)}, u32[]{:S(2)}) copy-start(bf16[2,256,2048]{2,1,0:T(8,128)(2,1)} %tokens_ref.3) | copy-start | bytes 6291460
  0.8 12.3 %copy-start.9 = (bf16[2048,1]{0,1:T(2,128)(2,1)S(1)}, bf16[2048,1]{0,1:T(2,128)(2,1)}, u32[]{:S(2)}) copy-start(bf16[2048,1]{0,1:T(2,128)(2,1)} %param.10) | copy-start | bytes 12292
  7.1 32.5 %collective-permute-start = (bf16[768,512]{1,0:T(8,128)(2,1)S(1)}, bf16[768,512]{1,0:T(8,128)(2,1)S(1)}, u32[]{:S(2)}, u32[]{:S(2)}) collective-permute-start(bf16[768,512]{1,0:T(8,128)(2,1)S(1)} %get-tuple-element.48), channel_id=1, source_target_pairs={{0,0},{1,8},{2,2},{3,10},{4,4},{5,12},{6,6},{7,14},{8,1},{9,9},{10... | collective-permute-start | bytes 2359304 | tf_op jit(solution)/shard_map/ppermute | solution.py:48
  11.7 28.0 %collective-permute-start.1 = (bf16[768,512]{1,0:T(8,128)(2,1)S(1)}, bf16[768,512]{1,0:T(8,128)(2,1)S(1)}, u32[]{:S(2)}, u32[]{:S(2)}) collective-permute-start(bf16[768,512]{1,0:T(8,128)(2,1)S(1)} %get-tuple-element.49), channel_id=1, source_target_pairs={{0,4},{1,12},{2,6},{3,14},{4,0},{5,8},{6,2},{7,10},{8,5},{9,13},{1... | collective-permute-start | bytes 2359304 | tf_op jit(solution)/shard_map/ppermute | solution.py:48
  15.2 11.3 %collective-permute-start.2 = (bf16[384,512]{1,0:T(8,128)(2,1)S(1)}, bf16[384,512]{1,0:T(8,128)(2,1)S(1)}, u32[]{:S(2)}, u32[]{:S(2)}) collective-permute-start(bf16[384,512]{1,0:T(8,128)(2,1)S(1)} %get-tuple-element.51), channel_id=1, source_target_pairs={{0,32},{1,33},{2,34},{3,35},{4,36},{5,37},{6,38},{7,39},{8,40},{9,... | collective-permute-start | bytes 1179656 | tf_op jit(solution)/shard_map/ppermute | solution.py:48
  16.5 19.0 %collective-permute-start.3 = (bf16[384,512]{1,0:T(8,128)(2,1)S(1)}, bf16[384,512]{1,0:T(8,128)(2,1)S(1)}, u32[]{:S(2)}, u32[]{:S(2)}) collective-permute-start(bf16[384,512]{1,0:T(8,128)(2,1)S(1)} %get-tuple-element.52), channel_id=1, source_target_pairs={{0,64},{1,65},{2,66},{3,67},{4,68},{5,69},{6,70},{7,71},{8,72},{9,... | collective-permute-start | bytes 1179656 | tf_op jit(solution)/shard_map/ppermute | solution.py:48
  19.0 19.7 %collective-permute-start.4 = (bf16[384,512]{1,0:T(8,128)(2,1)S(1)}, bf16[384,512]{1,0:T(8,128)(2,1)S(1)}, u32[]{:S(2)}, u32[]{:S(2)}) collective-permute-start(bf16[384,512]{1,0:T(8,128)(2,1)S(1)} %get-tuple-element.53), channel_id=1, source_target_pairs={{0,96},{1,97},{2,98},{3,99},{4,100},{5,101},{6,102},{7,103},{8,104... | collective-permute-start | bytes 1179656 | tf_op jit(solution)/shard_map/ppermute | solution.py:48
  40.7 24.8 %collective-permute-start.12 = (bf16[512,512]{1,0:T(8,128)(2,1)S(1)}, bf16[512,512]{1,0:T(8,128)(2,1)}, u32[]{:S(2)}, u32[]{:S(2)}) collective-permute-start(bf16[512,512]{1,0:T(8,128)(2,1)S(1)} %pad_maximum_fusion.1.own), channel_id=1, source_target_pairs={{0,32},{1,33},{2,34},{3,35},{4,36},{5,37},{6,38},{7,39},{8,40},{9,... | collective-permute-start | bytes 1572872 | tf_op jit(solution)/shard_map/ppermute | solution.py:48
  42.8 4.5 %collective-permute-start.5 = (bf16[96,512]{1,0:T(8,128)(2,1)S(1)}, bf16[96,512]{1,0:T(8,128)(2,1)S(1)}, u32[]{:S(2)}, u32[]{:S(2)}) collective-permute-start(bf16[96,512]{1,0:T(8,128)(2,1)S(1)} %get-tuple-element.57), channel_id=1, source_target_pairs={{0,8},{1,9},{2,10},{3,11},{4,12},{5,13},{6,14},{7,15},{8,0},{9,1},... | collective-permute-start | bytes 294920 | tf_op jit(solution)/shard_map/ppermute | solution.py:48
  42.8 8.1 %collective-permute-start.6 = (bf16[96,512]{1,0:T(8,128)(2,1)S(1)}, bf16[96,512]{1,0:T(8,128)(2,1)S(1)}, u32[]{:S(2)}, u32[]{:S(2)}) collective-permute-start(bf16[96,512]{1,0:T(8,128)(2,1)S(1)} %get-tuple-element.58), channel_id=1, source_target_pairs={{0,16},{1,17},{2,18},{3,19},{4,20},{5,21},{6,22},{7,23},{8,24},{9,... | collective-permute-start | bytes 294920 | tf_op jit(solution)/shard_map/ppermute | solution.py:48
  45.7 7.5 %collective-permute-start.7 = (bf16[96,512]{1,0:T(8,128)(2,1)S(1)}, bf16[96,512]{1,0:T(8,128)(2,1)S(1)}, u32[]{:S(2)}, u32[]{:S(2)}) collective-permute-start(bf16[96,512]{1,0:T(8,128)(2,1)S(1)} %get-tuple-element.59), channel_id=1, source_target_pairs={{0,24},{1,25},{2,26},{3,27},{4,28},{5,29},{6,30},{7,31},{8,16},{9,... | collective-permute-start | bytes 294920 | tf_op jit(solution)/shard_map/ppermute | solution.py:48
  53.2 4.9 %collective-permute-start.8 = (bf16[96,512]{1,0:T(8,128)(2,1)S(1)}, bf16[96,512]{1,0:T(8,128)(2,1)S(1)}, u32[]{:S(2)}, u32[]{:S(2)}) collective-permute-start(bf16[96,512]{1,0:T(8,128)(2,1)S(1)} %reduce_y.1.refs_0_), channel_id=1, source_target_pairs={{0,4},{1,5},{2,6},{3,7},{4,0},{5,1},{6,2},{7,3},{8,12},{9,13},{10,... | collective-permute-start | bytes 294920 | tf_op jit(solution)/shard_map/ppermute | solution.py:48
  58.2 12.4 %collective-permute-start.11 = (bf16[96,512]{1,0:T(8,128)(2,1)S(1)}, bf16[96,512]{1,0:T(8,128)(2,1)S(1)}, u32[]{:S(2)}, u32[]{:S(2)}) collective-permute-start(bf16[96,512]{1,0:T(8,128)(2,1)S(1)} %reduce_z.1), channel_id=1, source_target_pairs={{0,24},{1,25},{2,26},{3,27},{4,28},{5,29},{6,30},{7,31},{8,16},{9,... | collective-permute-start | bytes 294920 | tf_op jit(solution)/shard_map/ppermute | solution.py:48
  58.4 12.1 %collective-permute-start.10 = (bf16[96,512]{1,0:T(8,128)(2,1)S(1)}, bf16[96,512]{1,0:T(8,128)(2,1)S(1)}, u32[]{:S(2)}, u32[]{:S(2)}) collective-permute-start(bf16[96,512]{1,0:T(8,128)(2,1)S(1)} %reduce_z.1), channel_id=1, source_target_pairs={{0,16},{1,17},{2,18},{3,19},{4,20},{5,21},{6,22},{7,23},{8,24},{9,... | collective-permute-start | bytes 294920 | tf_op jit(solution)/shard_map/ppermute | solution.py:48
  61.4 9.2 %collective-permute-start.9 = (bf16[96,512]{1,0:T(8,128)(2,1)S(1)}, bf16[96,512]{1,0:T(8,128)(2,1)S(1)}, u32[]{:S(2)}, u32[]{:S(2)}) collective-permute-start(bf16[96,512]{1,0:T(8,128)(2,1)S(1)} %reduce_z.1), channel_id=1, source_target_pairs={{0,8},{1,9},{2,10},{3,11},{4,12},{5,13},{6,14},{7,15},{8,0},{9,1},... | collective-permute-start | bytes 294920 | tf_op jit(solution)/shard_map/ppermute | solution.py:48
  63.3 16.5 %collective-permute-start.16 = (bf16[512,512]{1,0:T(8,128)(2,1)}, bf16[512,512]{1,0:T(8,128)(2,1)}, u32[]{:S(2)}, u32[]{:S(2)}) collective-permute-start(bf16[512,512]{1,0:T(8,128)(2,1)} %pad_maximum_fusion.2.own), channel_id=1, source_target_pairs={{0,32},{1,33},{2,34},{3,35},{4,36},{5,37},{6,38},{7,39},{8,40},{9,... | collective-permute-start | bytes 1572872 | tf_op jit(solution)/shard_map/ppermute | solution.py:48
  67.5 14.1 %collective-permute-start.13 = (bf16[512,512]{1,0:T(8,128)(2,1)}, bf16[512,512]{1,0:T(8,128)(2,1)}, u32[]{:S(2)}, u32[]{:S(2)}) collective-permute-start(bf16[512,512]{1,0:T(8,128)(2,1)} %get-tuple-element.93), channel_id=1, source_target_pairs={{0,16},{1,17},{2,18},{3,19},{4,20},{5,21},{6,22},{7,23},{8,24},{9,... | collective-permute-start | bytes 1572872 | tf_op jit(solution)/shard_map/ppermute | solution.py:48
  72.0 24.4 %all-to-all-start = ((bf16[4,384,512]{2,1,0:T(8,128)(2,1)}), bf16[4,384,512]{2,1,0:T(8,128)(2,1)}, u32[]{:S(2)}, u32[]{:S(2)}) async-start(bf16[4,384,512]{2,1,0:T(8,128)(2,1)} %broadcast_in_dim.15), calls=%async_computation | async-start | bytes 3145728 | tf_op jit(solution)/shard_map/all_to_all | solution.py:432
  77.7 11.3 %copy-start.11 = (bf16[256,512]{1,0:T(8,128)(2,1)S(1)}, bf16[256,512]{1,0:T(8,128)(2,1)}, u32[]{:S(2)}) copy-start(bf16[256,512]{1,0:T(8,128)(2,1)} %get-tuple-element.96) | copy-start | bytes 786436
  77.7 11.3 %copy-start.12 = (bf16[256,512]{1,0:T(8,128)(2,1)S(1)}, bf16[256,512]{1,0:T(8,128)(2,1)}, u32[]{:S(2)}) copy-start(bf16[256,512]{1,0:T(8,128)(2,1)} %get-tuple-element.100) | copy-start | bytes 786436
  77.7 11.9 %collective-permute-start.15 = (bf16[512,512]{1,0:T(8,128)(2,1)}, bf16[512,512]{1,0:T(8,128)(2,1)S(1)}, u32[]{:S(2)}, u32[]{:S(2)}) collective-permute-start(bf16[512,512]{1,0:T(8,128)(2,1)} %get-tuple-element.92), channel_id=1, source_target_pairs={{0,1},{1,0},{2,3},{3,2},{4,5},{5,4},{6,7},{7,6},{8,9},{9,8},{10,11... | collective-permute-start | bytes 1572872 | tf_op jit(solution)/shard_map/ppermute | solution.py:48
  81.6 7.9 %collective-permute-start.14 = (bf16[512,512]{1,0:T(8,128)(2,1)}, bf16[512,512]{1,0:T(8,128)(2,1)S(1)}, u32[]{:S(2)}, u32[]{:S(2)}) collective-permute-start(bf16[512,512]{1,0:T(8,128)(2,1)} %collective-permute-done.13.one), channel_id=1, source_target_pairs={{0,1},{1,0},{2,3},{3,2},{4,5},{5,4},{6,7},{7,6},{8,9},{9,8},{10,11... | collective-permute-start | bytes 1572872 | tf_op jit(solution)/shard_map/ppermute | solution.py:48
  86.0 15.4 %collective-permute-start.17 = (bf16[512,512]{1,0:T(8,128)(2,1)}, bf16[512,512]{1,0:T(8,128)(2,1)}, u32[]{:S(2)}, u32[]{:S(2)}) collective-permute-start(bf16[512,512]{1,0:T(8,128)(2,1)} %get-tuple-element.91), channel_id=1, source_target_pairs={{0,16},{1,17},{2,18},{3,19},{4,20},{5,21},{6,22},{7,23},{8,24},{9,... | collective-permute-start | bytes 1572872 | tf_op jit(solution)/shard_map/ppermute | solution.py:48
  89.0 15.8 %collective-permute-start.19 = (bf16[512,512]{1,0:T(8,128)(2,1)}, bf16[512,512]{1,0:T(8,128)(2,1)}, u32[]{:S(2)}, u32[]{:S(2)}) collective-permute-start(bf16[512,512]{1,0:T(8,128)(2,1)} %get-tuple-element.90), channel_id=1, source_target_pairs={{0,1},{1,0},{2,3},{3,2},{4,5},{5,4},{6,7},{7,6},{8,9},{9,8},{10,11... | collective-permute-start | bytes 1572872 | tf_op jit(solution)/shard_map/ppermute | solution.py:48
  94.9 1.5 %copy-start.7 = (bf16[5,512,512]{2,1,0:T(8,128)(2,1)}, bf16[5,512,512]{2,1,0:T(8,128)(2,1)S(1)}, u32[]{:S(2)}) copy-start(bf16[5,512,512]{2,1,0:T(8,128)(2,1)S(1)} %get-tuple-element.67.weights_ref) | copy-start | bytes 7864324
  96.4 10.2 %copy-start.8 = (bf16[5,512,512]{2,1,0:T(8,128)(2,1)S(1)}, bf16[5,512,512]{2,1,0:T(8,128)(2,1)}, u32[]{:S(2)}) copy-start(bf16[5,512,512]{2,1,0:T(8,128)(2,1)} %copy-done.7) | copy-start | bytes 7864324
  101.4 5.2 %collective-permute-start.18 = (bf16[512,512]{1,0:T(8,128)(2,1)}, bf16[512,512]{1,0:T(8,128)(2,1)S(1)}, u32[]{:S(2)}, u32[]{:S(2)}) collective-permute-start(bf16[512,512]{1,0:T(8,128)(2,1)} %collective-permute-done.17.one), channel_id=1, source_target_pairs={{0,1},{1,0},{2,3},{3,2},{4,5},{5,4},{6,7},{7,6},{8,9},{9,8},{10,11... | collective-permute-start | bytes 1572872 | tf_op jit(solution)/shard_map/ppermute | solution.py:48
  106.6 6.9 %copy-start.2 = (f32[1,512,512]{2,1,0:T(8,128)S(1)}, f32[1,512,512]{2,1,0:T(8,128)}, u32[]{:S(2)}) copy-start(f32[1,512,512]{2,1,0:T(8,128)} %param.14) | copy-start | bytes 3145732
  106.6 6.9 %copy-start.4 = (f32[1,512,512]{2,1,0:T(8,128)S(1)}, f32[1,512,512]{2,1,0:T(8,128)}, u32[]{:S(2)}) copy-start(f32[1,512,512]{2,1,0:T(8,128)} %param.15) | copy-start | bytes 3145732
  106.6 6.9 %copy-start.10 = (f32[1,512]{1,0:T(1,128)S(1)}, f32[1,512]{1,0:T(1,128)}, u32[]{:S(2)}) copy-start(f32[1,512]{1,0:T(1,128)} %gain_ref.3) | copy-start | bytes 6148
  109.8 10.0 %collective-permute-start.20 = (bf16[256,512]{1,0:T(8,128)(2,1)S(1)}, bf16[256,512]{1,0:T(8,128)(2,1)S(1)}, u32[]{:S(2)}, u32[]{:S(2)}) collective-permute-start(bf16[256,512]{1,0:T(8,128)(2,1)S(1)} %get-tuple-element.73), channel_id=1, source_target_pairs={{0,0},{1,8},{2,2},{3,10},{4,4},{5,12},{6,6},{7,14},{8,1},{9,9},{10... | collective-permute-start | bytes 786440 | tf_op jit(solution)/shard_map/ppermute | solution.py:48
  113.4 6.9 %collective-permute-start.21 = (bf16[256,512]{1,0:T(8,128)(2,1)S(1)}, bf16[256,512]{1,0:T(8,128)(2,1)S(1)}, u32[]{:S(2)}, u32[]{:S(2)}) collective-permute-start(bf16[256,512]{1,0:T(8,128)(2,1)S(1)} %get-tuple-element.74), channel_id=1, source_target_pairs={{0,4},{1,12},{2,6},{3,14},{4,0},{5,8},{6,2},{7,10},{8,5},{9,13},{1... | collective-permute-start | bytes 786440 | tf_op jit(solution)/shard_map/ppermute | solution.py:48
  114.3 6.0 %copy-start.5 = (bf16[1,512,2048]{2,1,0:T(8,128)(2,1)S(1)}, bf16[1,512,2048]{2,1,0:T(8,128)(2,1)}, u32[]{:S(2)}) copy-start(bf16[1,512,2048]{2,1,0:T(8,128)(2,1)} %param.11) | copy-start | bytes 6291460
  121.6 6.7 %collective-permute-start.22 = (bf16[2,256,512]{2,1,0:T(8,128)(2,1)S(1)}, bf16[2,256,512]{2,1,0:T(8,128)(2,1)S(1)}, u32[]{:S(2)}, u32[]{:S(2)}) collective-permute-start(bf16[2,256,512]{2,1,0:T(8,128)(2,1)S(1)} %get-tuple-element.80), channel_id=1, source_target_pairs={{0,1},{1,0},{2,3},{3,2},{4,5},{5,4},{6,7},{7,6},{8,9},{9,8},{10,11... | collective-permute-start | bytes 1572872 | tf_op jit(solution)/shard_map/ppermute | solution.py:48
  129.8 4.2 %collective-permute-start.24 = (bf16[2,256,512]{2,1,0:T(8,128)(2,1)S(1)}, bf16[2,256,512]{2,1,0:T(8,128)(2,1)S(1)}, u32[]{:S(2)}, u32[]{:S(2)}) collective-permute-start(bf16[2,256,512]{2,1,0:T(8,128)(2,1)S(1)} %get-tuple-element.86), channel_id=1, source_target_pairs={{0,1},{1,0},{2,3},{3,2},{4,5},{5,4},{6,7},{7,6},{8,9},{9,8},{10,11... | collective-permute-start | bytes 1572872 | tf_op jit(solution)/shard_map/ppermute | solution.py:48
  130.4 10.2 %collective-permute-start.23 = (bf16[256,512]{1,0:T(8,128)(2,1)S(1)}, bf16[256,512]{1,0:T(8,128)(2,1)S(1)}, u32[]{:S(2)}, u32[]{:S(2)}) collective-permute-start(bf16[256,512]{1,0:T(8,128)(2,1)S(1)} %fusion.5), channel_id=1, source_target_pairs={{0,2},{1,3},{2,0},{3,1},{4,6},{5,7},{6,4},{7,5},{8,10},{9,11},{10,... | collective-permute-start | bytes 786440 | tf_op jit(solution)/shard_map/ppermute | solution.py:48
  134.2 12.0 %collective-permute-start.25 = (bf16[256,512]{1,0:T(8,128)(2,1)S(1)}, bf16[256,512]{1,0:T(8,128)(2,1)S(1)}, u32[]{:S(2)}, u32[]{:S(2)}) collective-permute-start(bf16[256,512]{1,0:T(8,128)(2,1)S(1)} %fusion.7), channel_id=1, source_target_pairs={{0,2},{1,3},{2,0},{3,1},{4,6},{5,7},{6,4},{7,5},{8,10},{9,11},{10,... | collective-permute-start | bytes 786440 | tf_op jit(solution)/shard_map/ppermute | solution.py:48

commit v3 on v2

--- a/solution.py
+++ b/solution.py
@@ -412,15 +412,17 @@
     )(place, *grads)
     (own_keys,) = ordered([own_keys], grads[0])
     two_keys = moved(own_keys, quads_on(2))
-    grads = exchanged(grads, "y")
+    grads = ordered(exchanged(grads, "y"), own_values)
     (piece,) = call(reduce_y, [vmem()] * 4, [((96, 512), BF)])(*grads)
+    (piece,) = call(reduce_z, [vmem()] * 2, [((96, 512), BF)])(*exchanged([piece] * 2, "z"))
+
+    def onward(own, two):
+        one = jnp.where(y >= 2, two, own)
+        (two,) = ordered([two], one)
+        return one, jnp.where(core == 0, own, two)
+
     (own_values,) = ordered([own_values], piece)
     two_values = moved(own_values, quads_on(2))
-    (piece,) = call(reduce_z, [vmem()] * 2, [((96, 512), BF)])(*exchanged([piece] * 2, "z"))
-
-    def onward(own, two):
-        return jnp.where(y >= 2, two, own), jnp.where(core == 0, own, two)
-
     (two_keys,) = ordered([two_keys], piece)
     one_keys, swap_two_keys = onward(own_keys, two_keys)
     piece = exchanged([piece] * 4, "y")

time: 148 us -> 146 us (0.986)
    select_n x2 -> x4, other arithmetic: 4.32 us -> 4.87 us  [the longest x2 3.11 us: onward(): return (one, jnp.where(core == 0, own, two))]
  transfers between devices with their start and end apart: 27 -> 27, of which waited for: 13 -> 11; matrix products, arithmetic and copies ran while one was open for 5% -> 5% of each run, Pallas kernels for 18% -> 18%
where the time goes in v3:
time: 146 us; the launch traced here: 145 us
  starting transfers between devices  51 us (35%)
  waiting for transfers between devices  44.3 us (30%)
  Pallas kernels  37.9 us (26%)
  other arithmetic  7.05 us (5%)
  local copies, waits for them, and re-layouts  4.04 us (3%)
    ppermute x26, starting transfers between devices, moved(): return lax.ppermute(value, ('ctx', 'head'), pairs)  45.3 us
    ppermute x26, waiting for transfers between devices, moved(): return lax.ppermute(value, ('ctx', 'head'), pairs)  44.3 us
    pallas_call x1, Pallas kernels, shards(): call(update_end, [vmem()] * 6, [((512, 512), F32)] * 3 + [((HALF, 512), F...  6.42 us
    pallas_call x1, Pallas kernels, run_project(): call(project, [smem()] + [pl.BlockSpec(memory_space=pltpu.HBM)] * 2, [((2...  6.24 us
    all_to_all x1, starting transfers between devices, shards(): lax.all_to_all(sent, 'ctx', 0, 0, axis_index_groups=lines, tiled=True)  5.7 us
    pallas_call x1, Pallas kernels, shards(): held, = call(update_middle, [vmem()], [((3, 512, 512), BF)], limit=24)(held)  5.49 us
    pallas_call x1, Pallas kernels, shards(): call(scores, [smem()] + [vmem()] * 6, [((5, SUPER, SUPER), BF), ((SUPER,...  5.33 us
    pallas_call x1, Pallas kernels, shards(): call(update_start, [smem(), vmem()], [((3, 512, 512), BF)], scratch=(pltp...  4.91 us
  transfers between devices with their start and end apart: 27, of which 11 were waited for; matrix products, arithmetic and copies ran while one was open for 5% of the time, Pallas kernels for 18%

profile of v3, /device:TPU:1, one launch (start us, length us, event | category | flops | bytes accessed | tf_op | source)
XLA Modules:
  0.0 145.3 jit_solution(15980953566950798180)
XLA Ops:
  0.7 0.1 stack.39.place.refs_0_
  0.8 0.0 copy-start.6
  0.8 6.2 %project.1 = (bf16[2,256,1536]{2,1,0:T(8,128)(2,1)S(1)}, bf16[768,512]{1,0:T(8,128)(2,1)S(1)}, bf16[768,512]{1,0:T(8,128)(2,1)S(1)}) custom-call(s32[6]{0:T(128)S(1)} %stack.39.place.refs_0_, bf16[2,256,2048]{2,1,0:T(8,128)(2,1)} %tokens_ref.3, bf16[2048,1536]{1,0:T(8,128)(2,1)} %bitcast.51), custom_call_target="tpu_custom_call" | custom-call | flops 1048576 | bytes 1024 | tf_op jit(solution)/shard_map/project/pallas_call | solution.py:146
  7.1 4.6 %collective-permute-start = (bf16[768,512]{1,0:T(8,128)(2,1)S(1)}, bf16[768,512]{1,0:T(8,128)(2,1)S(1)}, u32[]{:S(2)}, u32[]{:S(2)}) collective-permute-start(bf16[768,512]{1,0:T(8,128)(2,1)S(1)} %get-tuple-element.54), channel_id=1, source_target_pairs={{0,0},{1,8},{2,2},{3,10},{4,4},{5,12},{6,6},{7,14},{8,1},{9,9},{10... | collective-permute-start | bytes 2359304 | tf_op jit(solution)/shard_map/ppermute | solution.py:48
  11.7 1.4 collective-permute-start.1
  13.1 2.1 %fast_grads.1 = (bf16[384,512]{1,0:T(8,128)(2,1)S(1)}, bf16[384,512]{1,0:T(8,128)(2,1)S(1)}, bf16[384,512]{1,0:T(8,128)(2,1)S(1)}, bf16[384,512]{1,0:T(8,128)(2,1)S(1)}) custom-call(s32[6]{0:T(128)S(1)} %stack.39.place.refs_0_, bf16[2,256,2048]{2,1,0:T(8,128)(2,1)S(1)} %copy-done.6, bf16[1,2048]{1,0:T(2,128)(2,1)S(1)} %bitcast.50, ...), custom_call_target="tpu_custom_call" | custom-call | flops 1048576 | bytes 1024 | tf_op jit(solution)/shard_map/fast_grads/pallas_call | solution.py:394
  15.2 1.3 collective-permute-start.2
  16.5 2.5 %collective-permute-start.3 = (bf16[384,512]{1,0:T(8,128)(2,1)S(1)}, bf16[384,512]{1,0:T(8,128)(2,1)S(1)}, u32[]{:S(2)}, u32[]{:S(2)}) collective-permute-start(bf16[384,512]{1,0:T(8,128)(2,1)S(1)} %get-tuple-element.58), channel_id=1, source_target_pairs={{0,64},{1,65},{2,66},{3,67},{4,68},{5,69},{6,70},{7,71},{8,72},{9,... | collective-permute-start | bytes 1179656 | tf_op jit(solution)/shard_map/ppermute | solution.py:48
  19.0 0.2 collective-permute-start.4
  19.2 7.3 %collective-permute-done.2.refs_1_ = bf16[384,512]{1,0:T(8,128)(2,1)S(1)} collective-permute-done((bf16[384,512]{1,0:T(8,128)(2,1)S(1)}, bf16[384,512]{1,0:T(8,128)(2,1)S(1)}, u32[]{:S(2)}, u32[]{:S(2)}) %collective-permute-start.2) | collective-permute-done | bytes 393248 | tf_op jit(solution)/shard_map/ppermute | solution.py:48
  26.5 9.0 %collective-permute-done.3.refs_2_ = bf16[384,512]{1,0:T(8,128)(2,1)S(1)} collective-permute-done((bf16[384,512]{1,0:T(8,128)(2,1)S(1)}, bf16[384,512]{1,0:T(8,128)(2,1)S(1)}, u32[]{:S(2)}, u32[]{:S(2)}) %collective-permute-start.3) | collective-permute-done | bytes 393248 | tf_op jit(solution)/shard_map/ppermute | solution.py:48
  35.5 3.1 %collective-permute-done.4.refs_3_ = bf16[384,512]{1,0:T(8,128)(2,1)S(1)} collective-permute-done((bf16[384,512]{1,0:T(8,128)(2,1)S(1)}, bf16[384,512]{1,0:T(8,128)(2,1)S(1)}, u32[]{:S(2)}, u32[]{:S(2)}) %collective-permute-start.4) | collective-permute-done | bytes 393248 | tf_op jit(solution)/shard_map/ppermute | solution.py:48
  38.7 0.9 reduce_x.1
  39.6 1.0 fusion.8
  40.6 2.1 %collective-permute-start.12 = (bf16[512,512]{1,0:T(8,128)(2,1)S(1)}, bf16[512,512]{1,0:T(8,128)(2,1)}, u32[]{:S(2)}, u32[]{:S(2)}) collective-permute-start(bf16[512,512]{1,0:T(8,128)(2,1)S(1)} %pad_maximum_fusion.2.own), channel_id=1, source_target_pairs={{0,32},{1,33},{2,34},{3,35},{4,36},{5,37},{6,38},{7,39},{8,40},{9,... | collective-permute-start | bytes 1572872 | tf_op jit(solution)/shard_map/ppermute | solution.py:48
  42.7 2.9 %collective-permute-start.6 = (bf16[96,512]{1,0:T(8,128)(2,1)S(1)}, bf16[96,512]{1,0:T(8,128)(2,1)S(1)}, u32[]{:S(2)}, u32[]{:S(2)}) collective-permute-start(bf16[96,512]{1,0:T(8,128)(2,1)S(1)} %get-tuple-element.64), channel_id=1, source_target_pairs={{0,16},{1,17},{2,18},{3,19},{4,20},{5,21},{6,22},{7,23},{8,24},{9,... | collective-permute-start | bytes 294920 | tf_op jit(solution)/shard_map/ppermute | solution.py:48
  45.7 0.9 collective-permute-start.7
  46.6 0.8 pad_maximum_fusion.1.own
  47.4 3.4 %collective-permute-done.6.refs_2_ = bf16[96,512]{1,0:T(8,128)(2,1)S(1)} collective-permute-done((bf16[96,512]{1,0:T(8,128)(2,1)S(1)}, bf16[96,512]{1,0:T(8,128)(2,1)S(1)}, u32[]{:S(2)}, u32[]{:S(2)}) %collective-permute-start.6) | collective-permute-done | bytes 98336 | tf_op jit(solution)/shard_map/ppermute | solution.py:48
  50.9 2.3 %collective-permute-done.7.refs_3_ = bf16[96,512]{1,0:T(8,128)(2,1)S(1)} collective-permute-done((bf16[96,512]{1,0:T(8,128)(2,1)S(1)}, bf16[96,512]{1,0:T(8,128)(2,1)S(1)}, u32[]{:S(2)}, u32[]{:S(2)}) %collective-permute-start.7) | collective-permute-done | bytes 98336 | tf_op jit(solution)/shard_map/ppermute | solution.py:48
  53.1 0.1 reduce_y.1.refs_0_
  53.2 0.1 collective-permute-start.8
  53.3 4.8 %collective-permute-done.8.refs_1_ = bf16[96,512]{1,0:T(8,128)(2,1)S(1)} collective-permute-done((bf16[96,512]{1,0:T(8,128)(2,1)S(1)}, bf16[96,512]{1,0:T(8,128)(2,1)S(1)}, u32[]{:S(2)}, u32[]{:S(2)}) %collective-permute-start.8) | collective-permute-done | bytes 98336 | tf_op jit(solution)/shard_map/ppermute | solution.py:48
  58.1 0.3 collective-permute-start.11
  58.4 2.9 %collective-permute-start.10 = (bf16[96,512]{1,0:T(8,128)(2,1)S(1)}, bf16[96,512]{1,0:T(8,128)(2,1)S(1)}, u32[]{:S(2)}, u32[]{:S(2)}) collective-permute-start(bf16[96,512]{1,0:T(8,128)(2,1)S(1)} %reduce_z.1), channel_id=1, source_target_pairs={{0,16},{1,17},{2,18},{3,19},{4,20},{5,21},{6,22},{7,23},{8,24},{9,... | collective-permute-start | bytes 294920 | tf_op jit(solution)/shard_map/ppermute | solution.py:48
  61.3 0.1 collective-permute-start.9
  61.4 2.1 %collective-permute-start.16 = (bf16[512,512]{1,0:T(8,128)(2,1)}, bf16[512,512]{1,0:T(8,128)(2,1)}, u32[]{:S(2)}, u32[]{:S(2)}) collective-permute-start(bf16[512,512]{1,0:T(8,128)(2,1)} %pad_maximum_fusion.1.own), channel_id=1, source_target_pairs={{0,32},{1,33},{2,34},{3,35},{4,36},{5,37},{6,38},{7,39},{8,40},{9,... | collective-permute-start | bytes 1572872 | tf_op jit(solution)/shard_map/ppermute | solution.py:48
  63.5 0.9 broadcast_select_fusion.3
  64.4 4.1 %collective-permute-start.13 = (bf16[512,512]{1,0:T(8,128)(2,1)}, bf16[512,512]{1,0:T(8,128)(2,1)}, u32[]{:S(2)}, u32[]{:S(2)}) collective-permute-start(bf16[512,512]{1,0:T(8,128)(2,1)} %broadcast_select_fusion.3), channel_id=1, source_target_pairs={{0,16},{1,17},{2,18},{3,19},{4,20},{5,21},{6,22},{7,23},{8,24},{9,... | collective-permute-start | bytes 1572872 | tf_op jit(solution)/shard_map/ppermute | solution.py:48
  68.6 1.3 broadcast_in_dim.15
  69.9 5.7 %all-to-all-start = ((bf16[4,384,512]{2,1,0:T(8,128)(2,1)}), bf16[4,384,512]{2,1,0:T(8,128)(2,1)}, u32[]{:S(2)}, u32[]{:S(2)}) async-start(bf16[4,384,512]{2,1,0:T(8,128)(2,1)} %broadcast_in_dim.15), calls=%async_computation | async-start | bytes 3145728 | tf_op jit(solution)/shard_map/all_to_all | solution.py:434
  75.6 1.2 broadcast_select_fusion.1
  76.8 1.1 collective-permute-start.15
  78.0 1.8 %collective-permute-done.13.one = bf16[512,512]{1,0:T(8,128)(2,1)} collective-permute-done((bf16[512,512]{1,0:T(8,128)(2,1)}, bf16[512,512]{1,0:T(8,128)(2,1)}, u32[]{:S(2)}, u32[]{:S(2)}) %collective-permute-start.13) | collective-permute-done | bytes 524320 | tf_op jit(solution)/shard_map/ppermute | solution.py:48
  79.7 2.0 %collective-permute-start.14 = (bf16[512,512]{1,0:T(8,128)(2,1)}, bf16[512,512]{1,0:T(8,128)(2,1)S(1)}, u32[]{:S(2)}, u32[]{:S(2)}) collective-permute-start(bf16[512,512]{1,0:T(8,128)(2,1)} %collective-permute-done.13.one), channel_id=1, source_target_pairs={{0,1},{1,0},{2,3},{3,2},{4,5},{5,4},{6,7},{7,6},{8,9},{9,8},{10,11... | collective-permute-start | bytes 1572872 | tf_op jit(solution)/shard_map/ppermute | solution.py:48
  81.7 0.9 broadcast_select_fusion.2
  82.6 4.0 %collective-permute-start.17 = (bf16[512,512]{1,0:T(8,128)(2,1)}, bf16[512,512]{1,0:T(8,128)(2,1)}, u32[]{:S(2)}, u32[]{:S(2)}) collective-permute-start(bf16[512,512]{1,0:T(8,128)(2,1)} %broadcast_select_fusion.2), channel_id=1, source_target_pairs={{0,16},{1,17},{2,18},{3,19},{4,20},{5,21},{6,22},{7,23},{8,24},{9,... | collective-permute-start | bytes 1572872 | tf_op jit(solution)/shard_map/ppermute | solution.py:48
  86.6 1.9 %broadcast_select_fusion = bf16[512,512]{1,0:T(8,128)(2,1)} fusion(bf16[512,512]{1,0:T(8,128)(2,1)S(1)} %copy-done.7, bf16[512,512]{1,0:T(8,128)(2,1)} %collective-permute-done.16.two, pred[]{:T(512)S(6)} %eq.8), kind=kLoop, calls=%fused_computation.14 | loop fusion | flops 262144 | bytes 1572865 | tf_op jit(solution)/shard_map/jit(_where)/select_n | solution.py:422
  88.6 5.3 %scores.1 = (bf16[5,512,512]{2,1,0:T(8,128)(2,1)S(1)}, f32[512,128]{1,0:T(8,128)S(1)}) custom-call(s32[6]{0:T(128)S(1)} %stack.39.place.refs_0_, bf16[512,512]{1,0:T(8,128)(2,1)S(1)} %pad_maximum_fusion.queries_ref, bf16[512,512]{1,0:T(8,128)(2,1)S(1)} %pad_maximum_fusion.2.own, bf16[512,512]{1,0:T(8,128)(2,1)S(1)} %collective-permute-done.14.swap_one, ...), custom_call_target="tpu_custom_call" | custom-call | flops 1048576 | bytes 1024 | tf_op jit(solution)/shard_map/scores/pallas_call | solution.py:442
  93.9 1.5 %copy-done.9 = bf16[5,512,512]{2,1,0:T(8,128)(2,1)} copy-done((bf16[5,512,512]{2,1,0:T(8,128)(2,1)}, bf16[5,512,512]{2,1,0:T(8,128)(2,1)S(1)}, u32[]{:S(2)}) %copy-start.9) | copy-done | bytes 2621464
  95.4 4.9 %update_start.1.in_ref = bf16[3,512,512]{2,1,0:T(8,128)(2,1)S(1)} custom-call(s32[6]{0:T(128)S(1)} %stack.39.place.refs_0_, bf16[4,384,512]{2,1,0:T(8,128)(2,1)} %all-to-all-done.parts_ref), custom_call_target="tpu_custom_call" | custom-call | flops 1048576 | bytes 1024 | tf_op jit(solution)/shard_map/update_start/pallas_call | solution.py:449
  100.3 2.6 %collective-permute-start.18 = (bf16[512,512]{1,0:T(8,128)(2,1)}, bf16[512,512]{1,0:T(8,128)(2,1)S(1)}, u32[]{:S(2)}, u32[]{:S(2)}) collective-permute-start(bf16[512,512]{1,0:T(8,128)(2,1)} %collective-permute-done.17.one), channel_id=1, source_target_pairs={{0,1},{1,0},{2,3},{3,2},{4,5},{5,4},{6,7},{7,6},{8,9},{9,8},{10,11... | collective-permute-start | bytes 1572872 | tf_op jit(solution)/shard_map/ppermute | solution.py:48
  103.0 1.7 %collective-permute-done.18.swap_one = bf16[512,512]{1,0:T(8,128)(2,1)S(1)} collective-permute-done((bf16[512,512]{1,0:T(8,128)(2,1)}, bf16[512,512]{1,0:T(8,128)(2,1)S(1)}, u32[]{:S(2)}, u32[]{:S(2)}) %collective-permute-start.18) | collective-permute-done | bytes 524320 | tf_op jit(solution)/shard_map/ppermute | solution.py:48
  104.7 0.0 copy-start.12
  104.7 3.0 %gathered.1 = (bf16[256,512]{1,0:T(8,128)(2,1)S(1)}, bf16[256,512]{1,0:T(8,128)(2,1)S(1)}) custom-call(bf16[5,512,512]{2,1,0:T(8,128)(2,1)S(1)} %copy-done.10, f32[512,128]{1,0:T(8,128)S(1)} %get-tuple-element.79.sum_ref, bf16[512,512]{1,0:T(8,128)(2,1)S(1)} %copy-done.8, bf16[512,512]{1,0:T(8,128)(2,1)S(1)} %collective-permute-done.18.swap_one, ...), custom_call_target="tpu_custom_call" | custom-call | flops 1048576 | bytes 1024 | tf_op jit(solution)/shard_map/gathered/pallas_call | solution.py:458
  107.8 3.6 %collective-permute-start.20 = (bf16[256,512]{1,0:T(8,128)(2,1)S(1)}, bf16[256,512]{1,0:T(8,128)(2,1)S(1)}, u32[]{:S(2)}, u32[]{:S(2)}) collective-permute-start(bf16[256,512]{1,0:T(8,128)(2,1)S(1)} %get-tuple-element.85), channel_id=1, source_target_pairs={{0,0},{1,8},{2,2},{3,10},{4,4},{5,12},{6,6},{7,14},{8,1},{9,9},{10... | collective-permute-start | bytes 786440 | tf_op jit(solution)/shard_map/ppermute | solution.py:48
  111.3 0.4 collective-permute-start.21
  111.7 0.7 fast_apply.1.refs_3_
  112.5 5.5 %update_middle.1.in_ref = bf16[3,512,512]{2,1,0:T(8,128)(2,1)S(1)} custom-call(bf16[3,512,512]{2,1,0:T(8,128)(2,1)S(1)} %update_start.1.in_ref), custom_call_target="tpu_custom_call" | custom-call | flops 1048576 | bytes 1024 | tf_op jit(solution)/shard_map/update_middle/pallas_call | solution.py:468
  118.0 0.5 collective-permute-done.21.refs_2_
  118.5 1.3 mix_zero.1
  119.8 0.3 collective-permute-start.22
  120.1 6.4 %update_end.1 = (f32[512,512]{1,0:T(8,128)}, f32[512,512]{1,0:T(8,128)}, f32[512,512]{1,0:T(8,128)}, f32[256,512]{1,0:T(8,128)S(1)}) custom-call(bf16[3,512,512]{2,1,0:T(8,128)(2,1)S(1)} %update_middle.1.in_ref, f32[512,512]{1,0:T(8,128)S(1)} %bitcast.41, f32[512,512]{1,0:T(8,128)S(1)} %bitcast.44, f32[512,512]{1,0:T(8,128)S(1)} %bitcast.47, ...), custom_call_target="tpu_custom_call" | custom-call | flops 1048576 | bytes 1024 | tf_op jit(solution)/shard_map/update_end/pallas_call | solution.py:473
  126.5 0.1 convert_add_fusion.1
  126.7 1.3 mix_one.1
  128.0 0.6 collective-permute-start.24
  128.6 3.6 %collective-permute-start.23 = (bf16[256,512]{1,0:T(8,128)(2,1)S(1)}, bf16[256,512]{1,0:T(8,128)(2,1)S(1)}, u32[]{:S(2)}, u32[]{:S(2)}) collective-permute-start(bf16[256,512]{1,0:T(8,128)(2,1)S(1)} %fusion.5), channel_id=1, source_target_pairs={{0,2},{1,3},{2,0},{3,1},{4,6},{5,7},{6,4},{7,5},{8,10},{9,11},{10,... | collective-permute-start | bytes 786440 | tf_op jit(solution)/shard_map/ppermute | solution.py:48
  132.2 0.2 convert_add_fusion
  132.4 1.6 %collective-permute-start.25 = (bf16[256,512]{1,0:T(8,128)(2,1)S(1)}, bf16[256,512]{1,0:T(8,128)(2,1)S(1)}, u32[]{:S(2)}, u32[]{:S(2)}) collective-permute-start(bf16[256,512]{1,0:T(8,128)(2,1)S(1)} %fusion.7), channel_id=1, source_target_pairs={{0,2},{1,3},{2,0},{3,1},{4,6},{5,7},{6,4},{7,5},{8,10},{9,11},{10,... | collective-permute-start | bytes 786440 | tf_op jit(solution)/shard_map/ppermute | solution.py:48
  134.0 4.8 %collective-permute-done.23 = bf16[256,512]{1,0:T(8,128)(2,1)S(1)} collective-permute-done((bf16[256,512]{1,0:T(8,128)(2,1)S(1)}, bf16[256,512]{1,0:T(8,128)(2,1)S(1)}, u32[]{:S(2)}, u32[]{:S(2)}) %collective-permute-start.23) | collective-permute-done | bytes 262176 | tf_op jit(solution)/shard_map/ppermute | solution.py:48
  138.8 0.1 fusion.4
  138.8 5.5 %collective-permute-done.25 = bf16[256,512]{1,0:T(8,128)(2,1)S(1)} collective-permute-done((bf16[256,512]{1,0:T(8,128)(2,1)S(1)}, bf16[256,512]{1,0:T(8,128)(2,1)S(1)}, u32[]{:S(2)}, u32[]{:S(2)}) %collective-permute-start.25) | collective-permute-done | bytes 262176 | tf_op jit(solution)/shard_map/ppermute | solution.py:48
  144.4 0.1 fusion.6
  144.4 0.8 pad_maximum_fusion.3
  (54 shorter events, 0.3 us)
Async XLA Ops:
  0.8 12.3 %copy-start = (f32[1,512,512]{2,1,0:T(8,128)S(1)}, f32[1,512,512]{2,1,0:T(8,128)}, u32[]{:S(2)}) copy-start(f32[1,512,512]{2,1,0:T(8,128)} %param.13) | copy-start | bytes 3145732
  0.8 12.3 %copy-start.1 = (f32[1,512,512]{2,1,0:T(8,128)S(1)}, f32[1,512,512]{2,1,0:T(8,128)}, u32[]{:S(2)}) copy-start(f32[1,512,512]{2,1,0:T(8,128)} %param.14) | copy-start | bytes 3145732
  0.8 12.3 %copy-start.3 = (f32[1,512,512]{2,1,0:T(8,128)S(1)}, f32[1,512,512]{2,1,0:T(8,128)}, u32[]{:S(2)}) copy-start(f32[1,512,512]{2,1,0:T(8,128)} %param.15) | copy-start | bytes 3145732
  0.8 12.3 %copy-start.6 = (bf16[2,256,2048]{2,1,0:T(8,128)(2,1)S(1)}, bf16[2,256,2048]{2,1,0:T(8,128)(2,1)}, u32[]{:S(2)}) copy-start(bf16[2,256,2048]{2,1,0:T(8,128)(2,1)} %tokens_ref.3) | copy-start | bytes 6291460
  0.8 12.3 %copy-start.11 = (bf16[2048,1]{0,1:T(2,128)(2,1)S(1)}, bf16[2048,1]{0,1:T(2,128)(2,1)}, u32[]{:S(2)}) copy-start(bf16[2048,1]{0,1:T(2,128)(2,1)} %param.10) | copy-start | bytes 12292
  7.1 32.5 %collective-permute-start = (bf16[768,512]{1,0:T(8,128)(2,1)S(1)}, bf16[768,512]{1,0:T(8,128)(2,1)S(1)}, u32[]{:S(2)}, u32[]{:S(2)}) collective-permute-start(bf16[768,512]{1,0:T(8,128)(2,1)S(1)} %get-tuple-element.54), channel_id=1, source_target_pairs={{0,0},{1,8},{2,2},{3,10},{4,4},{5,12},{6,6},{7,14},{8,1},{9,9},{10... | collective-permute-start | bytes 2359304 | tf_op jit(solution)/shard_map/ppermute | solution.py:48
  11.7 28.0 %collective-permute-start.1 = (bf16[768,512]{1,0:T(8,128)(2,1)S(1)}, bf16[768,512]{1,0:T(8,128)(2,1)S(1)}, u32[]{:S(2)}, u32[]{:S(2)}) collective-permute-start(bf16[768,512]{1,0:T(8,128)(2,1)S(1)} %get-tuple-element.55), channel_id=1, source_target_pairs={{0,4},{1,12},{2,6},{3,14},{4,0},{5,8},{6,2},{7,10},{8,5},{9,13},{1... | collective-permute-start | bytes 2359304 | tf_op jit(solution)/shard_map/ppermute | solution.py:48
  15.2 11.3 %collective-permute-start.2 = (bf16[384,512]{1,0:T(8,128)(2,1)S(1)}, bf16[384,512]{1,0:T(8,128)(2,1)S(1)}, u32[]{:S(2)}, u32[]{:S(2)}) collective-permute-start(bf16[384,512]{1,0:T(8,128)(2,1)S(1)} %get-tuple-element.57), channel_id=1, source_target_pairs={{0,32},{1,33},{2,34},{3,35},{4,36},{5,37},{6,38},{7,39},{8,40},{9,... | collective-permute-start | bytes 1179656 | tf_op jit(solution)/shard_map/ppermute | solution.py:48
  16.5 19.0 %collective-permute-start.3 = (bf16[384,512]{1,0:T(8,128)(2,1)S(1)}, bf16[384,512]{1,0:T(8,128)(2,1)S(1)}, u32[]{:S(2)}, u32[]{:S(2)}) collective-permute-start(bf16[384,512]{1,0:T(8,128)(2,1)S(1)} %get-tuple-element.58), channel_id=1, source_target_pairs={{0,64},{1,65},{2,66},{3,67},{4,68},{5,69},{6,70},{7,71},{8,72},{9,... | collective-permute-start | bytes 1179656 | tf_op jit(solution)/shard_map/ppermute | solution.py:48
  19.0 19.7 %collective-permute-start.4 = (bf16[384,512]{1,0:T(8,128)(2,1)S(1)}, bf16[384,512]{1,0:T(8,128)(2,1)S(1)}, u32[]{:S(2)}, u32[]{:S(2)}) collective-permute-start(bf16[384,512]{1,0:T(8,128)(2,1)S(1)} %get-tuple-element.59), channel_id=1, source_target_pairs={{0,96},{1,97},{2,98},{3,99},{4,100},{5,101},{6,102},{7,103},{8,104... | collective-permute-start | bytes 1179656 | tf_op jit(solution)/shard_map/ppermute | solution.py:48
  40.6 22.9 %collective-permute-start.12 = (bf16[512,512]{1,0:T(8,128)(2,1)S(1)}, bf16[512,512]{1,0:T(8,128)(2,1)}, u32[]{:S(2)}, u32[]{:S(2)}) collective-permute-start(bf16[512,512]{1,0:T(8,128)(2,1)S(1)} %pad_maximum_fusion.2.own), channel_id=1, source_target_pairs={{0,32},{1,33},{2,34},{3,35},{4,36},{5,37},{6,38},{7,39},{8,40},{9,... | collective-permute-start | bytes 1572872 | tf_op jit(solution)/shard_map/ppermute | solution.py:48
  42.7 4.7 %collective-permute-start.5 = (bf16[96,512]{1,0:T(8,128)(2,1)S(1)}, bf16[96,512]{1,0:T(8,128)(2,1)S(1)}, u32[]{:S(2)}, u32[]{:S(2)}) collective-permute-start(bf16[96,512]{1,0:T(8,128)(2,1)S(1)} %get-tuple-element.63), channel_id=1, source_target_pairs={{0,8},{1,9},{2,10},{3,11},{4,12},{5,13},{6,14},{7,15},{8,0},{9,1},... | collective-permute-start | bytes 294920 | tf_op jit(solution)/shard_map/ppermute | solution.py:48
  42.7 8.1 %collective-permute-start.6 = (bf16[96,512]{1,0:T(8,128)(2,1)S(1)}, bf16[96,512]{1,0:T(8,128)(2,1)S(1)}, u32[]{:S(2)}, u32[]{:S(2)}) collective-permute-start(bf16[96,512]{1,0:T(8,128)(2,1)S(1)} %get-tuple-element.64), channel_id=1, source_target_pairs={{0,16},{1,17},{2,18},{3,19},{4,20},{5,21},{6,22},{7,23},{8,24},{9,... | collective-permute-start | bytes 294920 | tf_op jit(solution)/shard_map/ppermute | solution.py:48
  45.7 7.5 %collective-permute-start.7 = (bf16[96,512]{1,0:T(8,128)(2,1)S(1)}, bf16[96,512]{1,0:T(8,128)(2,1)S(1)}, u32[]{:S(2)}, u32[]{:S(2)}) collective-permute-start(bf16[96,512]{1,0:T(8,128)(2,1)S(1)} %get-tuple-element.65), channel_id=1, source_target_pairs={{0,24},{1,25},{2,26},{3,27},{4,28},{5,29},{6,30},{7,31},{8,16},{9,... | collective-permute-start | bytes 294920 | tf_op jit(solution)/shard_map/ppermute | solution.py:48
  53.2 4.9 %collective-permute-start.8 = (bf16[96,512]{1,0:T(8,128)(2,1)S(1)}, bf16[96,512]{1,0:T(8,128)(2,1)S(1)}, u32[]{:S(2)}, u32[]{:S(2)}) collective-permute-start(bf16[96,512]{1,0:T(8,128)(2,1)S(1)} %reduce_y.1.refs_0_), channel_id=1, source_target_pairs={{0,4},{1,5},{2,6},{3,7},{4,0},{5,1},{6,2},{7,3},{8,12},{9,13},{10,... | collective-permute-start | bytes 294920 | tf_op jit(solution)/shard_map/ppermute | solution.py:48
  58.1 10.4 %collective-permute-start.11 = (bf16[96,512]{1,0:T(8,128)(2,1)S(1)}, bf16[96,512]{1,0:T(8,128)(2,1)S(1)}, u32[]{:S(2)}, u32[]{:S(2)}) collective-permute-start(bf16[96,512]{1,0:T(8,128)(2,1)S(1)} %reduce_z.1), channel_id=1, source_target_pairs={{0,24},{1,25},{2,26},{3,27},{4,28},{5,29},{6,30},{7,31},{8,16},{9,... | collective-permute-start | bytes 294920 | tf_op jit(solution)/shard_map/ppermute | solution.py:48
  58.4 10.1 %collective-permute-start.10 = (bf16[96,512]{1,0:T(8,128)(2,1)S(1)}, bf16[96,512]{1,0:T(8,128)(2,1)S(1)}, u32[]{:S(2)}, u32[]{:S(2)}) collective-permute-start(bf16[96,512]{1,0:T(8,128)(2,1)S(1)} %reduce_z.1), channel_id=1, source_target_pairs={{0,16},{1,17},{2,18},{3,19},{4,20},{5,21},{6,22},{7,23},{8,24},{9,... | collective-permute-start | bytes 294920 | tf_op jit(solution)/shard_map/ppermute | solution.py:48
  61.3 7.2 %collective-permute-start.9 = (bf16[96,512]{1,0:T(8,128)(2,1)S(1)}, bf16[96,512]{1,0:T(8,128)(2,1)S(1)}, u32[]{:S(2)}, u32[]{:S(2)}) collective-permute-start(bf16[96,512]{1,0:T(8,128)(2,1)S(1)} %reduce_z.1), channel_id=1, source_target_pairs={{0,8},{1,9},{2,10},{3,11},{4,12},{5,13},{6,14},{7,15},{8,0},{9,1},... | collective-permute-start | bytes 294920 | tf_op jit(solution)/shard_map/ppermute | solution.py:48
  61.4 16.5 %collective-permute-start.16 = (bf16[512,512]{1,0:T(8,128)(2,1)}, bf16[512,512]{1,0:T(8,128)(2,1)}, u32[]{:S(2)}, u32[]{:S(2)}) collective-permute-start(bf16[512,512]{1,0:T(8,128)(2,1)} %pad_maximum_fusion.1.own), channel_id=1, source_target_pairs={{0,32},{1,33},{2,34},{3,35},{4,36},{5,37},{6,38},{7,39},{8,40},{9,... | collective-permute-start | bytes 1572872 | tf_op jit(solution)/shard_map/ppermute | solution.py:48
  64.4 15.3 %collective-permute-start.13 = (bf16[512,512]{1,0:T(8,128)(2,1)}, bf16[512,512]{1,0:T(8,128)(2,1)}, u32[]{:S(2)}, u32[]{:S(2)}) collective-permute-start(bf16[512,512]{1,0:T(8,128)(2,1)} %broadcast_select_fusion.3), channel_id=1, source_target_pairs={{0,16},{1,17},{2,18},{3,19},{4,20},{5,21},{6,22},{7,23},{8,24},{9,... | collective-permute-start | bytes 1572872 | tf_op jit(solution)/shard_map/ppermute | solution.py:48
  69.9 25.5 %all-to-all-start = ((bf16[4,384,512]{2,1,0:T(8,128)(2,1)}), bf16[4,384,512]{2,1,0:T(8,128)(2,1)}, u32[]{:S(2)}, u32[]{:S(2)}) async-start(bf16[4,384,512]{2,1,0:T(8,128)(2,1)} %broadcast_in_dim.15), calls=%async_computation | async-start | bytes 3145728 | tf_op jit(solution)/shard_map/all_to_all | solution.py:434
  75.6 6.1 %copy-start.7 = (bf16[512,512]{1,0:T(8,128)(2,1)S(1)}, bf16[512,512]{1,0:T(8,128)(2,1)}, u32[]{:S(2)}) copy-start(bf16[512,512]{1,0:T(8,128)(2,1)} %pad_maximum_fusion.1.own) | copy-start | bytes 1572868
  75.6 11.0 %copy-start.13 = (bf16[256,512]{1,0:T(8,128)(2,1)S(1)}, bf16[256,512]{1,0:T(8,128)(2,1)}, u32[]{:S(2)}) copy-start(bf16[256,512]{1,0:T(8,128)(2,1)} %get-tuple-element.104) | copy-start | bytes 786436
  75.6 11.0 %copy-start.14 = (bf16[256,512]{1,0:T(8,128)(2,1)S(1)}, bf16[256,512]{1,0:T(8,128)(2,1)}, u32[]{:S(2)}) copy-start(bf16[256,512]{1,0:T(8,128)(2,1)} %get-tuple-element.108) | copy-start | bytes 786436
  76.8 11.7 %collective-permute-start.15 = (bf16[512,512]{1,0:T(8,128)(2,1)S(1)}, bf16[512,512]{1,0:T(8,128)(2,1)S(1)}, u32[]{:S(2)}, u32[]{:S(2)}) collective-permute-start(bf16[512,512]{1,0:T(8,128)(2,1)S(1)} %broadcast_select_fusion.1), channel_id=1, source_target_pairs={{0,1},{1,0},{2,3},{3,2},{4,5},{5,4},{6,7},{7,6},{8,9},{9,8},{10,11... | collective-permute-start | bytes 1572872 | tf_op jit(solution)/shard_map/ppermute | solution.py:48
  79.7 8.8 %collective-permute-start.14 = (bf16[512,512]{1,0:T(8,128)(2,1)}, bf16[512,512]{1,0:T(8,128)(2,1)S(1)}, u32[]{:S(2)}, u32[]{:S(2)}) collective-permute-start(bf16[512,512]{1,0:T(8,128)(2,1)} %collective-permute-done.13.one), channel_id=1, source_target_pairs={{0,1},{1,0},{2,3},{3,2},{4,5},{5,4},{6,7},{7,6},{8,9},{9,8},{10,11... | collective-permute-start | bytes 1572872 | tf_op jit(solution)/shard_map/ppermute | solution.py:48
  82.6 17.7 %collective-permute-start.17 = (bf16[512,512]{1,0:T(8,128)(2,1)}, bf16[512,512]{1,0:T(8,128)(2,1)}, u32[]{:S(2)}, u32[]{:S(2)}) collective-permute-start(bf16[512,512]{1,0:T(8,128)(2,1)} %broadcast_select_fusion.2), channel_id=1, source_target_pairs={{0,16},{1,17},{2,18},{3,19},{4,20},{5,21},{6,22},{7,23},{8,24},{9,... | collective-permute-start | bytes 1572872 | tf_op jit(solution)/shard_map/ppermute | solution.py:48
  88.6 14.4 %collective-permute-start.19 = (bf16[512,512]{1,0:T(8,128)(2,1)}, bf16[512,512]{1,0:T(8,128)(2,1)}, u32[]{:S(2)}, u32[]{:S(2)}) collective-permute-start(bf16[512,512]{1,0:T(8,128)(2,1)} %broadcast_select_fusion), channel_id=1, source_target_pairs={{0,1},{1,0},{2,3},{3,2},{4,5},{5,4},{6,7},{7,6},{8,9},{9,8},{10,11... | collective-permute-start | bytes 1572872 | tf_op jit(solution)/shard_map/ppermute | solution.py:48
  93.9 1.5 %copy-start.9 = (bf16[5,512,512]{2,1,0:T(8,128)(2,1)}, bf16[5,512,512]{2,1,0:T(8,128)(2,1)S(1)}, u32[]{:S(2)}) copy-start(bf16[5,512,512]{2,1,0:T(8,128)(2,1)S(1)} %get-tuple-element.78.weights_ref) | copy-start | bytes 7864324
  95.4 9.3 %copy-start.8 = (bf16[512,512]{1,0:T(8,128)(2,1)S(1)}, bf16[512,512]{1,0:T(8,128)(2,1)}, u32[]{:S(2)}) copy-start(bf16[512,512]{1,0:T(8,128)(2,1)} %pad_maximum_fusion.1.own) | copy-start | bytes 1572868
  95.4 9.3 %copy-start.10 = (bf16[5,512,512]{2,1,0:T(8,128)(2,1)S(1)}, bf16[5,512,512]{2,1,0:T(8,128)(2,1)}, u32[]{:S(2)}) copy-start(bf16[5,512,512]{2,1,0:T(8,128)(2,1)} %copy-done.9) | copy-start | bytes 7864324
  100.3 4.4 %collective-permute-start.18 = (bf16[512,512]{1,0:T(8,128)(2,1)}, bf16[512,512]{1,0:T(8,128)(2,1)S(1)}, u32[]{:S(2)}, u32[]{:S(2)}) collective-permute-start(bf16[512,512]{1,0:T(8,128)(2,1)} %collective-permute-done.17.one), channel_id=1, source_target_pairs={{0,1},{1,0},{2,3},{3,2},{4,5},{5,4},{6,7},{7,6},{8,9},{9,8},{10,11... | collective-permute-start | bytes 1572872 | tf_op jit(solution)/shard_map/ppermute | solution.py:48
  104.7 7.0 %copy-start.2 = (f32[1,512,512]{2,1,0:T(8,128)S(1)}, f32[1,512,512]{2,1,0:T(8,128)}, u32[]{:S(2)}) copy-start(f32[1,512,512]{2,1,0:T(8,128)} %param.14) | copy-start | bytes 3145732
  104.7 7.0 %copy-start.4 = (f32[1,512,512]{2,1,0:T(8,128)S(1)}, f32[1,512,512]{2,1,0:T(8,128)}, u32[]{:S(2)}) copy-start(f32[1,512,512]{2,1,0:T(8,128)} %param.15) | copy-start | bytes 3145732
  104.7 7.0 %copy-start.12 = (f32[1,512]{1,0:T(1,128)S(1)}, f32[1,512]{1,0:T(1,128)}, u32[]{:S(2)}) copy-start(f32[1,512]{1,0:T(1,128)} %gain_ref.3) | copy-start | bytes 6148
  107.8 10.2 %collective-permute-start.20 = (bf16[256,512]{1,0:T(8,128)(2,1)S(1)}, bf16[256,512]{1,0:T(8,128)(2,1)S(1)}, u32[]{:S(2)}, u32[]{:S(2)}) collective-permute-start(bf16[256,512]{1,0:T(8,128)(2,1)S(1)} %get-tuple-element.85), channel_id=1, source_target_pairs={{0,0},{1,8},{2,2},{3,10},{4,4},{5,12},{6,6},{7,14},{8,1},{9,9},{10... | collective-permute-start | bytes 786440 | tf_op jit(solution)/shard_map/ppermute | solution.py:48
  111.3 7.1 %collective-permute-start.21 = (bf16[256,512]{1,0:T(8,128)(2,1)S(1)}, bf16[256,512]{1,0:T(8,128)(2,1)S(1)}, u32[]{:S(2)}, u32[]{:S(2)}) collective-permute-start(bf16[256,512]{1,0:T(8,128)(2,1)S(1)} %get-tuple-element.86), channel_id=1, source_target_pairs={{0,4},{1,12},{2,6},{3,14},{4,0},{5,8},{6,2},{7,10},{8,5},{9,13},{1... | collective-permute-start | bytes 786440 | tf_op jit(solution)/shard_map/ppermute | solution.py:48
  112.5 6.0 %copy-start.5 = (bf16[1,512,2048]{2,1,0:T(8,128)(2,1)S(1)}, bf16[1,512,2048]{2,1,0:T(8,128)(2,1)}, u32[]{:S(2)}) copy-start(bf16[1,512,2048]{2,1,0:T(8,128)(2,1)} %param.11) | copy-start | bytes 6291460
  119.8 6.7 %collective-permute-start.22 = (bf16[2,256,512]{2,1,0:T(8,128)(2,1)S(1)}, bf16[2,256,512]{2,1,0:T(8,128)(2,1)S(1)}, u32[]{:S(2)}, u32[]{:S(2)}) collective-permute-start(bf16[2,256,512]{2,1,0:T(8,128)(2,1)S(1)} %get-tuple-element.92), channel_id=1, source_target_pairs={{0,1},{1,0},{2,3},{3,2},{4,5},{5,4},{6,7},{7,6},{8,9},{9,8},{10,11... | collective-permute-start | bytes 1572872 | tf_op jit(solution)/shard_map/ppermute | solution.py:48
  128.0 4.2 %collective-permute-start.24 = (bf16[2,256,512]{2,1,0:T(8,128)(2,1)S(1)}, bf16[2,256,512]{2,1,0:T(8,128)(2,1)S(1)}, u32[]{:S(2)}, u32[]{:S(2)}) collective-permute-start(bf16[2,256,512]{2,1,0:T(8,128)(2,1)S(1)} %get-tuple-element.98), channel_id=1, source_target_pairs={{0,1},{1,0},{2,3},{3,2},{4,5},{5,4},{6,7},{7,6},{8,9},{9,8},{10,11... | collective-permute-start | bytes 1572872 | tf_op jit(solution)/shard_map/ppermute | solution.py:48
  128.6 10.2 %collective-permute-start.23 = (bf16[256,512]{1,0:T(8,128)(2,1)S(1)}, bf16[256,512]{1,0:T(8,128)(2,1)S(1)}, u32[]{:S(2)}, u32[]{:S(2)}) collective-permute-start(bf16[256,512]{1,0:T(8,128)(2,1)S(1)} %fusion.5), channel_id=1, source_target_pairs={{0,2},{1,3},{2,0},{3,1},{4,6},{5,7},{6,4},{7,5},{8,10},{9,11},{10,... | collective-permute-start | bytes 786440 | tf_op jit(solution)/shard_map/ppermute | solution.py:48
  132.4 12.0 %collective-permute-start.25 = (bf16[256,512]{1,0:T(8,128)(2,1)S(1)}, bf16[256,512]{1,0:T(8,128)(2,1)S(1)}, u32[]{:S(2)}, u32[]{:S(2)}) collective-permute-start(bf16[256,512]{1,0:T(8,128)(2,1)S(1)} %fusion.7), channel_id=1, source_target_pairs={{0,2},{1,3},{2,0},{3,1},{4,6},{5,7},{6,4},{7,5},{8,10},{9,11},{10,... | collective-permute-start | bytes 786440 | tf_op jit(solution)/shard_map/ppermute | solution.py:48

commit v4 on v3

--- a/solution.py
+++ b/solution.py
@@ -434,7 +434,10 @@
     parts = [lax.all_to_all(sent, "ctx", 0, 0, axis_index_groups=lines, tiled=True)]
     (two_values,) = ordered([two_values], sent)
     one_values, swap_two_values = onward(own_values, two_values)
-    (queries,) = ordered([queries], piece)
+    (normed_zero,) = call(
+        fast_apply, [vmem()] * 5, [((HALF, 512), F32)]
+    )(natural, first, third, second, fw_gain)
+    (queries,) = ordered([queries], piece, normed_zero)
     one_values = moved(one_values, across)
     swap_two_values = moved(swap_two_values, other_core)
 
@@ -462,9 +465,6 @@
     near = moved(near, to_role_same)
     far = moved(far, to_role_other)
 
-    (normed_zero,) = call(
-        fast_apply, [vmem()] * 5, [((HALF, 512), F32)]
-    )(natural, first, third, second, fw_gain)
     (held,) = call(update_middle, [vmem()], [((3, 512, 512), BF)], limit=24)(held)
     normed_zero, near, far = ordered([normed_zero, near, far], held)
     keep, send = mixed_by(mix_zero, place, near, far, normed_zero, w_out[0])

time: 146 us -> 146 us (level)
  transfers between devices with their start and end apart: 27 -> 27, of which waited for: 11 -> 11; matrix products, arithmetic and copies ran while one was open for 5% -> 6% of each run, Pallas kernels for 18% -> 18%
where the time goes in v4:
time: 146 us
  starting transfers between devices  49.9 us (34%)
  waiting for transfers between devices  45.1 us (31%)
  Pallas kernels  37.7 us (26%)
  other arithmetic  8.23 us (6%)
  local copies, waits for them, and re-layouts  4.03 us (3%)
    ppermute x26, waiting for transfers between devices, moved(): return lax.ppermute(value, ('ctx', 'head'), pairs)  45.1 us
    ppermute x26, starting transfers between devices, moved(): return lax.ppermute(value, ('ctx', 'head'), pairs)  44.2 us
    pallas_call x1, Pallas kernels, shards(): call(update_end, [vmem()] * 6, [((512, 512), F32)] * 3 + [((HALF, 512), F...  6.42 us
    pallas_call x1, Pallas kernels, run_project(): call(project, [smem()] + [pl.BlockSpec(memory_space=pltpu.HBM)] * 2, [((2...  6.24 us
    all_to_all x1, starting transfers between devices, shards(): lax.all_to_all(sent, 'ctx', 0, 0, axis_index_groups=lines, tiled=True)  5.7 us
    pallas_call x1, Pallas kernels, shards(): held, = call(update_middle, [vmem()], [((3, 512, 512), BF)], limit=24)(held)  5.52 us
    pallas_call x1, Pallas kernels, shards(): call(scores, [smem()] + [vmem()] * 6, [((5, SUPER, SUPER), BF), ((SUPER,...  5.33 us
    pallas_call x1, Pallas kernels, shards(): call(update_start, [smem(), vmem()], [((3, 512, 512), BF)], scratch=(pltp...  4.89 us
  transfers between devices with their start and end apart: 27, of which 11 were waited for; matrix products, arithmetic and copies ran while one was open for 6% of the time, Pallas kernels for 18%

profile of v4, /device:TPU:1, one launch (start us, length us, event | category | flops | bytes accessed | tf_op | source)
XLA Modules:
  0.0 146.0 jit_solution(2595142268945680405)
XLA Ops:
  0.7 0.1 stack.39.place.refs_0_
  0.8 0.0 copy-start.8
  0.8 6.2 %project.1 = (bf16[2,256,1536]{2,1,0:T(8,128)(2,1)S(1)}, bf16[768,512]{1,0:T(8,128)(2,1)S(1)}, bf16[768,512]{1,0:T(8,128)(2,1)S(1)}) custom-call(s32[6]{0:T(128)S(1)} %stack.39.place.refs_0_, bf16[2,256,2048]{2,1,0:T(8,128)(2,1)} %tokens_ref.3, bf16[2048,1536]{1,0:T(8,128)(2,1)} %bitcast.51), custom_call_target="tpu_custom_call" | custom-call | flops 1048576 | bytes 1024 | tf_op jit(solution)/shard_map/project/pallas_call | solution.py:146
  7.1 4.6 %collective-permute-start = (bf16[768,512]{1,0:T(8,128)(2,1)S(1)}, bf16[768,512]{1,0:T(8,128)(2,1)S(1)}, u32[]{:S(2)}, u32[]{:S(2)}) collective-permute-start(bf16[768,512]{1,0:T(8,128)(2,1)S(1)} %get-tuple-element.54), channel_id=1, source_target_pairs={{0,0},{1,8},{2,2},{3,10},{4,4},{5,12},{6,6},{7,14},{8,1},{9,9},{10... | collective-permute-start | bytes 2359304 | tf_op jit(solution)/shard_map/ppermute | solution.py:48
  11.7 1.4 collective-permute-start.1
  13.1 2.1 %fast_grads.1 = (bf16[384,512]{1,0:T(8,128)(2,1)S(1)}, bf16[384,512]{1,0:T(8,128)(2,1)S(1)}, bf16[384,512]{1,0:T(8,128)(2,1)S(1)}, bf16[384,512]{1,0:T(8,128)(2,1)S(1)}) custom-call(s32[6]{0:T(128)S(1)} %stack.39.place.refs_0_, bf16[2,256,2048]{2,1,0:T(8,128)(2,1)S(1)} %copy-done.8, bf16[1,2048]{1,0:T(2,128)(2,1)S(1)} %bitcast.50, ...), custom_call_target="tpu_custom_call" | custom-call | flops 1048576 | bytes 1024 | tf_op jit(solution)/shard_map/fast_grads/pallas_call | solution.py:394
  15.2 1.3 collective-permute-start.2
  16.5 2.5 %collective-permute-start.3 = (bf16[384,512]{1,0:T(8,128)(2,1)S(1)}, bf16[384,512]{1,0:T(8,128)(2,1)S(1)}, u32[]{:S(2)}, u32[]{:S(2)}) collective-permute-start(bf16[384,512]{1,0:T(8,128)(2,1)S(1)} %get-tuple-element.58), channel_id=1, source_target_pairs={{0,64},{1,65},{2,66},{3,67},{4,68},{5,69},{6,70},{7,71},{8,72},{9,... | collective-permute-start | bytes 1179656 | tf_op jit(solution)/shard_map/ppermute | solution.py:48
  19.0 0.2 collective-permute-start.4
  19.2 7.3 %collective-permute-done.2.refs_1_ = bf16[384,512]{1,0:T(8,128)(2,1)S(1)} collective-permute-done((bf16[384,512]{1,0:T(8,128)(2,1)S(1)}, bf16[384,512]{1,0:T(8,128)(2,1)S(1)}, u32[]{:S(2)}, u32[]{:S(2)}) %collective-permute-start.2) | collective-permute-done | bytes 393248 | tf_op jit(solution)/shard_map/ppermute | solution.py:48
  26.5 9.0 %collective-permute-done.3.refs_2_ = bf16[384,512]{1,0:T(8,128)(2,1)S(1)} collective-permute-done((bf16[384,512]{1,0:T(8,128)(2,1)S(1)}, bf16[384,512]{1,0:T(8,128)(2,1)S(1)}, u32[]{:S(2)}, u32[]{:S(2)}) %collective-permute-start.3) | collective-permute-done | bytes 393248 | tf_op jit(solution)/shard_map/ppermute | solution.py:48
  35.5 3.1 %collective-permute-done.4.refs_3_ = bf16[384,512]{1,0:T(8,128)(2,1)S(1)} collective-permute-done((bf16[384,512]{1,0:T(8,128)(2,1)S(1)}, bf16[384,512]{1,0:T(8,128)(2,1)S(1)}, u32[]{:S(2)}, u32[]{:S(2)}) %collective-permute-start.4) | collective-permute-done | bytes 393248 | tf_op jit(solution)/shard_map/ppermute | solution.py:48
  38.7 0.9 reduce_x.1
  39.6 1.0 fusion.8
  40.6 2.1 %collective-permute-start.12 = (bf16[512,512]{1,0:T(8,128)(2,1)S(1)}, bf16[512,512]{1,0:T(8,128)(2,1)}, u32[]{:S(2)}, u32[]{:S(2)}) collective-permute-start(bf16[512,512]{1,0:T(8,128)(2,1)S(1)} %pad_maximum_fusion.2.own), channel_id=1, source_target_pairs={{0,32},{1,33},{2,34},{3,35},{4,36},{5,37},{6,38},{7,39},{8,40},{9,... | collective-permute-start | bytes 1572872 | tf_op jit(solution)/shard_map/ppermute | solution.py:48
  42.7 2.9 %collective-permute-start.6 = (bf16[96,512]{1,0:T(8,128)(2,1)S(1)}, bf16[96,512]{1,0:T(8,128)(2,1)S(1)}, u32[]{:S(2)}, u32[]{:S(2)}) collective-permute-start(bf16[96,512]{1,0:T(8,128)(2,1)S(1)} %get-tuple-element.64), channel_id=1, source_target_pairs={{0,16},{1,17},{2,18},{3,19},{4,20},{5,21},{6,22},{7,23},{8,24},{9,... | collective-permute-start | bytes 294920 | tf_op jit(solution)/shard_map/ppermute | solution.py:48
  45.6 0.9 collective-permute-start.7
  46.6 0.8 pad_maximum_fusion.1.own
  47.4 3.4 %collective-permute-done.6.refs_2_ = bf16[96,512]{1,0:T(8,128)(2,1)S(1)} collective-permute-done((bf16[96,512]{1,0:T(8,128)(2,1)S(1)}, bf16[96,512]{1,0:T(8,128)(2,1)S(1)}, u32[]{:S(2)}, u32[]{:S(2)}) %collective-permute-start.6) | collective-permute-done | bytes 98336 | tf_op jit(solution)/shard_map/ppermute | solution.py:48
  50.9 2.3 %collective-permute-done.7.refs_3_ = bf16[96,512]{1,0:T(8,128)(2,1)S(1)} collective-permute-done((bf16[96,512]{1,0:T(8,128)(2,1)S(1)}, bf16[96,512]{1,0:T(8,128)(2,1)S(1)}, u32[]{:S(2)}, u32[]{:S(2)}) %collective-permute-start.7) | collective-permute-done | bytes 98336 | tf_op jit(solution)/shard_map/ppermute | solution.py:48
  53.1 0.1 reduce_y.1.refs_0_
  53.2 0.1 collective-permute-start.8
  53.3 4.8 %collective-permute-done.8.refs_1_ = bf16[96,512]{1,0:T(8,128)(2,1)S(1)} collective-permute-done((bf16[96,512]{1,0:T(8,128)(2,1)S(1)}, bf16[96,512]{1,0:T(8,128)(2,1)S(1)}, u32[]{:S(2)}, u32[]{:S(2)}) %collective-permute-start.8) | collective-permute-done | bytes 98336 | tf_op jit(solution)/shard_map/ppermute | solution.py:48
  58.1 0.3 collective-permute-start.11
  58.4 3.0 %collective-permute-start.10 = (bf16[96,512]{1,0:T(8,128)(2,1)S(1)}, bf16[96,512]{1,0:T(8,128)(2,1)S(1)}, u32[]{:S(2)}, u32[]{:S(2)}) collective-permute-start(bf16[96,512]{1,0:T(8,128)(2,1)S(1)} %reduce_z.1), channel_id=1, source_target_pairs={{0,16},{1,17},{2,18},{3,19},{4,20},{5,21},{6,22},{7,23},{8,24},{9,... | collective-permute-start | bytes 294920 | tf_op jit(solution)/shard_map/ppermute | solution.py:48
  61.3 0.1 collective-permute-start.9
  61.4 2.1 %collective-permute-start.16 = (bf16[512,512]{1,0:T(8,128)(2,1)}, bf16[512,512]{1,0:T(8,128)(2,1)}, u32[]{:S(2)}, u32[]{:S(2)}) collective-permute-start(bf16[512,512]{1,0:T(8,128)(2,1)} %pad_maximum_fusion.1.own), channel_id=1, source_target_pairs={{0,32},{1,33},{2,34},{3,35},{4,36},{5,37},{6,38},{7,39},{8,40},{9,... | collective-permute-start | bytes 1572872 | tf_op jit(solution)/shard_map/ppermute | solution.py:48
  63.5 0.9 broadcast_select_fusion.3
  64.4 4.1 %collective-permute-start.13 = (bf16[512,512]{1,0:T(8,128)(2,1)}, bf16[512,512]{1,0:T(8,128)(2,1)}, u32[]{:S(2)}, u32[]{:S(2)}) collective-permute-start(bf16[512,512]{1,0:T(8,128)(2,1)} %broadcast_select_fusion.3), channel_id=1, source_target_pairs={{0,16},{1,17},{2,18},{3,19},{4,20},{5,21},{6,22},{7,23},{8,24},{9,... | collective-permute-start | bytes 1572872 | tf_op jit(solution)/shard_map/ppermute | solution.py:48
  68.6 1.3 broadcast_in_dim.15
  69.9 5.7 %all-to-all-start = ((bf16[4,384,512]{2,1,0:T(8,128)(2,1)}), bf16[4,384,512]{2,1,0:T(8,128)(2,1)}, u32[]{:S(2)}, u32[]{:S(2)}) async-start(bf16[4,384,512]{2,1,0:T(8,128)(2,1)} %broadcast_in_dim.15), calls=%async_computation | async-start | bytes 3145728 | tf_op jit(solution)/shard_map/all_to_all | solution.py:434
  75.6 1.3 broadcast_select_fusion.1
  76.9 1.1 collective-permute-start.15
  77.9 1.8 %collective-permute-done.13.one = bf16[512,512]{1,0:T(8,128)(2,1)} collective-permute-done((bf16[512,512]{1,0:T(8,128)(2,1)}, bf16[512,512]{1,0:T(8,128)(2,1)}, u32[]{:S(2)}, u32[]{:S(2)}) %collective-permute-start.13) | collective-permute-done | bytes 524320 | tf_op jit(solution)/shard_map/ppermute | solution.py:48
  79.7 2.0 %collective-permute-start.14 = (bf16[512,512]{1,0:T(8,128)(2,1)}, bf16[512,512]{1,0:T(8,128)(2,1)S(1)}, u32[]{:S(2)}, u32[]{:S(2)}) collective-permute-start(bf16[512,512]{1,0:T(8,128)(2,1)} %collective-permute-done.13.one), channel_id=1, source_target_pairs={{0,1},{1,0},{2,3},{3,2},{4,5},{5,4},{6,7},{7,6},{8,9},{9,8},{10,11... | collective-permute-start | bytes 1572872 | tf_op jit(solution)/shard_map/ppermute | solution.py:48
  81.7 1.9 %broadcast_select_fusion.2 = bf16[512,512]{1,0:T(8,128)(2,1)} fusion(bf16[512,512]{1,0:T(8,128)(2,1)} %collective-permute-done.16.two, bf16[512,512]{1,0:T(8,128)(2,1)} %pad_maximum_fusion.1.own, pred[]{:T(512)S(6)} %ge.4), kind=kLoop, calls=%fused_computation.16 | loop fusion | flops 262144 | bytes 1572865 | tf_op jit(solution)/shard_map/jit(_where)/select_n | solution.py:420
  83.6 3.0 %collective-permute-start.17 = (bf16[512,512]{1,0:T(8,128)(2,1)}, bf16[512,512]{1,0:T(8,128)(2,1)}, u32[]{:S(2)}, u32[]{:S(2)}) collective-permute-start(bf16[512,512]{1,0:T(8,128)(2,1)} %broadcast_select_fusion.2), channel_id=1, source_target_pairs={{0,16},{1,17},{2,18},{3,19},{4,20},{5,21},{6,22},{7,23},{8,24},{9,... | collective-permute-start | bytes 1572872 | tf_op jit(solution)/shard_map/ppermute | solution.py:48
  86.6 0.7 fast_apply.1.refs_3_
  87.4 2.0 %broadcast_select_fusion = bf16[512,512]{1,0:T(8,128)(2,1)} fusion(bf16[512,512]{1,0:T(8,128)(2,1)S(1)} %copy-done.9, bf16[512,512]{1,0:T(8,128)(2,1)} %collective-permute-done.16.two, pred[]{:T(512)S(6)} %eq.8), kind=kLoop, calls=%fused_computation.14 | loop fusion | flops 262144 | bytes 1572865 | tf_op jit(solution)/shard_map/jit(_where)/select_n | solution.py:422
  89.5 5.3 %scores.1 = (bf16[5,512,512]{2,1,0:T(8,128)(2,1)S(1)}, f32[512,128]{1,0:T(8,128)S(1)}) custom-call(s32[6]{0:T(128)S(1)} %stack.39.place.refs_0_, bf16[512,512]{1,0:T(8,128)(2,1)S(1)} %pad_maximum_fusion.queries_ref, bf16[512,512]{1,0:T(8,128)(2,1)S(1)} %pad_maximum_fusion.2.own, bf16[512,512]{1,0:T(8,128)(2,1)S(1)} %collective-permute-done.14.swap_one, ...), custom_call_target="tpu_custom_call" | custom-call | flops 1048576 | bytes 1024 | tf_op jit(solution)/shard_map/scores/pallas_call | solution.py:445
  94.8 1.5 %copy-done.11 = bf16[5,512,512]{2,1,0:T(8,128)(2,1)} copy-done((bf16[5,512,512]{2,1,0:T(8,128)(2,1)}, bf16[5,512,512]{2,1,0:T(8,128)(2,1)S(1)}, u32[]{:S(2)}) %copy-start.11) | copy-done | bytes 2621464
  96.3 4.9 %update_start.1.in_ref = bf16[3,512,512]{2,1,0:T(8,128)(2,1)S(1)} custom-call(s32[6]{0:T(128)S(1)} %stack.39.place.refs_0_, bf16[4,384,512]{2,1,0:T(8,128)(2,1)} %all-to-all-done.parts_ref), custom_call_target="tpu_custom_call" | custom-call | flops 1048576 | bytes 1024 | tf_op jit(solution)/shard_map/update_start/pallas_call | solution.py:452
  101.2 1.8 %collective-permute-start.18 = (bf16[512,512]{1,0:T(8,128)(2,1)}, bf16[512,512]{1,0:T(8,128)(2,1)S(1)}, u32[]{:S(2)}, u32[]{:S(2)}) collective-permute-start(bf16[512,512]{1,0:T(8,128)(2,1)} %collective-permute-done.17.one), channel_id=1, source_target_pairs={{0,1},{1,0},{2,3},{3,2},{4,5},{5,4},{6,7},{7,6},{8,9},{9,8},{10,11... | collective-permute-start | bytes 1572872 | tf_op jit(solution)/shard_map/ppermute | solution.py:48
  103.0 1.7 %collective-permute-done.18.swap_one = bf16[512,512]{1,0:T(8,128)(2,1)S(1)} collective-permute-done((bf16[512,512]{1,0:T(8,128)(2,1)}, bf16[512,512]{1,0:T(8,128)(2,1)S(1)}, u32[]{:S(2)}, u32[]{:S(2)}) %collective-permute-start.18) | collective-permute-done | bytes 524320 | tf_op jit(solution)/shard_map/ppermute | solution.py:48
  104.7 2.9 %gathered.1 = (bf16[256,512]{1,0:T(8,128)(2,1)S(1)}, bf16[256,512]{1,0:T(8,128)(2,1)S(1)}) custom-call(bf16[5,512,512]{2,1,0:T(8,128)(2,1)S(1)} %copy-done.12, f32[512,128]{1,0:T(8,128)S(1)} %get-tuple-element.79.sum_ref, bf16[512,512]{1,0:T(8,128)(2,1)S(1)} %copy-done.10, bf16[512,512]{1,0:T(8,128)(2,1)S(1)} %collective-permute-done.18.swap_one, ...), custom_call_target="tpu_custom_call" | custom-call | flops 1048576 | bytes 1024 | tf_op jit(solution)/shard_map/gathered/pallas_call | solution.py:461
  107.6 3.5 %collective-permute-start.20 = (bf16[256,512]{1,0:T(8,128)(2,1)S(1)}, bf16[256,512]{1,0:T(8,128)(2,1)S(1)}, u32[]{:S(2)}, u32[]{:S(2)}) collective-permute-start(bf16[256,512]{1,0:T(8,128)(2,1)S(1)} %get-tuple-element.85), channel_id=1, source_target_pairs={{0,0},{1,8},{2,2},{3,10},{4,4},{5,12},{6,6},{7,14},{8,1},{9,9},{10... | collective-permute-start | bytes 786440 | tf_op jit(solution)/shard_map/ppermute | solution.py:48
  111.2 0.0 copy-start.14
  111.2 1.3 collective-permute-start.21
  112.4 5.5 %update_middle.1.in_ref = bf16[3,512,512]{2,1,0:T(8,128)(2,1)S(1)} custom-call(bf16[3,512,512]{2,1,0:T(8,128)(2,1)S(1)} %update_start.1.in_ref), custom_call_target="tpu_custom_call" | custom-call | flops 1048576 | bytes 1024 | tf_op jit(solution)/shard_map/update_middle/pallas_call | solution.py:468
  118.0 1.2 collective-permute-done.21.refs_2_
  119.2 1.3 mix_zero.1
  120.5 0.3 collective-permute-start.22
  120.8 6.4 %update_end.1 = (f32[512,512]{1,0:T(8,128)}, f32[512,512]{1,0:T(8,128)}, f32[512,512]{1,0:T(8,128)}, f32[256,512]{1,0:T(8,128)S(1)}) custom-call(bf16[3,512,512]{2,1,0:T(8,128)(2,1)S(1)} %update_middle.1.in_ref, f32[512,512]{1,0:T(8,128)S(1)} %bitcast.41, f32[512,512]{1,0:T(8,128)S(1)} %bitcast.44, f32[512,512]{1,0:T(8,128)S(1)} %bitcast.47, ...), custom_call_target="tpu_custom_call" | custom-call | flops 1048576 | bytes 1024 | tf_op jit(solution)/shard_map/update_end/pallas_call | solution.py:473
  127.2 0.2 convert_add_fusion.1
  127.4 1.3 mix_one.1
  128.7 0.6 collective-permute-start.24
  129.3 3.6 %collective-permute-start.23 = (bf16[256,512]{1,0:T(8,128)(2,1)S(1)}, bf16[256,512]{1,0:T(8,128)(2,1)S(1)}, u32[]{:S(2)}, u32[]{:S(2)}) collective-permute-start(bf16[256,512]{1,0:T(8,128)(2,1)S(1)} %fusion.5), channel_id=1, source_target_pairs={{0,2},{1,3},{2,0},{3,1},{4,6},{5,7},{6,4},{7,5},{8,10},{9,11},{10,... | collective-permute-start | bytes 786440 | tf_op jit(solution)/shard_map/ppermute | solution.py:48
  132.9 0.2 convert_add_fusion
  133.1 1.6 %collective-permute-start.25 = (bf16[256,512]{1,0:T(8,128)(2,1)S(1)}, bf16[256,512]{1,0:T(8,128)(2,1)S(1)}, u32[]{:S(2)}, u32[]{:S(2)}) collective-permute-start(bf16[256,512]{1,0:T(8,128)(2,1)S(1)} %fusion.7), channel_id=1, source_target_pairs={{0,2},{1,3},{2,0},{3,1},{4,6},{5,7},{6,4},{7,5},{8,10},{9,11},{10,... | collective-permute-start | bytes 786440 | tf_op jit(solution)/shard_map/ppermute | solution.py:48
  134.7 4.8 %collective-permute-done.23 = bf16[256,512]{1,0:T(8,128)(2,1)S(1)} collective-permute-done((bf16[256,512]{1,0:T(8,128)(2,1)S(1)}, bf16[256,512]{1,0:T(8,128)(2,1)S(1)}, u32[]{:S(2)}, u32[]{:S(2)}) %collective-permute-start.23) | collective-permute-done | bytes 262176 | tf_op jit(solution)/shard_map/ppermute | solution.py:48
  139.4 0.1 fusion.4
  139.5 5.5 %collective-permute-done.25 = bf16[256,512]{1,0:T(8,128)(2,1)S(1)} collective-permute-done((bf16[256,512]{1,0:T(8,128)(2,1)S(1)}, bf16[256,512]{1,0:T(8,128)(2,1)S(1)}, u32[]{:S(2)}, u32[]{:S(2)}) %collective-permute-start.25) | collective-permute-done | bytes 262176 | tf_op jit(solution)/shard_map/ppermute | solution.py:48
  145.1 0.1 fusion.6
  145.1 0.8 pad_maximum_fusion.3
  (62 shorter events, 0.3 us)
Async XLA Ops:
  0.8 12.3 %copy-start = (f32[1,512,512]{2,1,0:T(8,128)S(1)}, f32[1,512,512]{2,1,0:T(8,128)}, u32[]{:S(2)}) copy-start(f32[1,512,512]{2,1,0:T(8,128)} %param.13) | copy-start | bytes 3145732
  0.8 12.3 %copy-start.1 = (f32[1,512,512]{2,1,0:T(8,128)S(1)}, f32[1,512,512]{2,1,0:T(8,128)}, u32[]{:S(2)}) copy-start(f32[1,512,512]{2,1,0:T(8,128)} %param.14) | copy-start | bytes 3145732
  0.8 12.3 %copy-start.4 = (f32[1,512,512]{2,1,0:T(8,128)S(1)}, f32[1,512,512]{2,1,0:T(8,128)}, u32[]{:S(2)}) copy-start(f32[1,512,512]{2,1,0:T(8,128)} %param.15) | copy-start | bytes 3145732
  0.8 12.3 %copy-start.8 = (bf16[2,256,2048]{2,1,0:T(8,128)(2,1)S(1)}, bf16[2,256,2048]{2,1,0:T(8,128)(2,1)}, u32[]{:S(2)}) copy-start(bf16[2,256,2048]{2,1,0:T(8,128)(2,1)} %tokens_ref.3) | copy-start | bytes 6291460
  0.8 12.3 %copy-start.15 = (bf16[2048,1]{0,1:T(2,128)(2,1)S(1)}, bf16[2048,1]{0,1:T(2,128)(2,1)}, u32[]{:S(2)}) copy-start(bf16[2048,1]{0,1:T(2,128)(2,1)} %param.10) | copy-start | bytes 12292
  7.1 32.5 %collective-permute-start = (bf16[768,512]{1,0:T(8,128)(2,1)S(1)}, bf16[768,512]{1,0:T(8,128)(2,1)S(1)}, u32[]{:S(2)}, u32[]{:S(2)}) collective-permute-start(bf16[768,512]{1,0:T(8,128)(2,1)S(1)} %get-tuple-element.54), channel_id=1, source_target_pairs={{0,0},{1,8},{2,2},{3,10},{4,4},{5,12},{6,6},{7,14},{8,1},{9,9},{10... | collective-permute-start | bytes 2359304 | tf_op jit(solution)/shard_map/ppermute | solution.py:48
  11.7 28.0 %collective-permute-start.1 = (bf16[768,512]{1,0:T(8,128)(2,1)S(1)}, bf16[768,512]{1,0:T(8,128)(2,1)S(1)}, u32[]{:S(2)}, u32[]{:S(2)}) collective-permute-start(bf16[768,512]{1,0:T(8,128)(2,1)S(1)} %get-tuple-element.55), channel_id=1, source_target_pairs={{0,4},{1,12},{2,6},{3,14},{4,0},{5,8},{6,2},{7,10},{8,5},{9,13},{1... | collective-permute-start | bytes 2359304 | tf_op jit(solution)/shard_map/ppermute | solution.py:48
  15.2 11.3 %collective-permute-start.2 = (bf16[384,512]{1,0:T(8,128)(2,1)S(1)}, bf16[384,512]{1,0:T(8,128)(2,1)S(1)}, u32[]{:S(2)}, u32[]{:S(2)}) collective-permute-start(bf16[384,512]{1,0:T(8,128)(2,1)S(1)} %get-tuple-element.57), channel_id=1, source_target_pairs={{0,32},{1,33},{2,34},{3,35},{4,36},{5,37},{6,38},{7,39},{8,40},{9,... | collective-permute-start | bytes 1179656 | tf_op jit(solution)/shard_map/ppermute | solution.py:48
  16.5 19.0 %collective-permute-start.3 = (bf16[384,512]{1,0:T(8,128)(2,1)S(1)}, bf16[384,512]{1,0:T(8,128)(2,1)S(1)}, u32[]{:S(2)}, u32[]{:S(2)}) collective-permute-start(bf16[384,512]{1,0:T(8,128)(2,1)S(1)} %get-tuple-element.58), channel_id=1, source_target_pairs={{0,64},{1,65},{2,66},{3,67},{4,68},{5,69},{6,70},{7,71},{8,72},{9,... | collective-permute-start | bytes 1179656 | tf_op jit(solution)/shard_map/ppermute | solution.py:48
  19.0 19.7 %collective-permute-start.4 = (bf16[384,512]{1,0:T(8,128)(2,1)S(1)}, bf16[384,512]{1,0:T(8,128)(2,1)S(1)}, u32[]{:S(2)}, u32[]{:S(2)}) collective-permute-start(bf16[384,512]{1,0:T(8,128)(2,1)S(1)} %get-tuple-element.59), channel_id=1, source_target_pairs={{0,96},{1,97},{2,98},{3,99},{4,100},{5,101},{6,102},{7,103},{8,104... | collective-permute-start | bytes 1179656 | tf_op jit(solution)/shard_map/ppermute | solution.py:48
  40.6 22.9 %collective-permute-start.12 = (bf16[512,512]{1,0:T(8,128)(2,1)S(1)}, bf16[512,512]{1,0:T(8,128)(2,1)}, u32[]{:S(2)}, u32[]{:S(2)}) collective-permute-start(bf16[512,512]{1,0:T(8,128)(2,1)S(1)} %pad_maximum_fusion.2.own), channel_id=1, source_target_pairs={{0,32},{1,33},{2,34},{3,35},{4,36},{5,37},{6,38},{7,39},{8,40},{9,... | collective-permute-start | bytes 1572872 | tf_op jit(solution)/shard_map/ppermute | solution.py:48
  42.7 4.7 %collective-permute-start.5 = (bf16[96,512]{1,0:T(8,128)(2,1)S(1)}, bf16[96,512]{1,0:T(8,128)(2,1)S(1)}, u32[]{:S(2)}, u32[]{:S(2)}) collective-permute-start(bf16[96,512]{1,0:T(8,128)(2,1)S(1)} %get-tuple-element.63), channel_id=1, source_target_pairs={{0,8},{1,9},{2,10},{3,11},{4,12},{5,13},{6,14},{7,15},{8,0},{9,1},... | collective-permute-start | bytes 294920 | tf_op jit(solution)/shard_map/ppermute | solution.py:48
  42.7 8.1 %collective-permute-start.6 = (bf16[96,512]{1,0:T(8,128)(2,1)S(1)}, bf16[96,512]{1,0:T(8,128)(2,1)S(1)}, u32[]{:S(2)}, u32[]{:S(2)}) collective-permute-start(bf16[96,512]{1,0:T(8,128)(2,1)S(1)} %get-tuple-element.64), channel_id=1, source_target_pairs={{0,16},{1,17},{2,18},{3,19},{4,20},{5,21},{6,22},{7,23},{8,24},{9,... | collective-permute-start | bytes 294920 | tf_op jit(solution)/shard_map/ppermute | solution.py:48
  45.6 7.5 %collective-permute-start.7 = (bf16[96,512]{1,0:T(8,128)(2,1)S(1)}, bf16[96,512]{1,0:T(8,128)(2,1)S(1)}, u32[]{:S(2)}, u32[]{:S(2)}) collective-permute-start(bf16[96,512]{1,0:T(8,128)(2,1)S(1)} %get-tuple-element.65), channel_id=1, source_target_pairs={{0,24},{1,25},{2,26},{3,27},{4,28},{5,29},{6,30},{7,31},{8,16},{9,... | collective-permute-start | bytes 294920 | tf_op jit(solution)/shard_map/ppermute | solution.py:48
  53.2 4.9 %collective-permute-start.8 = (bf16[96,512]{1,0:T(8,128)(2,1)S(1)}, bf16[96,512]{1,0:T(8,128)(2,1)S(1)}, u32[]{:S(2)}, u32[]{:S(2)}) collective-permute-start(bf16[96,512]{1,0:T(8,128)(2,1)S(1)} %reduce_y.1.refs_0_), channel_id=1, source_target_pairs={{0,4},{1,5},{2,6},{3,7},{4,0},{5,1},{6,2},{7,3},{8,12},{9,13},{10,... | collective-permute-start | bytes 294920 | tf_op jit(solution)/shard_map/ppermute | solution.py:48
  58.1 10.4 %collective-permute-start.11 = (bf16[96,512]{1,0:T(8,128)(2,1)S(1)}, bf16[96,512]{1,0:T(8,128)(2,1)S(1)}, u32[]{:S(2)}, u32[]{:S(2)}) collective-permute-start(bf16[96,512]{1,0:T(8,128)(2,1)S(1)} %reduce_z.1), channel_id=1, source_target_pairs={{0,24},{1,25},{2,26},{3,27},{4,28},{5,29},{6,30},{7,31},{8,16},{9,... | collective-permute-start | bytes 294920 | tf_op jit(solution)/shard_map/ppermute | solution.py:48
  58.4 10.1 %collective-permute-start.10 = (bf16[96,512]{1,0:T(8,128)(2,1)S(1)}, bf16[96,512]{1,0:T(8,128)(2,1)S(1)}, u32[]{:S(2)}, u32[]{:S(2)}) collective-permute-start(bf16[96,512]{1,0:T(8,128)(2,1)S(1)} %reduce_z.1), channel_id=1, source_target_pairs={{0,16},{1,17},{2,18},{3,19},{4,20},{5,21},{6,22},{7,23},{8,24},{9,... | collective-permute-start | bytes 294920 | tf_op jit(solution)/shard_map/ppermute | solution.py:48
  61.3 7.2 %collective-permute-start.9 = (bf16[96,512]{1,0:T(8,128)(2,1)S(1)}, bf16[96,512]{1,0:T(8,128)(2,1)S(1)}, u32[]{:S(2)}, u32[]{:S(2)}) collective-permute-start(bf16[96,512]{1,0:T(8,128)(2,1)S(1)} %reduce_z.1), channel_id=1, source_target_pairs={{0,8},{1,9},{2,10},{3,11},{4,12},{5,13},{6,14},{7,15},{8,0},{9,1},... | collective-permute-start | bytes 294920 | tf_op jit(solution)/shard_map/ppermute | solution.py:48
  61.4 16.5 %collective-permute-start.16 = (bf16[512,512]{1,0:T(8,128)(2,1)}, bf16[512,512]{1,0:T(8,128)(2,1)}, u32[]{:S(2)}, u32[]{:S(2)}) collective-permute-start(bf16[512,512]{1,0:T(8,128)(2,1)} %pad_maximum_fusion.1.own), channel_id=1, source_target_pairs={{0,32},{1,33},{2,34},{3,35},{4,36},{5,37},{6,38},{7,39},{8,40},{9,... | collective-permute-start | bytes 1572872 | tf_op jit(solution)/shard_map/ppermute | solution.py:48
  64.4 15.3 %collective-permute-start.13 = (bf16[512,512]{1,0:T(8,128)(2,1)}, bf16[512,512]{1,0:T(8,128)(2,1)}, u32[]{:S(2)}, u32[]{:S(2)}) collective-permute-start(bf16[512,512]{1,0:T(8,128)(2,1)} %broadcast_select_fusion.3), channel_id=1, source_target_pairs={{0,16},{1,17},{2,18},{3,19},{4,20},{5,21},{6,22},{7,23},{8,24},{9,... | collective-permute-start | bytes 1572872 | tf_op jit(solution)/shard_map/ppermute | solution.py:48
  69.9 26.4 %all-to-all-start = ((bf16[4,384,512]{2,1,0:T(8,128)(2,1)}), bf16[4,384,512]{2,1,0:T(8,128)(2,1)}, u32[]{:S(2)}, u32[]{:S(2)}) async-start(bf16[4,384,512]{2,1,0:T(8,128)(2,1)} %broadcast_in_dim.15), calls=%async_computation | async-start | bytes 3145728 | tf_op jit(solution)/shard_map/all_to_all | solution.py:434
  75.6 11.0 %copy-start.2 = (f32[1,512,512]{2,1,0:T(8,128)S(1)}, f32[1,512,512]{2,1,0:T(8,128)}, u32[]{:S(2)}) copy-start(f32[1,512,512]{2,1,0:T(8,128)} %param.14) | copy-start | bytes 3145732
  75.6 11.0 %copy-start.5 = (f32[1,512,512]{2,1,0:T(8,128)S(1)}, f32[1,512,512]{2,1,0:T(8,128)}, u32[]{:S(2)}) copy-start(f32[1,512,512]{2,1,0:T(8,128)} %param.15) | copy-start | bytes 3145732
  75.6 11.0 %copy-start.16 = (f32[1,512]{1,0:T(1,128)S(1)}, f32[1,512]{1,0:T(1,128)}, u32[]{:S(2)}) copy-start(f32[1,512]{1,0:T(1,128)} %gain_ref.3) | copy-start | bytes 6148
  76.9 12.6 %collective-permute-start.15 = (bf16[512,512]{1,0:T(8,128)(2,1)S(1)}, bf16[512,512]{1,0:T(8,128)(2,1)S(1)}, u32[]{:S(2)}, u32[]{:S(2)}) collective-permute-start(bf16[512,512]{1,0:T(8,128)(2,1)S(1)} %broadcast_select_fusion.1), channel_id=1, source_target_pairs={{0,1},{1,0},{2,3},{3,2},{4,5},{5,4},{6,7},{7,6},{8,9},{9,8},{10,11... | collective-permute-start | bytes 1572872 | tf_op jit(solution)/shard_map/ppermute | solution.py:48
  79.7 9.7 %collective-permute-start.14 = (bf16[512,512]{1,0:T(8,128)(2,1)}, bf16[512,512]{1,0:T(8,128)(2,1)S(1)}, u32[]{:S(2)}, u32[]{:S(2)}) collective-permute-start(bf16[512,512]{1,0:T(8,128)(2,1)} %collective-permute-done.13.one), channel_id=1, source_target_pairs={{0,1},{1,0},{2,3},{3,2},{4,5},{5,4},{6,7},{7,6},{8,9},{9,8},{10,11... | collective-permute-start | bytes 1572872 | tf_op jit(solution)/shard_map/ppermute | solution.py:48
  83.6 3.8 %copy-start.17 = (bf16[256,512]{1,0:T(8,128)(2,1)S(1)}, bf16[256,512]{1,0:T(8,128)(2,1)}, u32[]{:S(2)}) copy-start(bf16[256,512]{1,0:T(8,128)(2,1)} %get-tuple-element.104) | copy-start | bytes 786436
  83.6 3.8 %copy-start.18 = (bf16[256,512]{1,0:T(8,128)(2,1)S(1)}, bf16[256,512]{1,0:T(8,128)(2,1)}, u32[]{:S(2)}) copy-start(bf16[256,512]{1,0:T(8,128)(2,1)} %get-tuple-element.108) | copy-start | bytes 786436
  83.6 3.8 %copy-start.9 = (bf16[512,512]{1,0:T(8,128)(2,1)S(1)}, bf16[512,512]{1,0:T(8,128)(2,1)}, u32[]{:S(2)}) copy-start(bf16[512,512]{1,0:T(8,128)(2,1)} %pad_maximum_fusion.1.own) | copy-start | bytes 1572868
  83.6 17.6 %collective-permute-start.17 = (bf16[512,512]{1,0:T(8,128)(2,1)}, bf16[512,512]{1,0:T(8,128)(2,1)}, u32[]{:S(2)}, u32[]{:S(2)}) collective-permute-start(bf16[512,512]{1,0:T(8,128)(2,1)} %broadcast_select_fusion.2), channel_id=1, source_target_pairs={{0,16},{1,17},{2,18},{3,19},{4,20},{5,21},{6,22},{7,23},{8,24},{9,... | collective-permute-start | bytes 1572872 | tf_op jit(solution)/shard_map/ppermute | solution.py:48
  87.3 2.1 %copy-start.13 = (f32[256,512]{1,0:T(8,128)}, f32[256,512]{1,0:T(8,128)S(1)}, u32[]{:S(2)}) copy-start(f32[256,512]{1,0:T(8,128)S(1)} %fast_apply.1.refs_3_) | copy-start | bytes 1572868
  89.4 13.5 %collective-permute-start.19 = (bf16[512,512]{1,0:T(8,128)(2,1)}, bf16[512,512]{1,0:T(8,128)(2,1)}, u32[]{:S(2)}, u32[]{:S(2)}) collective-permute-start(bf16[512,512]{1,0:T(8,128)(2,1)} %broadcast_select_fusion), channel_id=1, source_target_pairs={{0,1},{1,0},{2,3},{3,2},{4,5},{5,4},{6,7},{7,6},{8,9},{9,8},{10,11... | collective-permute-start | bytes 1572872 | tf_op jit(solution)/shard_map/ppermute | solution.py:48
  94.8 1.5 %copy-start.11 = (bf16[5,512,512]{2,1,0:T(8,128)(2,1)}, bf16[5,512,512]{2,1,0:T(8,128)(2,1)S(1)}, u32[]{:S(2)}) copy-start(bf16[5,512,512]{2,1,0:T(8,128)(2,1)S(1)} %get-tuple-element.78.weights_ref) | copy-start | bytes 7864324
  96.3 8.4 %copy-start.10 = (bf16[512,512]{1,0:T(8,128)(2,1)S(1)}, bf16[512,512]{1,0:T(8,128)(2,1)}, u32[]{:S(2)}) copy-start(bf16[512,512]{1,0:T(8,128)(2,1)} %pad_maximum_fusion.1.own) | copy-start | bytes 1572868
  96.3 8.4 %copy-start.12 = (bf16[5,512,512]{2,1,0:T(8,128)(2,1)S(1)}, bf16[5,512,512]{2,1,0:T(8,128)(2,1)}, u32[]{:S(2)}) copy-start(bf16[5,512,512]{2,1,0:T(8,128)(2,1)} %copy-done.11) | copy-start | bytes 7864324
  101.2 3.5 %collective-permute-start.18 = (bf16[512,512]{1,0:T(8,128)(2,1)}, bf16[512,512]{1,0:T(8,128)(2,1)S(1)}, u32[]{:S(2)}, u32[]{:S(2)}) collective-permute-start(bf16[512,512]{1,0:T(8,128)(2,1)} %collective-permute-done.17.one), channel_id=1, source_target_pairs={{0,1},{1,0},{2,3},{3,2},{4,5},{5,4},{6,7},{7,6},{8,9},{9,8},{10,11... | collective-permute-start | bytes 1572872 | tf_op jit(solution)/shard_map/ppermute | solution.py:48
  107.6 10.4 %collective-permute-start.20 = (bf16[256,512]{1,0:T(8,128)(2,1)S(1)}, bf16[256,512]{1,0:T(8,128)(2,1)S(1)}, u32[]{:S(2)}, u32[]{:S(2)}) collective-permute-start(bf16[256,512]{1,0:T(8,128)(2,1)S(1)} %get-tuple-element.85), channel_id=1, source_target_pairs={{0,0},{1,8},{2,2},{3,10},{4,4},{5,12},{6,6},{7,14},{8,1},{9,9},{10... | collective-permute-start | bytes 786440 | tf_op jit(solution)/shard_map/ppermute | solution.py:48
  111.1 8.0 %copy-start.7 = (bf16[1,512,2048]{2,1,0:T(8,128)(2,1)S(1)}, bf16[1,512,2048]{2,1,0:T(8,128)(2,1)}, u32[]{:S(2)}) copy-start(bf16[1,512,2048]{2,1,0:T(8,128)(2,1)} %param.11) | copy-start | bytes 6291460
  111.2 8.0 %copy-start.14 = (f32[256,512]{1,0:T(8,128)S(1)}, f32[256,512]{1,0:T(8,128)}, u32[]{:S(2)}) copy-start(f32[256,512]{1,0:T(8,128)} %copy-done.13) | copy-start | bytes 1572868
  111.2 8.0 %collective-permute-start.21 = (bf16[256,512]{1,0:T(8,128)(2,1)S(1)}, bf16[256,512]{1,0:T(8,128)(2,1)S(1)}, u32[]{:S(2)}, u32[]{:S(2)}) collective-permute-start(bf16[256,512]{1,0:T(8,128)(2,1)S(1)} %get-tuple-element.86), channel_id=1, source_target_pairs={{0,4},{1,12},{2,6},{3,14},{4,0},{5,8},{6,2},{7,10},{8,5},{9,13},{1... | collective-permute-start | bytes 786440 | tf_op jit(solution)/shard_map/ppermute | solution.py:48
  119.2 1.6 %copy-start.3 = (f32[1,512,512]{2,1,0:T(8,128)S(1)}, f32[1,512,512]{2,1,0:T(8,128)}, u32[]{:S(2)}) copy-start(f32[1,512,512]{2,1,0:T(8,128)} %param.14) | copy-start | bytes 3145732
  119.2 1.6 %copy-start.6 = (f32[1,512,512]{2,1,0:T(8,128)S(1)}, f32[1,512,512]{2,1,0:T(8,128)}, u32[]{:S(2)}) copy-start(f32[1,512,512]{2,1,0:T(8,128)} %param.15) | copy-start | bytes 3145732
  120.5 6.8 %collective-permute-start.22 = (bf16[2,256,512]{2,1,0:T(8,128)(2,1)S(1)}, bf16[2,256,512]{2,1,0:T(8,128)(2,1)S(1)}, u32[]{:S(2)}, u32[]{:S(2)}) collective-permute-start(bf16[2,256,512]{2,1,0:T(8,128)(2,1)S(1)} %get-tuple-element.92), channel_id=1, source_target_pairs={{0,1},{1,0},{2,3},{3,2},{4,5},{5,4},{6,7},{7,6},{8,9},{9,8},{10,11... | collective-permute-start | bytes 1572872 | tf_op jit(solution)/shard_map/ppermute | solution.py:48
  128.7 4.2 %collective-permute-start.24 = (bf16[2,256,512]{2,1,0:T(8,128)(2,1)S(1)}, bf16[2,256,512]{2,1,0:T(8,128)(2,1)S(1)}, u32[]{:S(2)}, u32[]{:S(2)}) collective-permute-start(bf16[2,256,512]{2,1,0:T(8,128)(2,1)S(1)} %get-tuple-element.98), channel_id=1, source_target_pairs={{0,1},{1,0},{2,3},{3,2},{4,5},{5,4},{6,7},{7,6},{8,9},{9,8},{10,11... | collective-permute-start | bytes 1572872 | tf_op jit(solution)/shard_map/ppermute | solution.py:48
  129.3 10.2 %collective-permute-start.23 = (bf16[256,512]{1,0:T(8,128)(2,1)S(1)}, bf16[256,512]{1,0:T(8,128)(2,1)S(1)}, u32[]{:S(2)}, u32[]{:S(2)}) collective-permute-start(bf16[256,512]{1,0:T(8,128)(2,1)S(1)} %fusion.5), channel_id=1, source_target_pairs={{0,2},{1,3},{2,0},{3,1},{4,6},{5,7},{6,4},{7,5},{8,10},{9,11},{10,... | collective-permute-start | bytes 786440 | tf_op jit(solution)/shard_map/ppermute | solution.py:48
  133.1 12.0 %collective-permute-start.25 = (bf16[256,512]{1,0:T(8,128)(2,1)S(1)}, bf16[256,512]{1,0:T(8,128)(2,1)S(1)}, u32[]{:S(2)}, u32[]{:S(2)}) collective-permute-start(bf16[256,512]{1,0:T(8,128)(2,1)S(1)} %fusion.7), channel_id=1, source_target_pairs={{0,2},{1,3},{2,0},{3,1},{4,6},{5,7},{6,4},{7,5},{8,10},{9,11},{10,... | collective-permute-start | bytes 786440 | tf_op jit(solution)/shard_map/ppermute | solution.py:48
